TPU v7x, 32 devices: a whole 2x2x4 slice. The times are simulated.
32 devices in a mesh: dp: 8 (over y, x, core), tp: 4 (over z).
Axes of the slice: x: 2, y: 2, z: 4, core: 2. Of those that a mesh axis runs over, the one named last changes fastest.
Arguments:
- tokens: bfloat16 [20480, 768], P(('dp', 'tp')), may hold values from -6 to 6
- w_query: bfloat16 [768, 768], P('dp', 'tp'), may hold values from -0.3125 to 0.3125
- w_key: bfloat16 [768, 768], P('dp', 'tp'), may hold values from -0.3125 to 0.3125
- w_value: bfloat16 [768, 768], P('dp', 'tp'), may hold values from -0.21875 to 0.21875
- b_query: bfloat16 [768], P('dp'), may hold values from -3 to 3
- b_value: bfloat16 [768], P('dp'), may hold values from -3 to 3
- w_out: bfloat16 [768, 768], P('dp', 'tp'), may hold values from -0.875 to 0.875
- b_out: bfloat16 [768], P('dp'), may hold values from -3 to 3
- gain_attn: bfloat16 [768], P('dp'), may hold values from 0.25 to 1.75
- shift_attn: bfloat16 [768], P('dp'), may hold values from -3 to 3
- w_up: bfloat16 [768, 3072], P('dp', 'tp'), may hold values from -0.21875 to 0.21875
- b_up: bfloat16 [3072], P('dp'), may hold values from -3 to 3
- w_down: bfloat16 [768, 3072], P('dp', 'tp'), may hold values from -0.15625 to 0.15625
- b_down: bfloat16 [768], P('dp'), may hold values from -3 to 3
- gain_ffn: bfloat16 [768], P('dp'), may hold values from 0.25 to 1.75
- shift_ffn: bfloat16 [768], P('dp'), may hold values from -3 to 3
- lengths: int32 [16], replicated, may hold values from 1024 to 1536, as said below
- deal_order: int32 [16], replicated, may hold values from 0 to 15, as said below
- cotangent: bfloat16 [20480, 768], P(('dp', 'tp')), may hold values from -6 to 6
Outputs:
- encoder_output: bfloat16 [20480, 768], P(('dp', 'tp'))
- grad_tokens: float32 [20480, 768], P(('dp', 'tp'))
- grad_w_query: float32 [768, 768], P('dp', 'tp')
- grad_w_key: float32 [768, 768], P('dp', 'tp')
- grad_w_value: float32 [768, 768], P('dp', 'tp')
- grad_b_query: float32 [768], P('dp')
- grad_b_value: float32 [768], P('dp')
- grad_w_out: float32 [768, 768], P('dp', 'tp')
- grad_b_out: float32 [768], P('dp')
- grad_gain_attn: float32 [768], P('dp')
- grad_shift_attn: float32 [768], P('dp')
- grad_w_up: float32 [768, 3072], P('dp', 'tp')
- grad_b_up: float32 [3072], P('dp')
- grad_w_down: float32 [768, 3072], P('dp', 'tp')
- grad_b_down: float32 [768], P('dp')
- grad_gain_ffn: float32 [768], P('dp')
- grad_shift_ffn: float32 [768], P('dp')
Inputs may be any that keep to these rules, and one draw needn't show every extreme that they name: Group g holds sequence deal_order[2 g] in slot 0 and deal_order[2 g + 1] in slot 1; the two lengths of a group add up to 2560, and each is at least 1024. `deal_order`: each of 0 to 15 appears once.
All inputs are finite; a program needn't handle non-finite values.
Results may differ from a plain program's by a relative error of at most 0.015.
The roundings to bfloat16 on the way count: a program that leaves them out, or rounds other values in their place, can miss the bound.
Values may be sent and summed in bfloat16 or wider, within the bound.
A program may use at most 128 MiB of HBM per device.

v0:
```python
import jax
import jax.numpy as jnp
from jax import lax
from jax.sharding import PartitionSpec as P

HD = 64


EPS = 1e-05
SQRT_HALF = 0.7071067811865476
INV_ROOT_TAU = 0.3989422804014327


def normalize_layer(resid):
    center = resid - jnp.mean(resid, axis=-1, keepdims=True)
    inverse_deviation = lax.rsqrt(jnp.mean(center * center, axis=-1, keepdims=True) + EPS)
    return (center * inverse_deviation, inverse_deviation)


def normalize_backward(output_gradient, centered_scaled, inverse_deviation, norm_gain):
    scaled_rows = output_gradient * norm_gain
    return inverse_deviation * (
        scaled_rows
        - jnp.mean(scaled_rows, axis=-1, keepdims=True)
        - centered_scaled * jnp.mean(scaled_rows * centered_scaled, axis=-1, keepdims=True)
    )


def gelu_slope(pre_act):
    return (
        0.5 * (1.0 + lax.erf(pre_act * SQRT_HALF))
        + pre_act * jnp.exp(-0.5 * pre_act * pre_act) * INV_ROOT_TAU
    )


def contract_last(left, right):
    return lax.dot_general(
        left, right, (((1,), (1,)), ((), ())), preferred_element_type=jnp.float32
    )


def contract_first(left, right):
    return lax.dot_general(
        left, right, (((0,), (0,)), ((), ())), preferred_element_type=jnp.float32
    )


def body(
    tokens,
    w_query,
    w_key,
    w_value,
    b_query,
    b_value,
    w_out,
    b_out,
    gain_attn,
    shift_attn,
    w_up,
    b_up,
    w_down,
    b_down,
    gain_ffn,
    shift_ffn,
    lengths,
    deal_order,
    cotangent,
):
    own_rows = tokens.shape[0]
    tp_index = lax.axis_index("tp")
    group_rows = own_rows * lax.axis_size("tp")
    params = (
        w_query,
        w_key,
        w_value,
        w_out,
        w_up,
        w_down,
        b_query,
        b_value,
        b_out,
        gain_attn,
        shift_attn,
        b_up,
        b_down,
        gain_ffn,
        shift_ffn,
    )
    gathered = (
        lax.all_gather(params[0], "dp", axis=0, tiled=True),
        lax.all_gather(params[1], "dp", axis=0, tiled=True),
        lax.all_gather(params[2], "dp", axis=0, tiled=True),
        lax.all_gather(params[3], "dp", axis=0, tiled=True),
        lax.all_gather(params[4], "dp", axis=0, tiled=True),
        lax.all_gather(params[5], "dp", axis=0, tiled=True),
        lax.all_gather(params[6], "dp", axis=0, tiled=True),
        lax.all_gather(params[7], "dp", axis=0, tiled=True),
        lax.all_gather(params[8], "dp", axis=0, tiled=True),
        lax.all_gather(params[9], "dp", axis=0, tiled=True),
        lax.all_gather(params[10], "dp", axis=0, tiled=True),
        lax.all_gather(params[11], "dp", axis=0, tiled=True),
        lax.all_gather(params[12], "dp", axis=0, tiled=True),
        lax.all_gather(params[13], "dp", axis=0, tiled=True),
        lax.all_gather(params[14], "dp", axis=0, tiled=True),
    )
    (
        query_weight,
        key_weight,
        value_weight,
        out_weight,
        up_weight,
        down_weight,
        query_bias,
        value_bias,
        out_bias,
        first_norm_gain,
        first_norm_shift,
        up_bias,
        down_projection_bias,
        second_norm_gain,
        second_norm_shift,
    ) = gathered
    width = query_weight.shape[1]
    hidden_width = up_weight.shape[1]
    heads = width // HD
    block = min(512, group_rows)
    blocks = group_rows // block
    scale = HD ** (-0.5)
    pair = lax.dynamic_slice_in_dim(deal_order, 2 * lax.axis_index("dp"), 2)
    first_len = jnp.sum(
        jnp.where(jnp.arange(lengths.shape[0], dtype=jnp.int32) == pair[0], lengths, 0)
    )
    segment = (jnp.arange(group_rows, dtype=jnp.int32) >= first_len).astype(jnp.int32)
    own_query_bias = lax.dynamic_slice_in_dim(query_bias, tp_index * width, width).astype(
        jnp.float32
    )
    own_value_bias = lax.dynamic_slice_in_dim(value_bias, tp_index * width, width).astype(
        jnp.float32
    )
    own_up_bias = lax.dynamic_slice_in_dim(up_bias, tp_index * hidden_width, hidden_width).astype(
        jnp.float32
    )
    input_full = lax.all_gather(tokens, "tp", axis=0, tiled=True)
    query_rows = (
        jnp.dot(input_full, query_weight, preferred_element_type=jnp.float32) + own_query_bias
    ).astype(jnp.bfloat16)
    key_rows = jnp.dot(input_full, key_weight, preferred_element_type=jnp.float32).astype(
        jnp.bfloat16
    )
    value_rows = (
        jnp.dot(input_full, value_weight, preferred_element_type=jnp.float32) + own_value_bias
    ).astype(jnp.bfloat16)
    key_heads = key_rows.reshape(group_rows, heads, HD)
    value_heads = value_rows.reshape(group_rows, heads, HD)
    query_blocks = query_rows.reshape(blocks, block, heads, HD)
    seg_blocks = segment.reshape(blocks, block)

    def masked_scores(query_block, seg_block):
        scores = (
            jnp.einsum("qhd,khd->hqk", query_block, key_heads, preferred_element_type=jnp.float32)
            * scale
        )
        allowed = seg_block[:, None] == segment[None, :]
        return jnp.where(allowed[None], scores, -1e30)

    def attend(inputs):
        query_block, seg_block = inputs
        scores = masked_scores(query_block, seg_block)
        highest = jnp.max(scores, axis=-1, keepdims=True)
        raised = jnp.exp(scores - highest)
        total = jnp.sum(raised, axis=-1, keepdims=True)
        shares = (raised / total).astype(jnp.bfloat16)
        mixed = jnp.einsum("hqk,khd->qhd", shares, value_heads, preferred_element_type=jnp.float32)
        return (
            mixed.astype(jnp.bfloat16).reshape(block, width),
            (highest + jnp.log(total))[:, :, 0],
        )

    mixed_blocks, log_totals = lax.map(attend, (query_blocks, seg_blocks))
    mixed_rows = mixed_blocks.reshape(group_rows, width)
    attn_term = lax.psum_scatter(
        contract_last(mixed_rows, out_weight), "tp", scatter_dimension=0, tiled=True
    )
    first_residual = tokens.astype(jnp.float32) + attn_term + out_bias.astype(jnp.float32)
    first_centered_scaled, first_inverse_deviation = normalize_layer(first_residual)
    normalized_rows = first_centered_scaled * first_norm_gain.astype(
        jnp.float32
    ) + first_norm_shift.astype(jnp.float32)
    normed_full = lax.all_gather(normalized_rows.astype(jnp.bfloat16), "tp", axis=0, tiled=True)
    pre_act = jnp.dot(normed_full, up_weight, preferred_element_type=jnp.float32) + own_up_bias
    hidden = jax.nn.gelu(pre_act, approximate=False).astype(jnp.bfloat16)
    feedforward_term = lax.psum_scatter(
        contract_last(hidden, down_weight), "tp", scatter_dimension=0, tiled=True
    )
    second_centered_scaled, second_inverse_deviation = normalize_layer(
        normalized_rows + feedforward_term + down_projection_bias.astype(jnp.float32)
    )
    encoder_output = (
        second_centered_scaled * second_norm_gain.astype(jnp.float32)
        + second_norm_shift.astype(jnp.float32)
    ).astype(jnp.bfloat16)
    gathered = (
        lax.all_gather(params[0], "dp", axis=0, tiled=True),
        lax.all_gather(params[1], "dp", axis=0, tiled=True),
        lax.all_gather(params[2], "dp", axis=0, tiled=True),
        lax.all_gather(params[3], "dp", axis=0, tiled=True),
        lax.all_gather(params[4], "dp", axis=0, tiled=True),
        lax.all_gather(params[5], "dp", axis=0, tiled=True),
        lax.all_gather(params[6], "dp", axis=0, tiled=True),
        lax.all_gather(params[7], "dp", axis=0, tiled=True),
        lax.all_gather(params[8], "dp", axis=0, tiled=True),
        lax.all_gather(params[9], "dp", axis=0, tiled=True),
        lax.all_gather(params[10], "dp", axis=0, tiled=True),
        lax.all_gather(params[11], "dp", axis=0, tiled=True),
        lax.all_gather(params[12], "dp", axis=0, tiled=True),
        lax.all_gather(params[13], "dp", axis=0, tiled=True),
        lax.all_gather(params[14], "dp", axis=0, tiled=True),
    )
    (
        query_weight,
        key_weight,
        value_weight,
        out_weight,
        up_weight,
        down_weight,
        query_bias,
        value_bias,
        out_bias,
        first_norm_gain,
        first_norm_shift,
        up_bias,
        down_projection_bias,
        second_norm_gain,
        second_norm_shift,
    ) = gathered
    output_gradient = cotangent.astype(jnp.float32)
    second_gain_gradient = jnp.sum(output_gradient * second_centered_scaled, axis=0)
    grad_shift_two = jnp.sum(output_gradient, axis=0)
    second_residual_gradient = normalize_backward(
        output_gradient,
        second_centered_scaled,
        second_inverse_deviation,
        second_norm_gain.astype(jnp.float32),
    )
    grad_ffn_full = lax.all_gather(
        second_residual_gradient.astype(jnp.bfloat16), "tp", axis=0, tiled=True
    )
    grad_down_bias = jnp.sum(grad_ffn_full, axis=0, dtype=jnp.float32)
    grad_down_weight = contract_first(grad_ffn_full, hidden)
    grad_hidden = jnp.dot(grad_ffn_full, down_weight, preferred_element_type=jnp.float32)
    grad_pre = (grad_hidden * gelu_slope(pre_act)).astype(jnp.bfloat16)
    grad_up_bias = jnp.sum(grad_pre, axis=0, dtype=jnp.float32)
    grad_up_weight = contract_first(normed_full, grad_pre)
    normalized_gradient = second_residual_gradient + lax.psum_scatter(
        contract_last(grad_pre, up_weight), "tp", scatter_dimension=0, tiled=True
    )
    first_gain_gradient = jnp.sum(normalized_gradient * first_centered_scaled, axis=0)
    grad_shift_one = jnp.sum(normalized_gradient, axis=0)
    first_residual_gradient = normalize_backward(
        normalized_gradient,
        first_centered_scaled,
        first_inverse_deviation,
        first_norm_gain.astype(jnp.float32),
    )
    grad_attn_full = lax.all_gather(
        first_residual_gradient.astype(jnp.bfloat16), "tp", axis=0, tiled=True
    )
    grad_out_bias = jnp.sum(grad_attn_full, axis=0, dtype=jnp.float32)
    grad_out_weight = contract_first(grad_attn_full, mixed_rows)
    grad_mixed = jnp.dot(grad_attn_full, out_weight, preferred_element_type=jnp.float32).astype(
        jnp.bfloat16
    )

    def attend_back(carry, inputs):
        key_grad, value_grad = carry
        query_block, seg_block, total_block, grad_block = inputs
        scores = masked_scores(query_block, seg_block)
        shares = jnp.exp(scores - total_block[:, :, None])
        grad_shares = jnp.einsum(
            "qhd,khd->hqk", grad_block, value_heads, preferred_element_type=jnp.float32
        )
        centre = jnp.sum(shares * grad_shares, axis=-1, keepdims=True)
        grad_scores = (shares * (grad_shares - centre)).astype(jnp.bfloat16)
        query_grad = (
            jnp.einsum("hqk,khd->qhd", grad_scores, key_heads, preferred_element_type=jnp.float32)
            * scale
        )
        key_grad = (
            key_grad
            + jnp.einsum(
                "hqk,qhd->khd", grad_scores, query_block, preferred_element_type=jnp.float32
            )
            * scale
        )
        value_grad = value_grad + jnp.einsum(
            "hqk,qhd->khd",
            shares.astype(jnp.bfloat16),
            grad_block,
            preferred_element_type=jnp.float32,
        )
        return ((key_grad, value_grad), query_grad.astype(jnp.bfloat16).reshape(block, width))

    zero_heads = jnp.zeros((group_rows, heads, HD), jnp.float32)
    (key_grad, value_grad), query_grads = lax.scan(
        attend_back,
        (zero_heads, zero_heads),
        (query_blocks, seg_blocks, log_totals, grad_mixed.reshape(blocks, block, heads, HD)),
    )
    grad_query = query_grads.reshape(group_rows, width)
    grad_key = key_grad.astype(jnp.bfloat16).reshape(group_rows, width)
    grad_value = value_grad.astype(jnp.bfloat16).reshape(group_rows, width)
    grad_query_weight = contract_first(input_full, grad_query)
    grad_key_weight = contract_first(input_full, grad_key)
    grad_value_weight = contract_first(input_full, grad_value)
    total = contract_last(grad_query, query_weight)
    total = total + contract_last(grad_key, key_weight)
    back_term = lax.psum_scatter(
        (total + contract_last(grad_value, value_weight)).astype(jnp.bfloat16),
        "tp",
        scatter_dimension=0,
        tiled=True,
    ).astype(jnp.float32)
    grad_tokens = first_residual_gradient + back_term
    empty_model = jnp.zeros((query_bias.shape[0],), jnp.float32)
    query_bias_grad = lax.dynamic_update_slice_in_dim(
        empty_model, jnp.sum(grad_query, axis=0, dtype=jnp.float32), tp_index * width, 0
    )
    value_bias_grad = lax.dynamic_update_slice_in_dim(
        empty_model, jnp.sum(grad_value, axis=0, dtype=jnp.float32), tp_index * width, 0
    )
    up_bias_grad = lax.dynamic_update_slice_in_dim(
        jnp.zeros((up_bias.shape[0],), jnp.float32), grad_up_bias, tp_index * hidden_width, 0
    )
    (
        query_bias_grad,
        value_bias_grad,
        up_bias_grad,
        first_gain_gradient,
        grad_shift_one,
        second_gain_gradient,
        grad_shift_two,
    ) = lax.psum(
        (
            query_bias_grad,
            value_bias_grad,
            up_bias_grad,
            first_gain_gradient,
            grad_shift_one,
            second_gain_gradient,
            grad_shift_two,
        ),
        "tp",
    )
    owned = (
        lax.psum_scatter(grad_query_weight, "dp", scatter_dimension=0, tiled=True),
        lax.psum_scatter(grad_key_weight, "dp", scatter_dimension=0, tiled=True),
        lax.psum_scatter(grad_value_weight, "dp", scatter_dimension=0, tiled=True),
        lax.psum_scatter(grad_out_weight, "dp", scatter_dimension=0, tiled=True),
        lax.psum_scatter(grad_up_weight, "dp", scatter_dimension=0, tiled=True),
        lax.psum_scatter(grad_down_weight, "dp", scatter_dimension=0, tiled=True),
        lax.psum_scatter(query_bias_grad, "dp", scatter_dimension=0, tiled=True),
        lax.psum_scatter(value_bias_grad, "dp", scatter_dimension=0, tiled=True),
        lax.psum_scatter(grad_out_bias, "dp", scatter_dimension=0, tiled=True),
        lax.psum_scatter(first_gain_gradient, "dp", scatter_dimension=0, tiled=True),
        lax.psum_scatter(grad_shift_one, "dp", scatter_dimension=0, tiled=True),
        lax.psum_scatter(up_bias_grad, "dp", scatter_dimension=0, tiled=True),
        lax.psum_scatter(grad_down_bias, "dp", scatter_dimension=0, tiled=True),
        lax.psum_scatter(second_gain_gradient, "dp", scatter_dimension=0, tiled=True),
        lax.psum_scatter(grad_shift_two, "dp", scatter_dimension=0, tiled=True),
    )
    return (
        encoder_output,
        grad_tokens,
        owned[0],
        owned[1],
        owned[2],
        owned[6],
        owned[7],
        owned[3],
        owned[8],
        owned[9],
        owned[10],
        owned[4],
        owned[11],
        owned[5],
        owned[12],
        owned[13],
        owned[14],
    )


def solution(mesh):
    in_specs = (
        P(("dp", "tp"), None),
        P("dp", "tp"),
        P("dp", "tp"),
        P("dp", "tp"),
        P("dp"),
        P("dp"),
        P("dp", "tp"),
        P("dp"),
        P("dp"),
        P("dp"),
        P("dp", "tp"),
        P("dp"),
        P("dp", "tp"),
        P("dp"),
        P("dp"),
        P("dp"),
        P(),
        P(),
        P(("dp", "tp"), None),
    )
    out_specs = (
        P(("dp", "tp"), None),
        P(("dp", "tp"), None),
        P("dp", "tp"),
        P("dp", "tp"),
        P("dp", "tp"),
        P("dp"),
        P("dp"),
        P("dp", "tp"),
        P("dp"),
        P("dp"),
        P("dp"),
        P("dp", "tp"),
        P("dp"),
        P("dp", "tp"),
        P("dp"),
        P("dp"),
        P("dp"),
    )
    return jax.shard_map(body, mesh=mesh, in_specs=in_specs, out_specs=out_specs, check_vma=False)
```

profile of v0, /device:TPU:0, one launch (start us, length us, event | category | flops | bytes accessed | tf_op | source)
XLA Modules:
  0.0 1452.7 jit_solution(7568280337318745953)
XLA Ops:
  18.3 27.4 %all-reduce.19 = (bf16[768]{0:T(1024)(128)(2,1)S(1)}, bf16[768]{0:T(1024)(128)(2,1)S(1)}, bf16[768]{0:T(1024)(128)(2,1)}, bf16[768]{0:T(1024)(128)(2,1)}, bf16[7...) all-reduce(bf16[768]{0:T(1024)(128)(2,1)S(1)} %dynamic-update-slice, ...), channel_id=1, replica_groups=mesh['dp'=8,'tp'=4] {'dp'}, use_global_device_ids=true, to_apply=%add | all-reduce | flops 6144 | bytes 24576
  45.6 8.8 all_gather.66
  54.5 9.3 all_gather.68
  63.7 8.8 all_gather.69
  72.6 10.4 all_gather.71
  103.4 72.3 %while.28 = (s32[]{:T(128)}, bf16[5,512,192]{1,2,0:T(8,128)(2,1)}, f32[5,3,512]{2,1,0:T(4,128)S(1)}, s32[5,512]{1,0:T(8,128)S(1)}, bf16[5,512,3,64]{1,3,2,0:T(8,...) while((s32[]{:T(128)}, bf16[5,512,192]{1,2,0:T(8,128)(2,1)}, ...), condition=%wide.region_4.5_spmd.clone, body=%wide.region_1.4_spmd.clone.sunk | while | flops 1055231488 | bytes 55263352 | solution.py:179
  185.3 133.9 %reduce-scatter.17.cloned.1.call-done = f32[640,768]{1,0:T(8,128)} async-done(((f32[2560,768]{1,0:T(8,128)}), f32[640,768]{1,0:T(8,128)}) %reduce-scatter.17.cloned.1.call-update) | async-done | bytes 1966096 | tf_op jit(solution)/shard_map/reduce_scatter | solution.py:181
  323.7 8.9 all-gather
  332.7 67.2 %all-gather.10.cloned.1.call-done = bf16[2560,768]{1,0:T(8,128)(2,1)} async-done(((bf16[640,768]{1,0:T(8,128)(2,1)}), bf16[2560,768]{1,0:T(8,128)(2,1)}) %all-gather.10.cloned.1.call-update) | async-done | bytes 3932176 | tf_op jit(solution)/shard_map/all_gather | solution.py:189
  399.9 22.3 %fusion.42 = (bf16[2560,768]{1,0:T(8,128)(2,1)}, f32[2560,768]{1,0:T(8,128)}) fusion(f32[768]{0:T(1024)S(1)} %dynamic-slice_convert_fusion, bf16[2560,768]{1,0:T(8,128)(2,1)} %all-gather.10.cloned.1.call-done, bf16[768,768]{1,0:T(8,128)(2,1)} %all-gather.12.cloned.1.call-done), kind=kOutput, calls=%fused_computation.56 | convolution fusion | flops 3149660160 | bytes 16911360 | tf_op jit(solution)/shard_map/dot_general | solution.py:190
  424.0 8.9 fusion.76
  433.6 135.6 %reduce-scatter.19.cloned.1.call-done = f32[640,768]{1,0:T(8,128)} async-done(((f32[2560,768]{1,0:T(8,128)}), f32[640,768]{1,0:T(8,128)}) %reduce-scatter.19.cloned.1.call-update) | async-done | bytes 1966096 | tf_op jit(solution)/shard_map/reduce_scatter | solution.py:192
  575.1 77.0 %all-gather.16.cloned.1.call-done = bf16[2560,768]{1,0:T(8,128)(2,1)} async-done(((bf16[640,768]{1,0:T(8,128)(2,1)}), bf16[2560,768]{1,0:T(8,128)(2,1)}) %all-gather.16.cloned.1.call-update) | async-done | bytes 3932176 | tf_op jit(solution)/shard_map/all_gather | solution.py:245
  652.1 9.7 convert_reduce_fusion.1
  669.8 134.2 %reduce-scatter.21.cloned.1.call-done = f32[640,768]{1,0:T(8,128)} async-done(((f32[2560,768]{1,0:T(8,128)}), f32[640,768]{1,0:T(8,128)}) %reduce-scatter.21.cloned.1.call-update) | async-done | bytes 1966096 | tf_op jit(solution)/shard_map/reduce_scatter | solution.py:254
  804.0 5.6 multiply_reduce_fusion.1
  812.2 76.9 %all-gather.18.cloned.1.call-done = bf16[2560,768]{1,0:T(8,128)(2,1)} async-done(((bf16[640,768]{1,0:T(8,128)(2,1)}), bf16[2560,768]{1,0:T(8,128)(2,1)}) %all-gather.18.cloned.1.call-update) | async-done | bytes 3932176 | tf_op jit(solution)/shard_map/all_gather | solution.py:265
  898.4 215.4 %while.29 = (s32[]{:T(128)}, f32[2560,3,64]{0,2,1:T(8,128)}, f32[2560,3,64]{0,2,1:T(8,128)}, bf16[5,512,192]{1,2,0:T(8,128)(2,1)}, bf16[5,512,3,64]{1,3,2,0:T(8,...) while((s32[]{:T(128)}, f32[2560,3,64]{0,2,1:T(8,128)}, ...), condition=%wide.region_18.19_spmd.clone, body=%wide.region_16.18_spmd.clone.sunk | while | flops 2555940352 | bytes 180019440 | solution.py:304
  899.9 8.7 fusion.161
  908.6 9.1 multiply_reduce_fusion.7
  917.7 9.5 multiply_convert_fusion.2
  931.2 5.8 fusion.165
  942.4 8.7 fusion.161
  951.1 9.1 multiply_reduce_fusion.7
  960.2 9.5 multiply_convert_fusion.2
  974.4 5.9 fusion.165
  985.6 8.7 fusion.161
  994.3 9.1 multiply_reduce_fusion.7
  1003.4 9.5 multiply_convert_fusion.2
  1017.6 5.9 fusion.165
  1028.9 8.7 fusion.161
  1037.5 9.1 multiply_reduce_fusion.7
  1046.7 9.5 multiply_convert_fusion.2
  1060.8 5.8 fusion.165
  1072.1 8.7 fusion.161
  1080.8 9.1 multiply_reduce_fusion.7
  1089.9 9.5 multiply_convert_fusion.2
  1104.1 5.9 fusion.165
  1126.3 8.0 fusion.81
  1134.4 8.0 fusion.82
  1168.5 25.8 %all-reduce.17 = (f32[768]{0:T(1024)S(1)}, f32[768]{0:T(1024)S(1)}, f32[768]{0:T(1024)S(1)}, f32[768]{0:T(1024)S(1)}, f32[768]{0:T(1024)S(1)}, /*index=5*/f32[30...) all-reduce(f32[768]{0:T(1024)S(1)} %dynamic_update_slice.20, ...), channel_id=9, replica_groups=mesh['dp'=8,'tp'=4] {'dp'}, use_global_device_ids=true, to_apply=%region_25.26.clone | all-reduce | flops 9216 | bytes 73728
  1196.0 9.1 all-reduce.18
  1207.7 36.4 %reduce-scatter.27.cloned.1.call-done = f32[96,768]{1,0:T(8,128)} async-done(((f32[768,768]{1,0:T(8,128)}), f32[96,768]{1,0:T(8,128)}) %reduce-scatter.27.cloned.1.call-update) | async-done | bytes 294928 | tf_op jit(solution)/shard_map/reduce_scatter | solution.py:359
  1244.1 46.3 %reduce-scatter.29.cloned.1.call-done = f32[96,768]{1,0:T(8,128)} async-done(((f32[768,768]{1,0:T(8,128)}), f32[96,768]{1,0:T(8,128)}) %reduce-scatter.29.cloned.1.call-update) | async-done | bytes 294928 | tf_op jit(solution)/shard_map/reduce_scatter | solution.py:360
  1290.4 38.7 %reduce-scatter.25.cloned.1.call-done = f32[96,192]{1,0:T(8,128)} async-done(((f32[768,192]{1,0:T(8,128)}), f32[96,192]{1,0:T(8,128)}) %reduce-scatter.25.cloned.1.call-update) | async-done | bytes 73744 | tf_op jit(solution)/shard_map/reduce_scatter | solution.py:358
  1329.1 38.7 %reduce-scatter.31.cloned.1.call-done = f32[96,192]{1,0:T(8,128)} async-done(((f32[768,192]{1,0:T(8,128)}), f32[96,192]{1,0:T(8,128)}) %reduce-scatter.31.cloned.1.call-update) | async-done | bytes 73744
  1367.8 38.6 %reduce-scatter.33.cloned.1.call-done = f32[96,192]{1,0:T(8,128)} async-done(((f32[768,192]{1,0:T(8,128)}), f32[96,192]{1,0:T(8,128)}) %reduce-scatter.33.cloned.1.call-update) | async-done | bytes 73744
  1406.4 38.7 %reduce-scatter.35.cloned.1.call-done = f32[96,192]{1,0:T(8,128)} async-done(((f32[768,192]{1,0:T(8,128)}), f32[96,192]{1,0:T(8,128)}) %reduce-scatter.35.cloned.1.call-update) | async-done | bytes 73744
  (299 shorter events, 234.8 us)
Async XLA Ops:
  8.0 81.6 %all-gather.8.cloned.1.call-start = ((), (), s32[]{:S(2)}) async-start(), calls=%async_computation.10 | async-start | bytes 4915200 | tf_op jit(solution)/shard_map/all_gather | solution.py:143
  8.8 310.4 %reduce-scatter.17.cloned.1.call-start = ((), (), s32[]{:S(2)}) async-start(), calls=%async_computation.11 | async-start | bytes 9830400 | tf_op jit(solution)/shard_map/reduce_scatter | solution.py:181
  54.5 39.6 %copy-start.19 = (bf16[768,192]{1,0:T(8,128)(2,1)}, bf16[768,192]{1,0:T(8,128)(2,1)S(1)}, u32[]{:S(2)}) copy-start(bf16[768,192]{1,0:T(8,128)(2,1)S(1)} %all_gather.66) | copy-start | bytes 884740
  63.7 33.5 %copy-start.14 = (bf16[768,192]{1,0:T(8,128)(2,1)}, bf16[768,192]{1,0:T(8,128)(2,1)S(1)}, u32[]{:S(2)}) copy-start(bf16[768,192]{1,0:T(8,128)(2,1)S(1)} %all_gather.68) | copy-start | bytes 884740
  72.6 28.4 %copy-start.17 = (bf16[768,192]{1,0:T(8,128)(2,1)}, bf16[768,192]{1,0:T(8,128)(2,1)S(1)}, u32[]{:S(2)}) copy-start(bf16[768,192]{1,0:T(8,128)(2,1)S(1)} %all_gather.69) | copy-start | bytes 884740
  97.2 3.7 copy-start.3
  176.7 7.5 copy-start.5
  178.5 5.6 copy-start.7
  184.2 148.5 %all-gather.12.cloned.1.call-start = ((), (), s32[]{:S(2)}) async-start(), calls=%async_computation.13 | async-start | bytes 1327104 | tf_op jit(solution)/shard_map/all_gather | solution.py:94
  184.8 215.2 %all-gather.10.cloned.1.call-start = ((), (), s32[]{:S(2)}) async-start(), calls=%async_computation.12 | async-start | bytes 4915200 | tf_op jit(solution)/shard_map/all_gather | solution.py:189
  321.3 2.4 copy-start.31
  323.0 101.0 %all-gather.14.cloned.1.call-start = ((), (), s32[]{:S(2)}) async-start(), calls=%async_computation.14 | async-start | bytes 1327104 | tf_op jit(solution)/shard_map/all_gather | solution.py:95
  323.6 245.7 %reduce-scatter.19.cloned.1.call-start = ((), (), s32[]{:S(2)}) async-start(), calls=%async_computation.15 | async-start | bytes 9830400 | tf_op jit(solution)/shard_map/reduce_scatter | solution.py:192
  432.9 219.2 %all-gather.16.cloned.1.call-start = ((), (), s32[]{:S(2)}) async-start(), calls=%async_computation.16 | async-start | bytes 4915200 | tf_op jit(solution)/shard_map/all_gather | solution.py:245
  569.3 2.7 copy-start.11
  575.0 229.0 %reduce-scatter.21.cloned.1.call-start = ((), (), s32[]{:S(2)}) async-start(), calls=%async_computation.17 | async-start | bytes 9830400 | tf_op jit(solution)/shard_map/reduce_scatter | solution.py:254
  652.1 11.6 copy-start.32
  661.8 2.0 copy-start.33
  669.2 219.9 %all-gather.18.cloned.1.call-start = ((), (), s32[]{:S(2)}) async-start(), calls=%async_computation.18 | async-start | bytes 4915200 | tf_op jit(solution)/shard_map/all_gather | solution.py:265
  809.7 79.4 %copy-start.16 = (bf16[768,192]{1,0:T(8,128)(2,1)S(1)}, bf16[768,192]{1,0:T(8,128)(2,1)}, u32[]{:S(2)}) copy-start(bf16[768,192]{1,0:T(8,128)(2,1)} %all_gather.71) | copy-start | bytes 884740
  812.0 393.1 %reduce-scatter.23.cloned.1.call-start = ((), (), s32[]{:S(2)}) async-start(), calls=%async_computation.19 | async-start | bytes 4915200 | tf_op jit(solution)/shard_map/reduce_scatter | solution.py:317
  892.6 5.8 copy-start.6
  927.3 9.8 copy-start.1
  931.2 5.9 copy-start
  969.8 10.5 copy-start.1
  974.4 5.9 copy-start
  1013.0 10.5 copy-start.1
  1017.6 5.9 copy-start
  1056.2 10.5 copy-start.1
  1060.8 5.9 copy-start
  1099.4 10.5 copy-start.1
  1104.1 5.9 copy-start
  1117.2 4.5 copy-start.9
  1119.5 2.3 copy-start.15
  1126.2 117.9 %reduce-scatter.27.cloned.1.call-start = ((), (), s32[]{:S(2)}) async-start(), calls=%async_computation.21 | async-start | bytes 2654208 | tf_op jit(solution)/shard_map/reduce_scatter | solution.py:359
  1134.3 8.2 copy-start.8
  1134.3 156.1 %reduce-scatter.29.cloned.1.call-start = ((), (), s32[]{:S(2)}) async-start(), calls=%async_computation.22 | async-start | bytes 2654208 | tf_op jit(solution)/shard_map/reduce_scatter | solution.py:360
  1142.4 186.7 %reduce-scatter.25.cloned.1.call-start = ((), (), s32[]{:S(2)}) async-start(), calls=%async_computation.20 | async-start | bytes 884736 | tf_op jit(solution)/shard_map/reduce_scatter | solution.py:358
  1146.8 221.0 %reduce-scatter.31.cloned.1.call-start = ((), (), s32[]{:S(2)}) async-start(), calls=%async_computation.23 | async-start | bytes 884736
  1151.8 254.6 %reduce-scatter.33.cloned.1.call-start = ((), (), s32[]{:S(2)}) async-start(), calls=%async_computation.24 | async-start | bytes 884736
  1156.0 289.1 %reduce-scatter.35.cloned.1.call-start = ((), (), s32[]{:S(2)}) async-start(), calls=%async_computation.25 | async-start | bytes 884736
  1160.5 4.2 copy-start.24
  1160.5 4.5 copy-start.12
  1161.7 6.8 copy-start.20
  1161.7 6.8 copy-start.21
  1161.7 6.8 copy-start.22
  1161.7 6.8 copy-start.23
  1161.7 43.4 %copy-start.13 = (f32[640,768]{1,0:T(8,128)S(1)}, f32[640,768]{1,0:T(8,128)}, u32[]{:S(2)}) copy-start(f32[640,768]{1,0:T(8,128)} %get-tuple-element.363) | copy-start | bytes 5898244
  (14 other events, 16.2 us)
Sparse Core Ops, SparseCore 0:
  10.4 79.1 all-gather.7
  184.3 134.8 reduce-scatter.16
  575.2 76.9 all-gather.15
  812.1 76.9 all-gather.17
  1126.3 71.1 reduce-scatter.22
  1201.3 42.7 reduce-scatter.26
  1248.0 42.3 reduce-scatter.28
  1294.1 34.9 reduce-scatter.24
  1332.8 34.9 reduce-scatter.30
  1371.4 34.9 reduce-scatter.32
  1410.1 34.9 reduce-scatter.34
Sparse Core Ops, SparseCore 1:
  186.6 22.3 all-gather.11
  323.1 76.8 all-gather.9
  401.7 22.3 all-gather.13
  433.0 136.2 reduce-scatter.18
  669.3 134.7 reduce-scatter.20
where the time goes:
time: 1460 us; the launch traced here: 1450 us
  waiting for transfers between devices  870 us (60%)
  matrix products  295 us (20%)
  other arithmetic  116 us (8%)
  blocking collectives  109 us (7%)
  local copies, waits for them, and re-layouts  42.9 us (3%)
  between operations  18.4 us (1%)
    reduce_scatter x1, waiting for transfers between devices, body(): lax.psum_scatter(contract_last(hidden, down_weight), 'tp', scatter_dimens...  136 us
    reduce_scatter x1, waiting for transfers between devices, body(): lax.psum_scatter(contract_last(grad_pre, up_weight), 'tp', scatter_dimens...  134 us
    reduce_scatter x1, waiting for transfers between devices, body(): lax.psum_scatter(contract_last(mixed_rows, out_weight), 'tp', scatter_dim...  134 us
    unnamed x19, waiting for transfers between devices  118 us
    all_gather x1, waiting for transfers between devices, body(): lax.all_gather(second_residual_gradient.astype(jnp.bfloat16), 'tp', axis=...  77 us
    all_gather x1, waiting for transfers between devices, body(): lax.all_gather(first_residual_gradient.astype(jnp.bfloat16), 'tp', axis=0...  76.9 us
    all_gather x1, waiting for transfers between devices, body(): lax.all_gather(normalized_rows.astype(jnp.bfloat16), 'tp', axis=0, tiled=...  67.2 us
    dot_general x10, matrix products, masked_scores(): jnp.einsum('qhd,khd->hqk', query_block, key_heads, preferred_element_type...  61.8 us
  transfers between devices with their start and end apart: 16, of which 14 were waited for; matrix products, arithmetic and copies ran while one was open for 6% of the time, Pallas kernels for 0%

commit v1 on v0

v1 whole, which is shorter than its diff:
```python
import functools

import jax
import jax.numpy as jnp
from jax import lax
from jax.experimental import pallas as pl
from jax.experimental.pallas import tpu as pltpu
from jax.sharding import PartitionSpec as P

HD = 64
SHORT = 1024
EPS = 1e-05
SQRT_HALF = 0.7071067811865476
INV_ROOT_TAU = 0.3989422804014327
MASKED = -1e30
KEYS = 512
ROWS = 128
VMEM_MAX = 67043328
MESH = pl.DeviceIdType.MESH
F32 = jnp.float32
BF16 = jnp.bfloat16


def dot(left, right):
    return jnp.dot(left, right, preferred_element_type=F32)


def contract_last(left, right):
    return lax.dot_general(left, right, (((1,), (1,)), ((), ())), preferred_element_type=F32)


def contract_first(left, right):
    return lax.dot_general(left, right, (((0,), (0,)), ((), ())), preferred_element_type=F32)


def normalize_layer(resid):
    center = resid - jnp.mean(resid, axis=-1, keepdims=True)
    inverse_deviation = lax.rsqrt(jnp.mean(center * center, axis=-1, keepdims=True) + EPS)
    return (center * inverse_deviation, inverse_deviation)


def normalize_backward(output_gradient, xhat, inverse_deviation, gain):
    scaled_rows = output_gradient * gain
    return inverse_deviation * (
        scaled_rows
        - jnp.mean(scaled_rows, axis=-1, keepdims=True)
        - xhat * jnp.mean(scaled_rows * xhat, axis=-1, keepdims=True)
    )


def gelu_slope(pre_act):
    return (
        0.5 * (1.0 + lax.erf(pre_act * SQRT_HALF))
        + pre_act * jnp.exp(-0.5 * pre_act * pre_act) * INV_ROOT_TAU
    )


def position():
    z = lax.axis_index("tp")
    d = lax.axis_index("dp")
    core = lax.rem(d, 2)
    first = 2 + 2 * core
    second = 4 - 2 * core
    return z, d, core, first, second


def xor(d, mask):
    return d + mask * (1 - 2 * lax.rem(d // mask, 2))


def greet(z, d):
    barrier = pltpu.get_barrier_semaphore()
    for mask in (1, 2, 4):
        pl.semaphore_signal(barrier, inc=1, device_id=(xor(d, mask), z), device_id_type=MESH)
    for j in range(1, 4):
        pl.semaphore_signal(barrier, inc=1, device_id=(d, lax.rem(z + j, 4)), device_id_type=MESH)
    pl.semaphore_wait(barrier, 6)


def by_distance(z):
    low = z <= 1
    near = jnp.where(z == 0, 1, jnp.where(z == 3, 2, z - 1))
    mid = jnp.where(z == 0, 2, jnp.where(z == 3, 1, z + 1))
    far = jnp.where(low, 3, 0)
    return (z, near, mid, far)


def gather_kernel(
    own_w, own_s, own_t, w, s, t,
    wz_s, wz_r, wa_s, wa_r, wb_s, wb_r, wc_s, wc_r, tk_s, tk_r, sm_s, sm_r, lo_sem, blank, bl_sem,
):
    z, d, core, first, second = position()
    packs = own_w.shape[0]
    chunks = own_t.shape[0] // ROWS
    d1, d2 = xor(d, first), xor(d, second)
    d12 = xor(d1, second)
    pal = xor(d, 1)
    order = by_distance(z)

    def put(src, dst, send, recv, dp, tp):
        return pltpu.make_async_remote_copy(
            src_ref=src, dst_ref=dst, send_sem=send, recv_sem=recv, device_id=(dp, tp), device_id_type=MESH
        )

    greet(z, d)

    keep = [
        pltpu.make_async_copy(own_w, w.at[:, z, d], lo_sem.at[0]),
        pltpu.make_async_copy(own_s, s.at[d], lo_sem.at[1]),
        pltpu.make_async_copy(own_t, t.at[pl.ds(pl.multiple_of(z * own_t.shape[0], ROWS), own_t.shape[0])], lo_sem.at[2]),
    ]
    for copy in keep:
        copy.start()

    def along_z(p, tt, src, act):
        right = put(src, w.at[p, tt, d], wz_s.at[0, p, tt], wz_r.at[p, tt], d, jnp.minimum(z + 1, 3))
        left = put(src, w.at[p, tt, d], wz_s.at[1, p, tt], wz_r.at[p, tt], d, jnp.maximum(z - 1, 0))

        @pl.when((tt <= z) & (z < 3))
        def _():
            act(right)

        @pl.when((tt >= z) & (z > 0))
        def _():
            act(left)

    def across(p, tt, src):
        return (
            put(src, w.at[p, tt, d], wa_s.at[p, tt], wa_r.at[p, tt], d1, z),
            put(src, w.at[p, tt, d], wb_s.at[p, tt, 0], wb_r.at[p, tt, 0], d2, z),
            put(src, w.at[p, tt, d], wc_s.at[p, tt, 0], wc_r.at[p, tt, 0], pal, z),
        )

    def after_first(p, tt):
        src = w.at[p, tt, d1]
        return (
            put(src, src, wb_s.at[p, tt, 1], wb_r.at[p, tt, 1], d2, z),
            put(src, src, wc_s.at[p, tt, 1], wc_r.at[p, tt, 1], pal, z),
        )

    def after_second(p, tt, i):
        src = w.at[p, tt, d2 if i == 0 else d12]
        return put(src, src, wc_s.at[p, tt, 2 + i], wc_r.at[p, tt, 2 + i], pal, z)

    def source(p, j):
        return own_w.at[p] if j == 0 else w.at[p, order[j], d]

    def arrive(ref, sem):
        return put(ref, ref, lo_sem.at[0], sem, pal, z)

    def begin(p, j):
        if j > 0:
            arrive(w.at[p, order[j], d], wz_r.at[p, order[j]]).wait_recv()
        along_z(p, order[j], source(p, j), lambda c: c.start())
        for copy in across(p, order[j], source(p, j)):
            copy.start()

    def relay_first(p, j):
        tt = order[j]
        arrive(w.at[p, tt, d1], wa_r.at[p, tt]).wait_recv()
        for copy in after_first(p, tt):
            copy.start()

    def relay_second(p, j):
        tt = order[j]
        for i in range(2):
            arrive(w.at[p, tt, d2 if i == 0 else d12], wb_r.at[p, tt, i]).wait_recv()
            after_second(p, tt, i).start()

    def token_slice(o, i):
        return t.at[pl.ds(pl.multiple_of((o * chunks + i) * ROWS, ROWS), ROWS)]

    def token_hop(o, i, hop, step):
        src = own_t.at[pl.ds(i * ROWS, ROWS)] if hop == 0 else token_slice(o, i)
        way = 0 if step > 0 else 1
        return put(src, token_slice(o, i), tk_s.at[way, hop, i], tk_r.at[way, hop, i], d, jnp.clip(z + step, 0, 3))

    last = SHORT // ROWS

    def wanted(o, i, target, step):
        k = o * chunks + i
        if step > 0:
            return (target <= 2) | (k >= last)
        return (target >= 1) | (k < 4 * chunks - last)

    def tokens(hop, step, act):
        o = z - step * hop
        target = z + step
        valid = (o >= 0) & (o <= 3) & (target >= 0) & (target <= 3)
        ids = range(chunks) if step < 0 else reversed(range(chunks))
        for i in ids:

            @pl.when(valid & wanted(o, i, target, step))
            def _():
                act(token_hop(o, i, hop, step))

    def tokens_in(hop, step):
        o = z - step * (hop + 1)
        valid = (o >= 0) & (o <= 3) & (z - step >= 0) & (z - step <= 3)
        way = 0 if step > 0 else 1
        ids = range(chunks) if step < 0 else reversed(range(chunks))
        for i in ids:

            @pl.when(valid & wanted(o, i, z, step))
            def _():
                ref = token_slice(jnp.clip(o, 0, 3), i)
                arrive(ref, tk_r.at[way, hop, i]).wait_recv()

    def small(stage):
        if stage == 0:
            return [
                put(own_s, s.at[d], sm_s.at[0], sm_r.at[0], d1, z),
                put(own_s, s.at[d], sm_s.at[1], sm_r.at[1], d2, z),
                put(own_s, s.at[d], sm_s.at[3], sm_r.at[3], pal, z),
            ]
        if stage == 1:
            return [
                put(s.at[d1], s.at[d1], sm_s.at[2], sm_r.at[2], d2, z),
                put(s.at[d1], s.at[d1], sm_s.at[4], sm_r.at[4], pal, z),
            ]
        return [
            put(s.at[d2], s.at[d2], sm_s.at[5], sm_r.at[5], pal, z),
            put(s.at[d12], s.at[d12], sm_s.at[6], sm_r.at[6], pal, z),
        ]

    blank[...] = jnp.zeros_like(blank)

    def blanks(act):
        for i in range(last):
            rows = pl.ds(pl.multiple_of(jnp.where(z == 0, 4 * chunks - last + i, i) * ROWS, ROWS), ROWS)

            @pl.when((z == 0) | (z == 3))
            def _():
                act(pltpu.make_async_copy(blank, t.at[rows], bl_sem.at[i]))

    for p in range(packs):
        begin(p, 0)
        if p == 0:
            for copy in small(0):
                copy.start()
            for step in (1, -1):
                tokens(0, step, lambda c: c.start())
    blanks(lambda c: c.start())
    arrive(s.at[d1], sm_r.at[0]).wait_recv()
    for copy in small(1):
        copy.start()
    for p in range(packs):
        relay_first(p, 0)
    arrive(s.at[d2], sm_r.at[1]).wait_recv()
    arrive(s.at[d12], sm_r.at[2]).wait_recv()
    for copy in small(2):
        copy.start()
    for j in range(1, 4):
        for p in range(packs):
            begin(p, j)
        for p in range(packs):
            relay_second(p, j - 1)
        for p in range(packs):
            relay_first(p, j)
        if j < 3:
            for step in (1, -1):
                tokens_in(j - 1, step)
                tokens(j, step, lambda c: c.start())
    for p in range(packs):
        relay_second(p, 3)
    for step in (1, -1):
        tokens_in(2, step)
    pd, pd1, pd2, pd12 = (xor(e, 1) for e in (d, d1, d2, d12))
    for i, e in enumerate((pd, pd2, pd1, pd12)):
        arrive(s.at[e], sm_r.at[3 + i]).wait_recv()
    for p in range(packs):
        for tt in range(4):
            for i, e in enumerate((pd, pd2, pd1, pd12)):
                arrive(w.at[p, tt, e], wc_r.at[p, tt, i]).wait_recv()
    for stage in range(3):
        for copy in small(stage):
            copy.wait_send()
    for hop in range(3):
        for step in (1, -1):
            tokens(hop, step, lambda c: c.wait_send())
    for p in range(packs):
        for j in range(4):
            tt = order[j]
            along_z(p, tt, source(p, j), lambda c: c.wait_send())
            for copy in across(p, tt, source(p, j)) + after_first(p, tt):
                copy.wait_send()
            for i in range(2):
                after_second(p, tt, i).wait_send()
    for copy in keep:
        copy.wait()
    blanks(lambda c: c.wait())


def gather_all(own_w, own_s, own_t):
    packs, r, c = own_w.shape
    rows, width = own_t.shape
    chunks = rows // ROWS
    dma = pltpu.SemaphoreType.DMA
    any_ = pl.BlockSpec(memory_space=pl.ANY)
    vmem = pl.BlockSpec(memory_space=pltpu.VMEM)
    return pl.pallas_call(
        gather_kernel,
        out_shape=(
            jax.ShapeDtypeStruct((packs, 4, 8, r, c), BF16),
            jax.ShapeDtypeStruct((8,) + own_s.shape, own_s.dtype),
            jax.ShapeDtypeStruct((4 * rows, width), BF16),
        ),
        in_specs=[vmem, vmem, vmem],
        out_specs=(any_, any_, any_),
        scratch_shapes=[
            dma((2, packs, 4)),
            dma((packs, 4)),
            dma((packs, 4)),
            dma((packs, 4)),
            dma((packs, 4, 2)),
            dma((packs, 4, 2)),
            dma((packs, 4, 4)),
            dma((packs, 4, 4)),
            dma((2, 3, chunks)),
            dma((2, 3, chunks)),
            dma((7,)),
            dma((7,)),
            dma((3,)),
            pltpu.VMEM((ROWS, width), BF16),
            dma((SHORT // ROWS,)),
        ],
        compiler_params=pltpu.CompilerParams(collective_id=0, has_side_effects=True),
        name="gather_all",
    )(own_w, own_s, own_t)


def reduce_kernel(
    g, sv, dt, base, out_w, out_s, out_t,
    gk, r1, b2, r2, b3, r3, s3, b4, r4, ds, dr, sk, q1, q2, q3, c2, c3, q4,
    gk_sem, p1_s, p1_r, p2_s, p2_r, p3_s, p3_r, p4_s, p4_r, t_l, t_s, t_r, v_s, v_r,
):
    z, d, core, first, second = position()
    e_mask, f_mask = second, first
    packs = g.shape[0]
    xy = d // 2
    e, f = xor(d, e_mask) // 2, xor(d, f_mask) // 2
    ef = xor(xor(d, e_mask), f_mask) // 2
    d_e, d_f, pal = xor(d, e_mask), xor(d, f_mask), xor(d, 1)
    chunks = base.shape[0] // ROWS
    total = 4 * chunks
    edge = SHORT // ROWS

    def put(src, dst, send, recv, dp, tp):
        return pltpu.make_async_remote_copy(
            src_ref=src, dst_ref=dst, send_sem=send, recv_sem=recv, device_id=(dp, tp), device_id_type=MESH
        )

    def up(ref):
        return ref[...].astype(F32)

    greet(z, d)
    fetch = [
        [pltpu.make_async_copy(g.at[p, t, :, core], gk.at[p, t], gk_sem.at[p, t]) for t in range(4)]
        for p in range(packs)
    ]
    one = [
        [put(g.at[p, t, :, 1 - core], r1.at[p, t], p1_s.at[p, t], p1_r.at[p, t], pal, z) for t in range(4)]
        for p in range(packs)
    ]
    two = [
        [put(b2.at[p, t], r2.at[p, t], p2_s.at[p, t], p2_r.at[p, t], d_e, z) for t in range(4)]
        for p in range(packs)
    ]
    three = [
        [put(b3.at[p, t], r3.at[p, t], p3_s.at[p, t], p3_r.at[p, t], d_f, z) for t in range(4)]
        for p in range(packs)
    ]

    def four(p, t, way):
        to = jnp.minimum(z + 1, 3) if way == 0 else jnp.maximum(z - 1, 0)
        return put(b4.at[p, way, t], r4.at[p, way, t], p4_s.at[p, way, t], p4_r.at[p, way, t], d, to)

    load = pltpu.make_async_copy(dt, ds, t_l)
    load.start()
    for p in range(packs):
        for t in range(4):
            one[p][t].start()
            fetch[p][t].start()

    small = [
        put(sv.at[:, 1 - core], q1, v_s.at[0], v_r.at[0], pal, z),
        put(c2, q2, v_s.at[1], v_r.at[1], d_e, z),
        put(c3, q3, v_s.at[2], v_r.at[2], d_f, z),
    ]
    small_z = [
        put(sk, q4.at[j - 1], v_s.at[2 + j], v_r.at[2 + j], d, lax.rem(z + j, 4)) for j in range(1, 4)
    ]
    small[0].start()

    def token(k, way):
        to = jnp.minimum(z + 1, 3) if way == 0 else jnp.maximum(z - 1, 0)
        slot = k if way == 0 else jnp.where(k // chunks == to, total + k % chunks, k)
        return put(ds.at[k], dr.at[slot], t_s.at[k], t_r.at[slot], d, to)

    def token_in(k, way):
        slot = k if way == 0 else jnp.where(k // chunks == z, total + k % chunks, k)
        return put(ds.at[k], dr.at[slot], t_s.at[k], t_r.at[slot], d, z), slot

    def sends(k, way):
        o = k // chunks
        if way == 0:
            low = 0 if k < total - edge else 1
            return (z >= low) & (z < o) & (o > low)
        high = 3 if k >= edge else 2
        return (z <= high) & (z > o) & (o < high)

    def starts(k, way):
        if way == 0:
            return z == (0 if k < total - edge else 1)
        return z == (3 if k >= edge else 2)

    right_order = [k for o in (3, 2, 1) for k in range(o * chunks, (o + 1) * chunks)]
    left_order = [total - 1 - k for k in right_order]
    load.wait()
    for kr, kl in zip(right_order, left_order):
        for k, way in ((kr, 0), (kl, 1)):

            @pl.when(sends(k, way) & starts(k, way))
            def _():
                token(k, way).start()

    def forward_tokens(at):
        for k, way in [(k, 0) for k in right_order] + [(k, 1) for k in left_order]:
            pos = at if way == 0 else 3 - at

            @pl.when(sends(k, way) & jnp.logical_not(starts(k, way)) & (z == pos))
            def _():
                got, slot = token_in(k, way)
                got.wait_recv()
                ds[k] = (ds[k].astype(F32) + dr[slot].astype(F32)).astype(BF16)
                token(k, way).start()

    def stage_two(p):
        for t in range(4):
            fetch[p][t].wait()
            one[p][t].wait_recv()
            for i, x in enumerate((e, ef)):
                b2[p, t, i] = (up(gk.at[p, t, x]) + up(r1.at[p, t, x])).astype(BF16)
            two[p][t].start()

    def stage_three(p):
        for t in range(4):
            two[p][t].wait_recv()
            b3[p, t] = (up(gk.at[p, t, f]) + up(r1.at[p, t, f]) + up(r2.at[p, t, 1])).astype(BF16)
            three[p][t].start()

    def stage_kept(p):
        for t in range(4):
            three[p][t].wait_recv()
            s3[p, t] = up(gk.at[p, t, xy]) + up(r1.at[p, t, xy]) + up(r2.at[p, t, 0]) + up(r3.at[p, t])

    def stage_four(p, t, way):
        goes = (t > z) if way == 0 else (t < z)
        inner = z > 0 if way == 0 else z < 3

        @pl.when(goes & inner)
        def _():
            four(p, t, way).wait_recv()
            b4[p, way, t] = (s3[p, t] + up(r4.at[p, way, t])).astype(BF16)

        @pl.when(goes & jnp.logical_not(inner))
        def _():
            b4[p, way, t] = s3[p, t].astype(BF16)

        @pl.when(goes)
        def _():
            four(p, t, way).start()

    for p in range(packs):
        stage_two(p)
        if p == 0:
            small[0].wait_recv()
            for i, x in enumerate((e, ef)):
                c2[i] = sv[x, core] + q1[x]
            small[1].start()
    forward_tokens(1)
    for p in range(packs):
        stage_three(p)
        if p == 0:
            small[1].wait_recv()
            c3[...] = sv[f, core] + q1[f] + q2[1]
            small[2].start()
    forward_tokens(2)
    small[2].wait_recv()
    sk[...] = sv[xy, core] + q1[xy] + q2[0] + q3[...]
    for copy in small_z:
        copy.start()
    for p in range(packs):
        stage_kept(p)
        for i in range(3):
            stage_four(p, 3 - i, 0)
            stage_four(p, i, 1)
    for copy in small_z:
        copy.wait_recv()
    out_s[...] = sk[...] + q4[0] + q4[1] + q4[2]
    for i in range(chunks):
        k = z * chunks + i
        rows = pl.ds(i * ROWS, ROWS)
        out_t[rows, :] = base[rows, :]
        from_left = (z > 0) & ((z > 1) | (k < total - edge))
        from_left = from_left & ((z != 1) | (k < total - edge))
        from_right = (z < 3) & ((z < 2) | (k >= edge))

        @pl.when(from_left)
        def _():
            put(ds.at[k], dr.at[k], t_s.at[k], t_r.at[k], d, z).wait_recv()
            out_t[rows, :] += dr[k].astype(F32)

        @pl.when(from_right)
        def _():
            put(ds.at[k], dr.at[total + i], t_s.at[k], t_r.at[total + i], d, z).wait_recv()
            out_t[rows, :] += dr[total + i].astype(F32)

    for p in range(packs):
        out_w[p] = s3[p, z]

        @pl.when(z > 0)
        def _():
            four(p, z, 0).wait_recv()
            out_w[p] += up(r4.at[p, 0, z])

        @pl.when(z < 3)
        def _():
            four(p, z, 1).wait_recv()
            out_w[p] += up(r4.at[p, 1, z])

    for copy in small + small_z:
        copy.wait_send()
    for p in range(packs):
        for t in range(4):
            one[p][t].wait_send()
            two[p][t].wait_send()
            three[p][t].wait_send()
            for way in range(2):

                @pl.when((t > z) if way == 0 else (t < z))
                def _():
                    four(p, t, way).wait_send()

    for k, way in [(k, 0) for k in right_order] + [(k, 1) for k in left_order]:

        @pl.when(sends(k, way))
        def _():
            token(k, way).wait_send()


def reduce_all(g, sv, dt, base):
    packs, _, _, r, c = g.shape
    rows, width = base.shape
    chunks = rows // ROWS
    dma = pltpu.SemaphoreType.DMA
    any_ = pl.BlockSpec(memory_space=pl.ANY)
    vmem = pl.BlockSpec(memory_space=pltpu.VMEM)
    vm = pltpu.VMEM
    block, sb = (r, c), sv.shape[1:]
    return pl.pallas_call(
        reduce_kernel,
        out_shape=(
            jax.ShapeDtypeStruct((packs,) + block, F32),
            jax.ShapeDtypeStruct(sb, F32),
            jax.ShapeDtypeStruct((rows, width), F32),
        ),
        in_specs=[any_, vmem, any_, vmem],
        out_specs=(vmem, vmem, vmem),
        scratch_shapes=[
            vm((packs, 4, 4) + block, BF16),
            vm((packs, 4, 4) + block, BF16),
            vm((packs, 4, 2) + block, BF16),
            vm((packs, 4, 2) + block, BF16),
            vm((packs, 4) + block, BF16),
            vm((packs, 4) + block, BF16),
            vm((packs, 4) + block, F32),
            vm((packs, 2, 4) + block, BF16),
            vm((packs, 2, 4) + block, BF16),
            vm((4 * chunks, ROWS, width), BF16),
            vm((5 * chunks, ROWS, width), BF16),
            vm(sb, F32),
            vm((4,) + sb, F32),
            vm((2,) + sb, F32),
            vm(sb, F32),
            vm((2,) + sb, F32),
            vm(sb, F32),
            vm((3,) + sb, F32),
            dma((packs, 4)),
            dma((packs, 4)),
            dma((packs, 4)),
            dma((packs, 4)),
            dma((packs, 4)),
            dma((packs, 4)),
            dma((packs, 4)),
            dma((packs, 2, 4)),
            dma((packs, 2, 4)),
            dma(()),
            dma((4 * chunks,)),
            dma((5 * chunks,)),
            dma((6,)),
            dma((6,)),
        ],
        compiler_params=pltpu.CompilerParams(
            collective_id=1, has_side_effects=True, vmem_limit_bytes=VMEM_MAX
        ),
        name="reduce_all",
    )(
        g.reshape(packs, 4, 4, 2, r, c),
        sv.reshape((4, 2) + sb),
        dt.reshape(4 * chunks, ROWS, width),
        base,
    )


def parts_of(z, own):
    sure = SHORT - own
    low = z < 2
    return (
        (jnp.where(low, 0, own - sure), sure, jnp.where(low, 0, SHORT)),
        (jnp.where(low, sure, 0), own - sure, jnp.where(z == 3, SHORT, 0)),
    )


def over_keys(z, part, start, total, act):
    window = total - SHORT
    for c in range(window // KEYS):
        act(pl.multiple_of(start + c * KEYS, KEYS))
    if part == 1:

        @pl.when((z == 1) | (z == 2))
        def _():
            for c in range(window // KEYS, total // KEYS):
                act(c * KEYS)


def aug_rows(top, r):
    return jnp.concatenate([top.astype(BF16), jnp.zeros((128 - 16, r), BF16)], axis=0)


def pick_rows(rows, r):
    index = lax.broadcasted_iota(jnp.int32, (16, r), 0)
    out = jnp.zeros((16, r), F32)
    for i, row in enumerate(rows):
        out = jnp.where(index == i, jnp.broadcast_to(row, (16, r)), out)
    return out


def split3(x):
    hi = x.astype(BF16).astype(F32)
    mid = (x - hi).astype(BF16).astype(F32)
    return hi, mid, x - hi - mid


def padded(head_rows, half, aug, r):
    zero = jnp.zeros((HD, r), BF16)
    pair = [head_rows, zero] if half == 0 else [zero, head_rows]
    return jnp.concatenate(pair + [aug], axis=0)


def attention_kernel(qt, k, vt, ka, ma, mixed_t, lse, s, m, l, acc):
    z = lax.axis_index("tp")
    own, total = qt.shape[1], k.shape[0]
    pairs = k.shape[1] // 128
    for part, (row0, r, start) in enumerate(parts_of(z, own)):
        cols = pl.ds(pl.multiple_of(row0, 128), r)
        aug = aug_rows(pick_rows((ma[0:1, cols], ma[1:2, cols]), r), r)

        def one_pair(pair, carry):
            lanes = pl.ds(pl.multiple_of(pair * 128, 128), 128)
            for half in range(2):
                m[half, :, :r] = jnp.full((1, r), MASKED, F32)
                l[half, :, :r] = jnp.zeros((1, r), F32)
                acc[half, :, :r] = jnp.zeros((HD, r), F32)
            qs = [
                padded(qt[pl.ds(pl.multiple_of(pair * 128 + half * HD, HD), HD), cols], half, aug, r)
                for half in range(2)
            ]

            def scores(key0):
                keys = pl.ds(key0, KEYS)
                left = jnp.concatenate([k[keys, lanes], ka[keys, :]], axis=1)
                for half in range(2):
                    score = dot(left, qs[half])
                    s[half, keys, :r] = score
                    m[half, :, :r] = jnp.maximum(m[half, :, :r], jnp.max(score, axis=0, keepdims=True))

            over_keys(z, part, start, total, scores)
            tops = [m[half, :, :r] for half in range(2)]

            def mix(key0):
                keys = pl.ds(key0, KEYS)
                for half in range(2):
                    raised = jnp.exp(s[half, keys, :r] - tops[half])
                    l[half, :, :r] += jnp.sum(raised, axis=0, keepdims=True)
                    values = vt[pl.ds(pl.multiple_of(pair * 128 + half * HD, HD), HD), keys]
                    acc[half, :, :r] += dot(values, raised.astype(BF16))

            over_keys(z, part, start, total, mix)
            for half in range(2):
                sums = l[half, :, :r]
                rows = pl.ds(pl.multiple_of(pair * 128 + half * HD, HD), HD)
                mixed_t[rows, cols] = acc[half, :, :r] / sums
                lse[pair, half : half + 1, cols] = tops[half] + jnp.log(sums)
            return carry

        lax.fori_loop(0, pairs, one_pair, 0)


def attention(qt, k, vt, ka, ma):
    width, own = qt.shape
    total = k.shape[0]
    widest = max(SHORT - own, own - (SHORT - own))
    vm = pltpu.VMEM
    return pl.pallas_call(
        attention_kernel,
        out_shape=(
            jax.ShapeDtypeStruct((width, own), F32),
            jax.ShapeDtypeStruct((width // 128, 8, own), F32),
        ),
        in_specs=[pl.BlockSpec(memory_space=pltpu.VMEM)] * 5,
        out_specs=(pl.BlockSpec(memory_space=pltpu.VMEM),) * 2,
        scratch_shapes=[
            vm((2, total, widest), F32),
            vm((2, 1, widest), F32),
            vm((2, 1, widest), F32),
            vm((2, HD, widest), F32),
        ],
        compiler_params=pltpu.CompilerParams(vmem_limit_bytes=VMEM_MAX),
        name="attention",
    )(qt, k, vt, ka, ma)


def attention_back_kernel(qt, q, k, kt, v, ka, ma, mixed_t, lse, dmt, dm, dqt, dk, dv, dka, dva, dqa):
    z = lax.axis_index("tp")
    own, total = qt.shape[1], k.shape[0]
    pairs = k.shape[1] // 128

    def one_pair(pair, carry):
        lanes = pl.ds(pl.multiple_of(pair * 128, 128), 128)
        dka[...] = jnp.zeros_like(dka)
        dva[...] = jnp.zeros_like(dva)
        for part, (row0, r, start) in enumerate(parts_of(z, own)):
            cols = pl.ds(pl.multiple_of(row0, 128), r)
            qs, gs, qm, gm = [], [], [], []
            low = lax.broadcasted_iota(jnp.int32, (r, 128), 1) < HD
            for half in range(2):
                rows = pl.ds(pl.multiple_of(pair * 128 + half * HD, HD), HD)
                delta = jnp.sum(dmt[rows, cols].astype(F32) * mixed_t[rows, cols], axis=0, keepdims=True)
                total_log = lse[pair, half : half + 1, cols]
                q_aug = pick_rows((ma[0:1, cols], ma[1:2, cols]) + split3(-total_log), r)
                zero = jnp.zeros((1, r), F32)
                g_aug = pick_rows((zero, zero) + split3(-delta), r)
                qs.append(padded(qt[rows, cols], half, aug_rows(q_aug, r), r))
                gs.append(padded(dmt[rows, cols], half, aug_rows(g_aug, r), r))
                mine = low if half == 0 else jnp.logical_not(low)
                here = pl.ds(pl.multiple_of(row0, 128), r)
                qm.append(jnp.where(mine, q[here, lanes], jnp.zeros((), BF16)))
                gm.append(jnp.where(mine, dm[here, lanes], jnp.zeros((), BF16)))
                dqa[half, :, :r] = jnp.zeros((HD, r), F32)

            def step(key0):
                keys = pl.ds(key0, KEYS)
                k_left = jnp.concatenate([k[keys, lanes], ka[keys, :]], axis=1)
                v_left = jnp.concatenate([v[keys, lanes], ka[keys, :]], axis=1)
                for half in range(2):
                    share = jnp.exp(dot(k_left, qs[half]))
                    slope = (share * dot(v_left, gs[half])).astype(BF16)
                    dva[keys, :] += dot(share.astype(BF16), gm[half])
                    dka[keys, :] += dot(slope, qm[half])
                    rows = pl.ds(pl.multiple_of(pair * 128 + half * HD, HD), HD)
                    dqa[half, :, :r] += dot(kt[rows, keys], slope)

            over_keys(z, part, start, total, step)
            for half in range(2):
                rows = pl.ds(pl.multiple_of(pair * 128 + half * HD, HD), HD)
                dqt[rows, cols] = (dqa[half, :, :r] * HD ** (-0.5)).astype(BF16)
        dk[:, lanes] = dka[...].astype(BF16)
        dv[:, lanes] = dva[...].astype(BF16)
        return carry

    lax.fori_loop(0, pairs, one_pair, 0)


def attention_back(qt, q, k, kt, v, ka, ma, mixed_t, lse, dmt, dm):
    width, own = qt.shape
    total = k.shape[0]
    widest = max(SHORT - own, own - (SHORT - own))
    vm = pltpu.VMEM
    return pl.pallas_call(
        attention_back_kernel,
        out_shape=(
            jax.ShapeDtypeStruct((width, own), BF16),
            jax.ShapeDtypeStruct((total, width), BF16),
            jax.ShapeDtypeStruct((total, width), BF16),
        ),
        in_specs=[pl.BlockSpec(memory_space=pltpu.VMEM)] * 11,
        out_specs=(pl.BlockSpec(memory_space=pltpu.VMEM),) * 3,
        scratch_shapes=[
            vm((total, 128), F32),
            vm((total, 128), F32),
            vm((2, HD, widest), F32),
        ],
        compiler_params=pltpu.CompilerParams(vmem_limit_bytes=VMEM_MAX),
        name="attention_back",
    )(qt, q, k, kt, v, ka, ma, mixed_t, lse, dmt, dm)


def body(
    tokens, w_query, w_key, w_value, b_query, b_value, w_out, b_out, gain_attn, shift_attn,
    w_up, b_up, w_down, b_down, gain_ffn, shift_ffn, lengths, deal_order, cotangent,
):
    own, width = tokens.shape
    n_tp, n_dp = lax.axis_size("tp"), lax.axis_size("dp")
    z, g = lax.axis_index("tp"), lax.axis_index("dp")
    total = own * n_tp
    r, hw = w_query.shape
    direct = n_tp == 4 and n_dp == 8 and r % 16 == 0

    own_w = jnp.stack([jnp.concatenate([w_query, w_key, w_value, w_out], axis=1), w_up, w_down])
    vectors = (b_query, b_value, b_out, gain_attn, shift_attn, b_down, gain_ffn, shift_ffn, b_up)
    own_s = jnp.concatenate(vectors)
    n_small = own_s.shape[0]
    if direct:
        padded_s = jnp.pad(own_s, (0, 2048 - n_small)).reshape(16, 128)
        w, s, x = gather_all(own_w, padded_s, tokens)
        s = s.reshape(n_dp, 2048)
    else:
        w = lax.all_gather(own_w, ("tp", "dp"), axis=0).reshape((n_tp, n_dp) + own_w.shape)
        w = jnp.moveaxis(w, 2, 0)
        s = lax.all_gather(own_s, "dp", axis=0)
        x = lax.all_gather(tokens, "tp", axis=0, tiled=True)
    w = w.reshape(3, n_tp, width, w_up.shape[1])
    small = [s[:, i * r : (i + 1) * r].reshape(width).astype(F32) for i in range(8)]
    bq, bv, bo, g1, h1, bd, g2, h2 = small
    bu = s[:, 8 * r : n_small].reshape(-1).astype(F32)
    wq, wk, wv, wo = (
        w[0, :, :, i * hw : (i + 1) * hw].transpose(1, 0, 2).reshape(width, width) for i in range(4)
    )

    pair = lax.dynamic_slice_in_dim(deal_order, 2 * g, 1)
    first_len = jnp.sum(jnp.where(jnp.arange(lengths.shape[0], dtype=jnp.int32) == pair[0], lengths, 0))
    key_seg = jnp.arange(total, dtype=jnp.int32)[:, None] >= first_len
    lane = jnp.arange(128, dtype=jnp.int32)[None, :]
    ka = jnp.where(lane == 0, ~key_seg, jnp.where(lane == 1, key_seg, (lane >= 2) & (lane < 5))).astype(BF16)
    row_seg = (z * own + jnp.arange(own, dtype=jnp.int32))[None, :] >= first_len
    sub = jnp.arange(8, dtype=jnp.int32)[:, None]
    ma = jnp.where(((sub == 0) & row_seg) | ((sub == 1) & ~row_seg), MASKED, 0.0).astype(F32)

    q = (dot(tokens, wq) + bq).astype(BF16) * jnp.asarray(HD ** (-0.5), BF16)
    k = dot(x, wk).astype(BF16)
    v = (dot(x, wv) + bv).astype(BF16)
    qt = q.T
    mixed_t, lse = attention(qt, k, v.T, ka, ma)
    mixed = mixed_t.T.astype(BF16)
    first_residual = tokens.astype(F32) + contract_last(mixed, wo) + bo
    xhat1, inv1 = normalize_layer(first_residual)
    y1 = xhat1 * g1 + h1
    y1r = y1.astype(BF16)

    u = [dot(y1r, w[1, t]) + bu.reshape(n_tp, -1)[t] for t in range(n_tp)]
    hr = [jax.nn.gelu(a, approximate=False).astype(BF16) for a in u]
    ffn = sum(contract_last(hr[t], w[2, t]) for t in range(n_tp))
    xhat2, inv2 = normalize_layer(y1 + ffn + bd)
    encoder_output = (xhat2 * g2 + h2).astype(BF16)

    grad = cotangent.astype(F32)
    dr2 = normalize_backward(grad, xhat2, inv2, g2)
    dfr = dr2.astype(BF16)
    du = [(dot(dfr, w[2, t]) * gelu_slope(u[t])).astype(BF16) for t in range(n_tp)]
    dy1 = dr2 + sum(contract_last(du[t], w[1, t]) for t in range(n_tp))
    dr1 = normalize_backward(dy1, xhat1, inv1, g1)
    dar = dr1.astype(BF16)
    dm = dot(dar, wo).astype(BF16)
    dqt, dk, dv = attention_back(qt, q, k, k.T, v, ka, ma, mixed_t, lse, dm.T, dm)
    dq = dqt.T
    base = dr1 + contract_last(dq, wq)
    far = contract_last(dk, wk) + contract_last(dv, wv)
    base = base + lax.dynamic_slice_in_dim(far, z * own, own)
    dt = far.astype(BF16)
    gq, gk, gv = contract_first(tokens, dq), contract_first(x, dk), contract_first(x, dv)
    go = contract_first(dar, mixed)
    ga = jnp.stack(
        [
            jnp.concatenate([m[:, t * hw : (t + 1) * hw] for m in (gq, gk, gv, go)], axis=1)
            for t in range(n_tp)
        ]
    )
    gu = jnp.stack([contract_first(y1r, du[t]) for t in range(n_tp)])
    gd = jnp.stack([contract_first(dfr, hr[t]) for t in range(n_tp)])
    sums = [
        jnp.sum(dq, axis=0, dtype=F32),
        jnp.sum(dv, axis=0, dtype=F32),
        jnp.sum(dar, axis=0, dtype=F32),
        jnp.sum(dy1 * xhat1, axis=0),
        jnp.sum(dy1, axis=0),
        jnp.sum(dfr, axis=0, dtype=F32),
        jnp.sum(grad * xhat2, axis=0),
        jnp.sum(grad, axis=0),
    ]
    sums = [a.reshape(n_dp, r) for a in sums]
    sums.append(jnp.concatenate([jnp.sum(a, axis=0, dtype=F32) for a in du]).reshape(n_dp, -1))
    sv = jnp.concatenate(sums, axis=1)
    if direct:
        grads = jnp.stack([ga, gu, gd]).astype(BF16).reshape(3, n_tp, n_dp, r, -1)
        sv = jnp.pad(sv, ((0, 0), (0, 2048 - n_small))).reshape(n_dp, 16, 128)
        gw, gs, grad_tokens = reduce_all(grads, sv, dt, base)
        gs = gs.reshape(-1)
    else:
        grads = jnp.stack([ga, gu, gd], axis=1).reshape(n_tp, 3, n_dp, r, -1)
        grads = jnp.moveaxis(grads, 1, 2).reshape(n_tp * n_dp, 3, r, -1)
        gw = lax.psum_scatter(grads, ("tp", "dp"), scatter_dimension=0, tiled=True)[0]
        gs = lax.psum_scatter(lax.psum(sv, "tp"), "dp", scatter_dimension=0, tiled=True)[0]
        others = jnp.where(jnp.arange(total)[:, None] // own == z, jnp.zeros((), BF16), dt)
        grad_tokens = base + lax.psum_scatter(others, "tp", scatter_dimension=0, tiled=True).astype(F32)
    gs = [gs[i * r : (i + 1) * r] for i in range(8)] + [gs[8 * r : n_small]]
    a = gw[0]
    return (
        encoder_output, grad_tokens,
        a[:, :hw], a[:, hw : 2 * hw], a[:, 2 * hw : 3 * hw], gs[0], gs[1],
        a[:, 3 * hw :], gs[2], gs[3], gs[4],
        gw[1], gs[8], gw[2], gs[5], gs[6], gs[7],
    )


def solution(mesh):
    rows, block, vector = P(("dp", "tp"), None), P("dp", "tp"), P("dp")
    in_specs = (
        rows, block, block, block, vector, vector, block, vector, vector, vector,
        block, vector, block, vector, vector, vector, P(), P(), rows,
    )
    out_specs = (
        rows, rows, block, block, block, vector, vector, block, vector, vector, vector,
        block, vector, block, vector, vector, vector,
    )
    return jax.shard_map(body, mesh=mesh, in_specs=in_specs, out_specs=out_specs, check_vma=False)
```

time: 1460 us -> 523 us (0.36)
  waiting for transfers between devices: 870 us -> 0 us
  Pallas kernels: 0 us -> 282 us
  matrix products: 295 us -> 121 us
  blocking collectives: 109 us -> 0 us
  other arithmetic: 116 us -> 37.4 us
  local copies, waits for them, and re-layouts: 42.9 us -> 71 us
  between operations: 18.4 us -> 1.65 us
    reduce_scatter x7 -> x0, waiting for transfers between devices: 525 us -> none  [the longest x1 136 us: body(): lax.psum_scatter(contract_last(hidden, down_weight), 'tp', scatter_dimens...]
    pallas_call x0 -> x4, Pallas kernels: none -> 282 us  [the longest x1 115 us: reduce_all(): pl.pallas_call(reduce_kernel, out_shape=(jax.ShapeDtypeStruct((packs,) +...]
    all_gather x6 -> x0, waiting for transfers between devices: 227 us -> none  [the longest x1 77 us: body(): lax.all_gather(second_residual_gradient.astype(jnp.bfloat16), 'tp', axis=...]
    dot_general x41 -> x12, matrix products: 238 us -> 57.6 us  [dot(): return jnp.dot(left, right, preferred_element_type=F32)]
    unnamed x19 -> x0, waiting for transfers between devices: 118 us -> none
    convert_element_type x29 -> x4, other arithmetic: 61.8 us -> 3.12 us  [the longest x1 2.67 us: body(): jnp.where(lane == 0, ~key_seg, jnp.where(lane == 1, key_seg, (lane >= 2)...]
    unnamed x2 -> x0, blocking collectives: 53.2 us -> none
    all_gather x5 -> x0, blocking collectives: 46.3 us -> none  [the longest x1 10.4 us: body(): lax.all_gather(params[3], 'dp', axis=0, tiled=True)]
  transfers between devices with their start and end apart: 16 -> 0, of which waited for: 14 -> 0; matrix products, arithmetic and copies ran while one was open for 6% -> 0% of each run, Pallas kernels for 0% -> 0%
where the time goes in v1:
time: 523 us; the launch traced here: 513 us
  Pallas kernels  282 us (54%)
  matrix products  121 us (23%)
  local copies, waits for them, and re-layouts  71 us (14%)
  other arithmetic  37.4 us (7%)
    pallas_call x1, Pallas kernels, reduce_all(): pl.pallas_call(reduce_kernel, out_shape=(jax.ShapeDtypeStruct((packs,) +...  115 us
    pallas_call x1, Pallas kernels, gather_all(): pl.pallas_call(gather_kernel, out_shape=(jax.ShapeDtypeStruct((packs, 4,...  97.7 us
    dot_general x12, matrix products, dot(): return jnp.dot(left, right, preferred_element_type=F32)  57.6 us
    pallas_call x1, Pallas kernels, attention_back(): pl.pallas_call(attention_back_kernel, out_shape=(jax.ShapeDtypeStruct((wi...  43.6 us
    dot_general x12, matrix products, contract_first(): lax.dot_general(left, right, (((0,), (0,)), ((), ())), preferred_element_...  33.2 us
    dot_general x12, matrix products, contract_last(): lax.dot_general(left, right, (((1,), (1,)), ((), ())), preferred_element_...  30.3 us
    pallas_call x1, Pallas kernels, attention(): pl.pallas_call(attention_kernel, out_shape=(jax.ShapeDtypeStruct((width,...  25.4 us
    unnamed x128, local copies, waits for them, and re-layouts  14.6 us

profile of v1, /device:TPU:0, one launch (start us, length us, event | category | flops | bytes accessed | tf_op | source)
XLA Modules:
  0.0 513.1 jit_solution(2759069837992897046)
XLA Ops:
  4.5 6.1 %concatenate.46 = bf16[1152]{0:T(1024)(128)(2,1)S(1)} concatenate(bf16[96]{0:T(256)(128)(2,1)} %param.23, bf16[96]{0:T(256)(128)(2,1)} %param.24, bf16[96]{0:T(256)(128)(2,1)} %param.26, bf16[96]{0:T(256)(128)(2,1)} %param.27, bf16[96]{0:T(256)(128)(2,1)} %param.28, bf16[96]{0:T(256)(128)(2,1)} %param.32, bf16[96]{0:T(256)(128)(2,1)} %param.33, bf16[96]{0:T(256)(128)(2,1)} %param.34, ...), dimensions={0} | concatenate | bytes 4608 | tf_op jit(solution)/shard_map/concatenate | solution.py:822
  15.3 2.7 select_convert_fusion.ka
  18.0 97.7 %gather_all.1 = (bf16[3,4,8,96,768]{4,3,2,1,0:T(8,128)(2,1)}, bf16[8,16,128]{2,1,0:T(8,128)(2,1)}, bf16[2560,768]{1,0:T(8,128)(2,1)}) custom-call(bf16[3,96,768]{2,1,0:T(8,128)(2,1)} %pad_maximum_fusion.4.own_w, bf16[16,128]{1,0:T(8,128)(2,1)} %pad_bitcast_fusion.1.own_s, bf16[640,768]{1,0:T(8,128)(2,1)} %own_t.1), custom_call_target="tpu_custom_call" | custom-call | tf_op jit(solution)/shard_map/gather_all/pallas_call | solution.py:301
  123.1 6.5 %fusion.93 = (bf16[1,4,768,192]{3,2,1,0:T(8,128)(2,1)}, bf16[1,4,768,192]{3,2,1,0:T(8,128)(2,1)}, bf16[1,4,768,192]{3,2,1,0:T(8,128)(2,1)S(1)}, bf16[1,4,768,192]{3,2,1,0:T(8,128)(2,1)S(1)}) fusion(bf16[3,4,768,768]{3,2,1,0:T(8,128)(2,1)} %bitcast.171), kind=kLoop, calls=%fused_computation.224 | loop fusion | bytes 9437184 | tf_op jit(solution)/shard_map/slice | solution.py:838
  129.6 2.5 copy.68
  132.1 2.5 copy.67
  136.1 3.5 fusion.73
  139.6 2.3 copy.53.qt
  143.4 7.4 %add_convert_fusion.v = bf16[2560,768]{1,0:T(8,128)(2,1)} fusion(bf16[2560,768]{1,0:T(8,128)(2,1)} %get-tuple-element.30, bf16[768,768]{0,1:T(8,128)(2,1)S(1)} %bitcast.194, f32[768]{0:T(1024)S(1)} %reshape.322), kind=kOutput, calls=%fused_computation.2 | convolution fusion | flops 3023831040 | bytes 9047040 | tf_op jit(solution)/shard_map/dot_general | solution.py:25
  150.8 4.8 convolution_convert_fusion
  155.6 6.3 %copy.54.k = bf16[2560,768]{1,0:T(8,128)(2,1)} copy(bf16[2560,768]{0,1:T(8,128)(2,1)} %convolution_convert_fusion) | data formatting | bytes 7864320 | tf_op jit(solution)/shard_map/convert_element_type | solution.py:851
  161.9 6.3 %copy.55.vt = bf16[768,2560]{1,0:T(8,128)(2,1)} copy(bf16[768,2560]{0,1:T(8,128)(2,1)} %bitcast.169) | data formatting | bytes 7864320 | tf_op jit(solution)/shard_map/convert_element_type | solution.py:852
  168.2 25.4 %attention.1 = (f32[768,640]{1,0:T(8,128)}, f32[6,8,640]{2,1,0:T(8,128)}) custom-call(bf16[768,640]{1,0:T(8,128)(2,1)} %copy.53.qt, bf16[2560,768]{1,0:T(8,128)(2,1)} %copy.54.k, bf16[768,2560]{1,0:T(8,128)(2,1)} %copy.55.vt, bf16[2560,128]{1,0:T(8,128)(2,1)} %select_convert_fusion.ka, f32[8,640]{1,0:T(8,128)} %or_select_fusion.ma), custom_call_target="tpu_custom_call" | custom-call | tf_op jit(solution)/shard_map/attention/pallas_call | solution.py:715
  193.6 3.3 fusion.101
  198.0 7.7 %fusion.17 = (bf16[640,768]{1,0:T(8,128)(2,1)S(1)}, f32[640,768]{1,0:T(8,128)}) fusion(f32[768]{0:T(1024)S(1)} %copy-done.39, bf16[640,768]{1,0:T(8,128)(2,1)S(1)} %fusion.71, bf16[3,4,768,768]{3,2,1,0:T(8,128)(2,1)} %bitcast.172), kind=kOutput, calls=%fused_computation.33 | convolution fusion | flops 787415040 | bytes 5114880 | tf_op jit(solution)/shard_map/dot_general | solution.py:25
  205.7 5.9 %fusion.14 = (bf16[640,768]{1,0:T(8,128)(2,1)S(1)}, f32[640,768]{1,0:T(8,128)}) fusion(f32[768]{0:T(1024)S(1)} %copy-done.38, bf16[640,768]{1,0:T(8,128)(2,1)S(1)} %fusion.71, bf16[3,4,768,768]{3,2,1,0:T(8,128)(2,1)S(1)} %bitcast.183), kind=kOutput, calls=%fused_computation.30 | convolution fusion | flops 787415040 | bytes 5115904 | tf_op jit(solution)/shard_map/dot_general | solution.py:25
  212.7 6.4 %fusion.11 = (bf16[640,768]{1,0:T(8,128)(2,1)S(1)}, f32[640,768]{1,0:T(8,128)}) fusion(f32[768]{0:T(1024)S(1)} %copy-done.37, bf16[640,768]{1,0:T(8,128)(2,1)S(1)} %fusion.71, bf16[3,4,768,768]{3,2,1,0:T(8,128)(2,1)S(1)} %bitcast.185), kind=kOutput, calls=%fused_computation.27 | convolution fusion | flops 787415040 | bytes 5115904 | tf_op jit(solution)/shard_map/dot_general | solution.py:25
  220.0 6.0 %fusion.8 = (bf16[640,768]{1,0:T(8,128)(2,1)S(1)}, f32[640,768]{1,0:T(8,128)}) fusion(f32[768]{0:T(1024)S(1)} %copy-done.36, bf16[640,768]{1,0:T(8,128)(2,1)S(1)} %fusion.71, bf16[3,4,768,768]{3,2,1,0:T(8,128)(2,1)S(1)} %bitcast.187), kind=kOutput, calls=%fused_computation.24 | convolution fusion | flops 787415040 | bytes 5115904 | tf_op jit(solution)/shard_map/dot_general | solution.py:25
  233.7 3.1 convert_reduce_fusion.6
  236.8 3.9 convert_reduce_fusion.2
  240.8 3.7 convert_reduce_fusion.3
  244.5 3.7 convert_reduce_fusion.4
  248.2 3.7 convert_reduce_fusion.5
  253.2 3.8 convolution_convert_fusion.4
  257.0 2.1 convolution_convert_fusion.5
  261.3 2.1 convolution_convert_fusion.7
  263.4 2.1 convolution_convert_fusion.8
  265.6 2.2 convolution_convert_fusion.9
  267.7 2.3 fusion.80
  270.1 2.1 convolution_convert_fusion.10
  272.2 2.1 convolution_convert_fusion.11
  274.3 2.2 fusion.74
  276.6 2.4 fusion.77
  279.0 4.9 multiply_reduce_fusion
  284.5 2.2 convert_reduce_fusion.7
  290.8 43.6 %attention_back.1 = (bf16[768,640]{1,0:T(8,128)(2,1)}, bf16[2560,768]{1,0:T(8,128)(2,1)}, bf16[2560,768]{1,0:T(8,128)(2,1)}) custom-call(bf16[768,640]{1,0:T(8,128)(2,1)} %copy.53.qt, bf16[640,768]{1,0:T(8,128)(2,1)} %bitcast.198, bf16[2560,768]{1,0:T(8,128)(2,1)} %copy.54.k, bf16[768,2560]{1,0:T(8,128)(2,1)} %bitcast.170, ...), custom_call_target="tpu_custom_call" | custom-call | tf_op jit(solution)/shard_map/attention_back/pallas_call | solution.py:790
  334.4 3.2 convolution_convert_fusion.3
  339.5 2.7 convert_reduce_fusion
  343.1 6.7 %convolution_convert_fusion.2 = bf16[768,768]{0,1:T(8,128)(2,1)S(1)} fusion(bf16[2560,768]{1,0:T(8,128)(2,1)} %get-tuple-element.30, bf16[2560,768]{1,0:T(8,128)(2,1)} %get-tuple-element.34), kind=kOutput, calls=%fused_computation.143 | convolution fusion | flops 3020488704 | bytes 9043968 | tf_op jit(solution)/shard_map/dot_general | solution.py:33
  349.8 3.4 convolution_convert_fusion.1
  359.9 2.3 pad_maximum_fusion.2
  363.8 2.3 pad_maximum_fusion.1
  366.1 2.4 copy.61
  368.6 11.0 %maximum_maximum_fusion.g = bf16[3,4,4,2,96,768]{5,4,3,2,1,0:T(8,128)(2,1)} fusion(bf16[1,1,4,2,96,768]{5,4,3,2,1,0:T(8,128)(2,1)} %bitcast.200, bf16[1,1,4,2,96,768]{5,4,3,2,1,0:T(8,128)(2,1)} %bitcast.201, bf16[1,1,4,2,96,768]{5,4,3,2,1,0:T(8,128)(2,1)} %bitcast.202, bf16[1,1,4,2,96,768]{5,4,3,2,1,0:T(8,128)(2,1)} %bitcast.203, ...), kind=kLoop, calls=%fused_computation | loop fusion | flops 77856768 | bytes 28311552 | tf_op jit(solution)/shard_map/stack | solution.py:905
  379.6 3.3 fusion.104
  383.0 5.2 %fusion.103 = (bf16[2560,768]{1,0:T(8,128)(2,1)}, f32[2560,768]{1,0:T(8,128)S(1)}) fusion(f32[2560,768]{1,0:T(8,128)S(1)} %fusion.104, bf16[2560,768]{1,0:T(8,128)(2,1)S(1)} %copy-done.3, bf16[768,768]{0,1:T(8,128)(2,1)S(1)} %bitcast.195), kind=kOutput, calls=%fused_computation.234 | convolution fusion | flops 3023831040 | bytes 24772608 | tf_op jit(solution)/shard_map/dot_general | solution.py:29
  388.2 2.3 dynamic-slice_add_fusion.base
  390.5 115.2 %reduce_all.1 = (f32[3,96,768]{2,1,0:T(8,128)}, f32[16,128]{1,0:T(8,128)}, f32[640,768]{1,0:T(8,128)}) custom-call(bf16[3,4,4,2,96,768]{5,4,3,2,1,0:T(8,128)(2,1)} %maximum_maximum_fusion.g, f32[4,2,16,128]{3,2,1,0:T(8,128)} %bitcast.212, bf16[20,128,768]{2,1,0:T(8,128)(2,1)} %bitcast.168, f32[640,768]{1,0:T(8,128)} %dynamic-slice_add_fusion.base), custom_call_target="tpu_custom_call" | custom-call | tf_op jit(solution)/shard_map/reduce_all/pallas_call | solution.py:561
  (201 shorter events, 55.7 us)
Async XLA Ops:
  139.6 3.8 copy-start.7
  143.4 7.4 %copy-start.14 = (bf16[1,4,768,192]{2,3,1,0:T(8,128)(2,1)S(1)}, bf16[1,4,768,192]{2,3,1,0:T(8,128)(2,1)}, u32[]{:S(2)}) copy-start(bf16[1,4,768,192]{2,3,1,0:T(8,128)(2,1)} %copy.67) | copy-start | bytes 3538948
  143.4 7.4 %copy-start.40 = (bf16[2560,768]{1,0:T(8,128)(2,1)S(1)}, bf16[2560,768]{1,0:T(8,128)(2,1)}, u32[]{:S(2)}) copy-start(bf16[2560,768]{1,0:T(8,128)(2,1)} %get-tuple-element.30) | copy-start | bytes 11796484
  197.6 8.1 %slice-start = ((s8[14155776]{0:T(1024)(128)(4,1)}), s8[4194304]{0:T(1024)(128)(4,1)S(1)}, s32[]{:S(2)}) async-start(s8[14155776]{0:T(1024)(128)(4,1)} %bitcast.181), calls=%async_computation | async-start | bytes 8388608
  198.0 22.1 %copy-start.18 = (bf16[640,768]{1,0:T(8,128)(2,1)}, bf16[640,768]{1,0:T(8,128)(2,1)S(1)}, u32[]{:S(2)}) copy-start(bf16[640,768]{1,0:T(8,128)(2,1)S(1)} %fusion.71) | copy-start | bytes 2949124
  198.0 7.7 %slice-start.1 = ((s8[14155776]{0:T(1024)(128)(4,1)}), s8[4194304]{0:T(1024)(128)(4,1)S(1)}, s32[]{:S(2)}) async-start(s8[14155776]{0:T(1024)(128)(4,1)} %bitcast.181), calls=%async_computation.1 | async-start | bytes 8388608
  198.0 7.7 %slice-start.2 = ((s8[14155776]{0:T(1024)(128)(4,1)}), s8[4194304]{0:T(1024)(128)(4,1)S(1)}, s32[]{:S(2)}) async-start(s8[14155776]{0:T(1024)(128)(4,1)} %bitcast.181), calls=%async_computation.2 | async-start | bytes 8388608
  198.0 7.7 %slice-start.3 = ((s8[14155776]{0:T(1024)(128)(4,1)}), s8[1572864]{0:T(1024)(128)(4,1)S(1)}, s32[]{:S(2)}) async-start(s8[14155776]{0:T(1024)(128)(4,1)} %bitcast.181), calls=%async_computation.3 | async-start | bytes 3145728
  198.0 7.7 %copy-start.38 = (f32[768]{0:T(1024)S(1)}, f32[768]{0:T(1024)}, u32[]{:S(2)}) copy-start(f32[768]{0:T(1024)} %slice.234) | copy-start | bytes 9220
  205.7 22.3 %copy-start.20 = (bf16[640,768]{1,0:T(8,128)(2,1)}, bf16[640,768]{1,0:T(8,128)(2,1)S(1)}, u32[]{:S(2)}) copy-start(bf16[640,768]{1,0:T(8,128)(2,1)S(1)} %get-tuple-element.107) | copy-start | bytes 2949124
  229.5 2.9 copy-start
  229.5 1.9 copy-start.6
  229.5 1.9 copy-start.25
  229.9 3.8 copy-start.35
  233.7 3.1 copy-start.55
  236.8 11.3 %copy-start.22 = (bf16[640,768]{1,0:T(8,128)(2,1)}, bf16[640,768]{1,0:T(8,128)(2,1)S(1)}, u32[]{:S(2)}) copy-start(bf16[640,768]{1,0:T(8,128)(2,1)S(1)} %get-tuple-element.48) | copy-start | bytes 2949124
  236.8 3.9 copy-start.52
  240.8 3.7 copy-start.53
  244.5 3.7 copy-start.54
  253.2 3.8 copy-start.23
  253.2 3.8 copy-start.44
  257.0 2.1 copy-start.46
  259.1 2.1 copy-start.48
  261.3 2.2 copy-start.19
  261.3 2.2 copy-start.21
  263.4 2.1 copy-start.50
  267.7 2.3 copy-start.49
  270.1 2.1 copy-start.51
  276.6 2.4 copy-start.1
  284.5 2.3 copy-start.16
  339.4 2.9 copy-start.26
  339.4 2.9 copy-start.29
  339.4 2.9 copy-start.30
  339.4 2.9 copy-start.31
  339.5 2.9 copy-start.32
  339.5 2.9 copy-start.33
  339.5 2.9 copy-start.34
  343.1 6.7 %copy-start.2 = (bf16[2560,768]{1,0:T(8,128)(2,1)S(1)}, bf16[2560,768]{1,0:T(8,128)(2,1)}, u32[]{:S(2)}) copy-start(bf16[2560,768]{1,0:T(8,128)(2,1)} %get-tuple-element.35) | copy-start | bytes 11796484
  343.1 6.7 %copy-start.41 = (bf16[2560,768]{1,0:T(8,128)(2,1)S(1)}, bf16[2560,768]{1,0:T(8,128)(2,1)}, u32[]{:S(2)}) copy-start(bf16[2560,768]{1,0:T(8,128)(2,1)} %get-tuple-element.30) | copy-start | bytes 11796484
  353.3 1.9 copy-start.17
  368.5 11.0 %copy-start.15 = (bf16[1,4,768,192]{2,3,1,0:T(8,128)(2,1)S(1)}, bf16[1,4,768,192]{2,3,1,0:T(8,128)(2,1)}, u32[]{:S(2)}) copy-start(bf16[1,4,768,192]{2,3,1,0:T(8,128)(2,1)} %copy.67) | copy-start | bytes 3538948
  368.5 11.0 %copy-start.42 = (bf16[2560,768]{1,0:T(8,128)(2,1)S(1)}, bf16[2560,768]{1,0:T(8,128)(2,1)}, u32[]{:S(2)}) copy-start(bf16[2560,768]{1,0:T(8,128)(2,1)} %get-tuple-element.34) | copy-start | bytes 11796484
  379.6 3.4 copy-start.3
  379.6 3.4 copy-start.8
  382.9 5.2 %copy-start.5 = (f32[640,768]{1,0:T(8,128)S(1)}, f32[640,768]{1,0:T(8,128)}, u32[]{:S(2)}) copy-start(f32[640,768]{1,0:T(8,128)} %copy-done.4) | copy-start | bytes 5898244
  382.9 5.2 %copy-start.9 = (bf16[1,4,768,192]{2,3,1,0:T(8,128)(2,1)S(1)}, bf16[1,4,768,192]{2,3,1,0:T(8,128)(2,1)}, u32[]{:S(2)}) copy-start(bf16[1,4,768,192]{2,3,1,0:T(8,128)(2,1)} %copy.66) | copy-start | bytes 3538948
  383.0 5.2 %copy-start.12 = (bf16[768,640]{1,0:T(8,128)(2,1)S(1)}, bf16[768,640]{1,0:T(8,128)(2,1)}, u32[]{:S(2)}) copy-start(bf16[768,640]{1,0:T(8,128)(2,1)} %get-tuple-element.33) | copy-start | bytes 2949124
  505.7 5.8 %copy-start.13 = (f32[640,768]{1,0:T(8,128)S(1)}, f32[640,768]{1,0:T(8,128)}, u32[]{:S(2)}) copy-start(f32[640,768]{1,0:T(8,128)} %get-tuple-element.148) | copy-start | bytes 5898244
  (12 other events, 12.2 us)

commit v2 on v1

--- a/solution.py
+++ b/solution.py
@@ -85,36 +85,40 @@
     return (z, near, mid, far)
 
 
-def gather_kernel(
-    own_w, own_s, own_t, w, s, t,
-    wz_s, wz_r, wa_s, wa_r, wb_s, wb_r, wc_s, wc_r, tk_s, tk_r, sm_s, sm_r, lo_sem, blank, bl_sem,
+def put(src, dst, send, recv, dp, tp):
+    return pltpu.make_async_remote_copy(
+        src_ref=src, dst_ref=dst, send_sem=send, recv_sem=recv, device_id=(dp, tp), device_id_type=MESH
+    )
+
+
+def forward_kernel(
+    lengths, deal, own_w, own_s, own_t,
+    w, vec, bu, x_out, q_out, qt_out, k_out, v_out, kt_out, wd_out, mixed_t, lse,
+    wa, s, x, q, qt, k, v, kt, vt, wd, ka, sc, m, l, acc,
+    wz_s, wz_r, wa_s, wa_r, wb_s, wb_r, wc_s, wc_r, tk_s, tk_r, sm_s, sm_r, lo_sem, arr_sem, out_sem,
 ):
     z, d, core, first, second = position()
     packs = own_w.shape[0]
-    chunks = own_t.shape[0] // ROWS
+    own, width = own_t.shape
+    total = 4 * own
+    hw = width // 4
+    chunks = own // ROWS
     d1, d2 = xor(d, first), xor(d, second)
     d12 = xor(d1, second)
     pal = xor(d, 1)
+    pd, pd1, pd2, pd12 = (xor(e, 1) for e in (d, d1, d2, d12))
     order = by_distance(z)
-
-    def put(src, dst, send, recv, dp, tp):
-        return pltpu.make_async_remote_copy(
-            src_ref=src, dst_ref=dst, send_sem=send, recv_sem=recv, device_id=(dp, tp), device_id_type=MESH
-        )
+    first_len = lengths[deal[2 * d]]
 
     greet(z, d)
 
-    keep = [
-        pltpu.make_async_copy(own_w, w.at[:, z, d], lo_sem.at[0]),
-        pltpu.make_async_copy(own_s, s.at[d], lo_sem.at[1]),
-        pltpu.make_async_copy(own_t, t.at[pl.ds(pl.multiple_of(z * own_t.shape[0], ROWS), own_t.shape[0])], lo_sem.at[2]),
-    ]
-    for copy in keep:
-        copy.start()
+    def block(p, tt, e):
+        return wa.at[tt, e] if p == 0 else w.at[p - 1, tt, e]
 
     def along_z(p, tt, src, act):
-        right = put(src, w.at[p, tt, d], wz_s.at[0, p, tt], wz_r.at[p, tt], d, jnp.minimum(z + 1, 3))
-        left = put(src, w.at[p, tt, d], wz_s.at[1, p, tt], wz_r.at[p, tt], d, jnp.maximum(z - 1, 0))
+        dst = block(p, tt, d)
+        right = put(src, dst, wz_s.at[0, p, tt], wz_r.at[p, tt], d, jnp.minimum(z + 1, 3))
+        left = put(src, dst, wz_s.at[1, p, tt], wz_r.at[p, tt], d, jnp.maximum(z - 1, 0))
 
         @pl.when((tt <= z) & (z < 3))
         def _():
@@ -125,50 +129,65 @@
             act(left)
 
     def across(p, tt, src):
+        dst = block(p, tt, d)
         return (
-            put(src, w.at[p, tt, d], wa_s.at[p, tt], wa_r.at[p, tt], d1, z),
-            put(src, w.at[p, tt, d], wb_s.at[p, tt, 0], wb_r.at[p, tt, 0], d2, z),
-            put(src, w.at[p, tt, d], wc_s.at[p, tt, 0], wc_r.at[p, tt, 0], pal, z),
+            put(src, dst, wa_s.at[p, tt], wa_r.at[p, tt], d1, z),
+            put(src, dst, wb_s.at[p, tt, 0], wb_r.at[p, tt, 0], d2, z),
+            put(src, dst, wc_s.at[p, tt, 0], wc_r.at[p, tt, 0], pal, z),
         )
 
     def after_first(p, tt):
-        src = w.at[p, tt, d1]
+        src = block(p, tt, d1)
         return (
             put(src, src, wb_s.at[p, tt, 1], wb_r.at[p, tt, 1], d2, z),
             put(src, src, wc_s.at[p, tt, 1], wc_r.at[p, tt, 1], pal, z),
         )
 
     def after_second(p, tt, i):
-        src = w.at[p, tt, d2 if i == 0 else d12]
+        src = block(p, tt, d2 if i == 0 else d12)
         return put(src, src, wc_s.at[p, tt, 2 + i], wc_r.at[p, tt, 2 + i], pal, z)
 
     def source(p, j):
-        return own_w.at[p] if j == 0 else w.at[p, order[j], d]
+        return own_w.at[p] if j == 0 else block(p, order[j], d)
 
     def arrive(ref, sem):
-        return put(ref, ref, lo_sem.at[0], sem, pal, z)
+        put(ref, ref, arr_sem, sem, pal, z).wait_recv()
 
     def begin(p, j):
         if j > 0:
-            arrive(w.at[p, order[j], d], wz_r.at[p, order[j]]).wait_recv()
+            arrive(block(p, order[j], d), wz_r.at[p, order[j]])
         along_z(p, order[j], source(p, j), lambda c: c.start())
         for copy in across(p, order[j], source(p, j)):
             copy.start()
 
     def relay_first(p, j):
         tt = order[j]
-        arrive(w.at[p, tt, d1], wa_r.at[p, tt]).wait_recv()
+        arrive(block(p, tt, d1), wa_r.at[p, tt])
         for copy in after_first(p, tt):
             copy.start()
 
     def relay_second(p, j):
         tt = order[j]
         for i in range(2):
-            arrive(w.at[p, tt, d2 if i == 0 else d12], wb_r.at[p, tt, i]).wait_recv()
+            arrive(block(p, tt, d2 if i == 0 else d12), wb_r.at[p, tt, i])
             after_second(p, tt, i).start()
 
+    def from_pal(p):
+        for tt in range(4):
+            for i, e in enumerate((pd, pd2, pd1, pd12)):
+                arrive(block(p, tt, e), wc_r.at[p, tt, i])
+
+    def sent(p):
+        for j in range(4):
+            tt = order[j]
+            along_z(p, tt, source(p, j), lambda c: c.wait_send())
+            for copy in across(p, tt, source(p, j)) + after_first(p, tt):
+                copy.wait_send()
+            for i in range(2):
+                after_second(p, tt, i).wait_send()
+
     def token_slice(o, i):
-        return t.at[pl.ds(pl.multiple_of((o * chunks + i) * ROWS, ROWS), ROWS)]
+        return x.at[pl.ds(pl.multiple_of((o * chunks + i) * ROWS, ROWS), ROWS)]
 
     def token_hop(o, i, hop, step):
         src = own_t.at[pl.ds(i * ROWS, ROWS)] if hop == 0 else token_slice(o, i)
@@ -178,33 +197,38 @@
     last = SHORT // ROWS
 
     def wanted(o, i, target, step):
-        k = o * chunks + i
+        n = o * chunks + i
         if step > 0:
-            return (target <= 2) | (k >= last)
-        return (target >= 1) | (k < 4 * chunks - last)
+            return (target <= 2) | (n >= last)
+        return (target >= 1) | (n < 4 * chunks - last)
+
+    def chunk_ids(step):
+        return range(chunks) if step < 0 else reversed(range(chunks))
 
     def tokens(hop, step, act):
-        o = z - step * hop
-        target = z + step
+        o, target = z - step * hop, z + step
         valid = (o >= 0) & (o <= 3) & (target >= 0) & (target <= 3)
-        ids = range(chunks) if step < 0 else reversed(range(chunks))
-        for i in ids:
+        for i in chunk_ids(step):
 
             @pl.when(valid & wanted(o, i, target, step))
             def _():
                 act(token_hop(o, i, hop, step))
 
-    def tokens_in(hop, step):
-        o = z - step * (hop + 1)
+    def tokens_on(hop, step, onward):
+        o, target = z - step * (hop + 1), z + step
         valid = (o >= 0) & (o <= 3) & (z - step >= 0) & (z - step <= 3)
         way = 0 if step > 0 else 1
-        ids = range(chunks) if step < 0 else reversed(range(chunks))
-        for i in ids:
+        for i in chunk_ids(step):
 
             @pl.when(valid & wanted(o, i, z, step))
             def _():
-                ref = token_slice(jnp.clip(o, 0, 3), i)
-                arrive(ref, tk_r.at[way, hop, i]).wait_recv()
+                arrive(token_slice(jnp.clip(o, 0, 3), i), tk_r.at[way, hop, i])
+
+            if onward:
+
+                @pl.when(valid & (target >= 0) & (target <= 3) & wanted(o, i, target, step))
+                def _():
+                    token_hop(o, i, hop + 1, step).start()
 
     def small(stage):
         if stage == 0:
@@ -223,91 +247,266 @@
             put(s.at[d12], s.at[d12], sm_s.at[6], sm_r.at[6], pal, z),
         ]
 
-    blank[...] = jnp.zeros_like(blank)
-
-    def blanks(act):
-        for i in range(last):
-            rows = pl.ds(pl.multiple_of(jnp.where(z == 0, 4 * chunks - last + i, i) * ROWS, ROWS), ROWS)
-
-            @pl.when((z == 0) | (z == 3))
-            def _():
-                act(pltpu.make_async_copy(blank, t.at[rows], bl_sem.at[i]))
-
-    for p in range(packs):
-        begin(p, 0)
-        if p == 0:
-            for copy in small(0):
-                copy.start()
-            for step in (1, -1):
-                tokens(0, step, lambda c: c.start())
-    blanks(lambda c: c.start())
-    arrive(s.at[d1], sm_r.at[0]).wait_recv()
+    begin(0, 0)
+    for copy in small(0):
+        copy.start()
+    s[d] = own_s[...]
+    wa[z, d] = own_w[0]
+    mine = pl.ds(pl.multiple_of(z * own, ROWS), own)
+    x[mine, :] = own_t[...]
+    keep = pltpu.make_async_copy(own_w.at[pl.ds(1, packs - 1)], w.at[:, z, d], lo_sem)
+    keep.start()
+
+    @pl.when(z == 0)
+    def _():
+        x[total - SHORT :, :] = jnp.zeros((SHORT, width), BF16)
+
+    @pl.when(z == 3)
+    def _():
+        x[:SHORT, :] = jnp.zeros((SHORT, width), BF16)
+
+    lane = lax.broadcasted_iota(jnp.int32, (own, 128), 1)
+    for i in range(4):
+        late = lax.broadcasted_iota(jnp.int32, (own, 128), 0) + i * own >= first_len
+        ones = jnp.where((lane >= 2) & (lane < 5), 1.0, 0.0)
+        flags = jnp.where(lane == 0, jnp.where(late, 0.0, 1.0), jnp.where(lane == 1, jnp.where(late, 1.0, 0.0), ones))
+        ka[pl.ds(i * own, own), :] = flags.astype(BF16)
+
+    relay_first(0, 0)
+    begin(0, 1)
+    for step in (1, -1):
+        tokens(0, step, lambda c: c.start())
+    relay_second(0, 0)
+    relay_first(0, 1)
+    arrive(s.at[d1], sm_r.at[0])
     for copy in small(1):
         copy.start()
-    for p in range(packs):
-        relay_first(p, 0)
-    arrive(s.at[d2], sm_r.at[1]).wait_recv()
-    arrive(s.at[d12], sm_r.at[2]).wait_recv()
+    begin(0, 2)
+    relay_second(0, 1)
+    relay_first(0, 2)
+    begin(0, 3)
+    relay_second(0, 2)
+    relay_first(0, 3)
+    for p in range(1, packs):
+        begin(p, 0)
+    arrive(s.at[d2], sm_r.at[1])
+    arrive(s.at[d12], sm_r.at[2])
     for copy in small(2):
         copy.start()
-    for j in range(1, 4):
-        for p in range(packs):
-            begin(p, j)
-        for p in range(packs):
-            relay_second(p, j - 1)
-        for p in range(packs):
-            relay_first(p, j)
-        if j < 3:
-            for step in (1, -1):
-                tokens_in(j - 1, step)
-                tokens(j, step, lambda c: c.start())
-    for p in range(packs):
-        relay_second(p, 3)
+    relay_second(0, 3)
+    for i, e in enumerate((pd, pd2, pd1, pd12)):
+        arrive(s.at[e], sm_r.at[3 + i])
+    r = width // 8
+    for e in range(8):
+        piece = s[e].astype(F32)
+        vec[0:8, e * r : (e + 1) * r] = piece[0:8, 0:r]
+        for j in range(hw * 2 // 128):
+            col = e * hw * 2 + j * 128
+            bu[0:1, col : col + 128] = piece[8 + j : 9 + j, :]
+    from_pal(0)
+    for tt in range(4):
+        rows = wa[tt].reshape(width, width)
+        for i in range(4):
+            wd[i, :, tt * hw : (tt + 1) * hw] = rows[:, i * hw : (i + 1) * hw]
+    wd_copy = pltpu.make_async_copy(wd, wd_out, out_sem.at[0])
+    wd_copy.start()
+
+    tile = 256
+
+    def q_tile(n, carry):
+        lanes = pl.ds(pl.multiple_of(n * tile, tile), tile)
+        rows = (dot(own_t[...], wd[0, :, lanes]) + vec[0:1, lanes]).astype(BF16) * jnp.asarray(HD ** (-0.5), BF16)
+        q[:, lanes] = rows
+        qt[lanes, :] = rows.T
+        return carry
+
+    def project(o):
+        rows = pl.ds(pl.multiple_of(o * own, ROWS), own)
+
+        def kv_tile(n, carry):
+            lanes = pl.ds(pl.multiple_of(n * tile, tile), tile)
+            keys = dot(x[rows, :], wd[1, :, lanes]).astype(BF16)
+            k[rows, lanes] = keys
+            kt[lanes, rows] = keys.T
+            values = (dot(x[rows, :], wd[2, :, lanes]) + vec[1:2, lanes]).astype(BF16)
+            v[rows, lanes] = values
+            vt[lanes, rows] = values.T
+            return carry
+
+        lax.fori_loop(0, width // tile, kv_tile, 0)
+
+    lax.fori_loop(0, width // tile, q_tile, 0)
+    project(z)
     for step in (1, -1):
-        tokens_in(2, step)
-    pd, pd1, pd2, pd12 = (xor(e, 1) for e in (d, d1, d2, d12))
-    for i, e in enumerate((pd, pd2, pd1, pd12)):
-        arrive(s.at[e], sm_r.at[3 + i]).wait_recv()
-    for p in range(packs):
-        for tt in range(4):
-            for i, e in enumerate((pd, pd2, pd1, pd12)):
-                arrive(w.at[p, tt, e], wc_r.at[p, tt, i]).wait_recv()
+        tokens_on(0, step, True)
+    for p in range(1, packs):
+        relay_first(p, 0)
+
+    @pl.when(z > 0)
+    def _():
+        project(jnp.maximum(z - 1, 0))
+
+    for p in range(1, packs):
+        begin(p, 1)
+
+    @pl.when(z < 3)
+    def _():
+        project(jnp.minimum(z + 1, 3))
+
+    for p in range(1, packs):
+        relay_second(p, 0)
+        relay_first(p, 1)
+    for step in (1, -1):
+        tokens_on(1, step, False)
+    for p in range(1, packs):
+        begin(p, 2)
+    project(jnp.where(z == 0, 2, jnp.where(z == 1, 3, z - 2)))
+    outs = [
+        pltpu.make_async_copy(a, b, out_sem.at[1 + i])
+        for i, (a, b) in enumerate(((x, x_out), (q, q_out), (qt, qt_out), (k, k_out), (v, v_out), (kt, kt_out)))
+    ]
+    for copy in outs:
+        copy.start()
+
+    def both(act, j):
+        def run():
+            for p in range(1, packs):
+                act(p, j)
+
+        return run
+
+    def seq(*runs):
+        def run():
+            for one in runs:
+                one()
+
+        return run
+
+    between = {
+        (0, 0): both(relay_second, 1),
+        (0, 1): both(relay_first, 2),
+        (0, 2): both(begin, 3),
+        (0, 4): both(relay_second, 2),
+        (1, 0): both(relay_first, 3),
+        (1, 4): both(relay_second, 3),
+    }
+    pairs = width // 128
+    for part, (row0, n, start) in enumerate(parts_of(z, own)):
+        cols = pl.ds(pl.multiple_of(row0, 128), n)
+        late = lax.broadcasted_iota(jnp.int32, (1, n), 1) + (z * own + row0) >= first_len
+        masks = (jnp.where(late, MASKED, 0.0), jnp.where(late, 0.0, MASKED))
+        aug = aug_rows(pick_rows(masks, n), n)
+
+        def one_pair(pair, carry):
+            for (at, i), run in between.items():
+                if at == part:
+
+                    @pl.when(pair == i)
+                    def _():
+                        run()
+
+            attend_pair(z, part, start, pair, cols, n, aug, qt, k, vt, ka, mixed_t, lse, sc, m, l, acc)
+            return carry
+
+        lax.fori_loop(0, pairs, one_pair, 0)
+
+    for p in range(1, packs):
+        from_pal(p)
     for stage in range(3):
         for copy in small(stage):
             copy.wait_send()
-    for hop in range(3):
+    for hop in range(2):
         for step in (1, -1):
             tokens(hop, step, lambda c: c.wait_send())
     for p in range(packs):
-        for j in range(4):
-            tt = order[j]
-            along_z(p, tt, source(p, j), lambda c: c.wait_send())
-            for copy in across(p, tt, source(p, j)) + after_first(p, tt):
-                copy.wait_send()
-            for i in range(2):
-                after_second(p, tt, i).wait_send()
-    for copy in keep:
+        sent(p)
+    keep.wait()
+    wd_copy.wait()
+    for copy in outs:
         copy.wait()
-    blanks(lambda c: c.wait())
-
-
-def gather_all(own_w, own_s, own_t):
+
+
+def attend_pair(z, part, start, pair, cols, n, aug, qt, k, vt, ka, mixed_t, lse, s, m, l, acc):
+    total = k.shape[0]
+    lanes = pl.ds(pl.multiple_of(pair * 128, 128), 128)
+    for half in range(2):
+        m[half, :, :n] = jnp.full((1, n), MASKED, F32)
+        l[half, :, :n] = jnp.zeros((1, n), F32)
+        acc[half, :, :n] = jnp.zeros((HD, n), F32)
+    qs = [padded(qt[pl.ds(pl.multiple_of(pair * 128 + half * HD, HD), HD), cols], half, aug, n) for half in range(2)]
+
+    def scores(key0):
+        keys = pl.ds(key0, KEYS)
+        left = jnp.concatenate([k[keys, lanes], ka[keys, :]], axis=1)
+        for half in range(2):
+            score = dot(left, qs[half])
+            s[half, keys, :n] = score
+            m[half, :, :n] = jnp.maximum(m[half, :, :n], jnp.max(score, axis=0, keepdims=True))
+
+    over_keys(z, part, start, total, scores)
+    tops = [m[half, :, :n] for half in range(2)]
+
+    def mix(key0):
+        keys = pl.ds(key0, KEYS)
+        for half in range(2):
+            raised = jnp.exp(s[half, keys, :n] - tops[half])
+            l[half, :, :n] += jnp.sum(raised, axis=0, keepdims=True)
+            values = vt[pl.ds(pl.multiple_of(pair * 128 + half * HD, HD), HD), keys]
+            acc[half, :, :n] += dot(values, raised.astype(BF16))
+
+    over_keys(z, part, start, total, mix)
+    for half in range(2):
+        sums = l[half, :, :n]
+        rows = pl.ds(pl.multiple_of(pair * 128 + half * HD, HD), HD)
+        mixed_t[rows, cols] = acc[half, :, :n] / sums
+        lse[pair, half : half + 1, cols] = tops[half] + jnp.log(sums)
+
+
+def forward_all(lengths, deal, own_w, own_s, own_t):
     packs, r, c = own_w.shape
-    rows, width = own_t.shape
-    chunks = rows // ROWS
-    dma = pltpu.SemaphoreType.DMA
+    own, width = own_t.shape
+    total = 4 * own
+    chunks = own // ROWS
+    widest = max(SHORT - own, own - (SHORT - own))
+    dma, vm = pltpu.SemaphoreType.DMA, pltpu.VMEM
     any_ = pl.BlockSpec(memory_space=pl.ANY)
     vmem = pl.BlockSpec(memory_space=pltpu.VMEM)
+    smem = pl.BlockSpec(memory_space=pltpu.SMEM)
+    shape = jax.ShapeDtypeStruct
     return pl.pallas_call(
-        gather_kernel,
+        forward_kernel,
         out_shape=(
-            jax.ShapeDtypeStruct((packs, 4, 8, r, c), BF16),
-            jax.ShapeDtypeStruct((8,) + own_s.shape, own_s.dtype),
-            jax.ShapeDtypeStruct((4 * rows, width), BF16),
+            shape((packs - 1, 4, 8, r, c), BF16),
+            shape((8, width), F32),
+            shape((1, 4 * c), F32),
+            shape((total, width), BF16),
+            shape((own, width), BF16),
+            shape((width, own), BF16),
+            shape((total, width), BF16),
+            shape((total, width), BF16),
+            shape((width, total), BF16),
+            shape((4, width, width), BF16),
+            shape((width, own), F32),
+            shape((width // 128, 8, own), F32),
         ),
-        in_specs=[vmem, vmem, vmem],
-        out_specs=(any_, any_, any_),
+        in_specs=[smem, smem, vmem, vmem, vmem],
+        out_specs=(any_, vmem, vmem) + (any_,) * 7 + (vmem, vmem),
         scratch_shapes=[
+            vm((4, 8, r, c), BF16),
+            vm((8, 16, 128), BF16),
+            vm((total, width), BF16),
+            vm((own, width), BF16),
+            vm((width, own), BF16),
+            vm((total, width), BF16),
+            vm((total, width), BF16),
+            vm((width, total), BF16),
+            vm((width, total), BF16),
+            vm((4, width, width), BF16),
+            vm((total, 128), BF16),
+            vm((2, total, widest), F32),
+            vm((2, 1, widest), F32),
+            vm((2, 1, widest), F32),
+            vm((2, HD, widest), F32),
             dma((2, packs, 4)),
             dma((packs, 4)),
             dma((packs, 4)),
@@ -316,17 +515,19 @@
             dma((packs, 4, 2)),
             dma((packs, 4, 4)),
             dma((packs, 4, 4)),
-            dma((2, 3, chunks)),
-            dma((2, 3, chunks)),
+            dma((2, 2, chunks)),
+            dma((2, 2, chunks)),
             dma((7,)),
             dma((7,)),
-            dma((3,)),
-            pltpu.VMEM((ROWS, width), BF16),
-            dma((SHORT // ROWS,)),
+            dma(()),
+            dma(()),
+            dma((7,)),
         ],
-        compiler_params=pltpu.CompilerParams(collective_id=0, has_side_effects=True),
-        name="gather_all",
-    )(own_w, own_s, own_t)
+        compiler_params=pltpu.CompilerParams(
+            collective_id=0, has_side_effects=True, vmem_limit_bytes=VMEM_MAX
+        ),
+        name="forward_all",
+    )(lengths, deal, own_w, own_s, own_t)
 
 
 def reduce_kernel(
@@ -344,11 +545,6 @@
     chunks = base.shape[0] // ROWS
     total = 4 * chunks
     edge = SHORT // ROWS
-
-    def put(src, dst, send, recv, dp, tp):
-        return pltpu.make_async_remote_copy(
-            src_ref=src, dst_ref=dst, send_sem=send, recv_sem=recv, device_id=(dp, tp), device_id_type=MESH
-        )
 
     def up(ref):
         return ref[...].astype(F32)
@@ -660,51 +856,16 @@
 
 def attention_kernel(qt, k, vt, ka, ma, mixed_t, lse, s, m, l, acc):
     z = lax.axis_index("tp")
-    own, total = qt.shape[1], k.shape[0]
-    pairs = k.shape[1] // 128
-    for part, (row0, r, start) in enumerate(parts_of(z, own)):
-        cols = pl.ds(pl.multiple_of(row0, 128), r)
-        aug = aug_rows(pick_rows((ma[0:1, cols], ma[1:2, cols]), r), r)
+    own = qt.shape[1]
+    for part, (row0, n, start) in enumerate(parts_of(z, own)):
+        cols = pl.ds(pl.multiple_of(row0, 128), n)
+        aug = aug_rows(pick_rows((ma[0:1, cols], ma[1:2, cols]), n), n)
 
         def one_pair(pair, carry):
-            lanes = pl.ds(pl.multiple_of(pair * 128, 128), 128)
-            for half in range(2):
-                m[half, :, :r] = jnp.full((1, r), MASKED, F32)
-                l[half, :, :r] = jnp.zeros((1, r), F32)
-                acc[half, :, :r] = jnp.zeros((HD, r), F32)
-            qs = [
-                padded(qt[pl.ds(pl.multiple_of(pair * 128 + half * HD, HD), HD), cols], half, aug, r)
-                for half in range(2)
-            ]
-
-            def scores(key0):
-                keys = pl.ds(key0, KEYS)
-                left = jnp.concatenate([k[keys, lanes], ka[keys, :]], axis=1)
-                for half in range(2):
-                    score = dot(left, qs[half])
-                    s[half, keys, :r] = score
-                    m[half, :, :r] = jnp.maximum(m[half, :, :r], jnp.max(score, axis=0, keepdims=True))
-
-            over_keys(z, part, start, total, scores)
-            tops = [m[half, :, :r] for half in range(2)]
-
-            def mix(key0):
-                keys = pl.ds(key0, KEYS)
-                for half in range(2):
-                    raised = jnp.exp(s[half, keys, :r] - tops[half])
-                    l[half, :, :r] += jnp.sum(raised, axis=0, keepdims=True)
-                    values = vt[pl.ds(pl.multiple_of(pair * 128 + half * HD, HD), HD), keys]
-                    acc[half, :, :r] += dot(values, raised.astype(BF16))
-
-            over_keys(z, part, start, total, mix)
-            for half in range(2):
-                sums = l[half, :, :r]
-                rows = pl.ds(pl.multiple_of(pair * 128 + half * HD, HD), HD)
-                mixed_t[rows, cols] = acc[half, :, :r] / sums
-                lse[pair, half : half + 1, cols] = tops[half] + jnp.log(sums)
+            attend_pair(z, part, start, pair, cols, n, aug, qt, k, vt, ka, mixed_t, lse, s, m, l, acc)
             return carry
 
-        lax.fori_loop(0, pairs, one_pair, 0)
+        lax.fori_loop(0, k.shape[1] // 128, one_pair, 0)
 
 
 def attention(qt, k, vt, ka, ma):
@@ -819,24 +980,31 @@
 
     own_w = jnp.stack([jnp.concatenate([w_query, w_key, w_value, w_out], axis=1), w_up, w_down])
     vectors = (b_query, b_value, b_out, gain_attn, shift_attn, b_down, gain_ffn, shift_ffn, b_up)
-    own_s = jnp.concatenate(vectors)
-    n_small = own_s.shape[0]
+    n_small = 8 * r + b_up.shape[0]
     if direct:
-        padded_s = jnp.pad(own_s, (0, 2048 - n_small)).reshape(16, 128)
-        w, s, x = gather_all(own_w, padded_s, tokens)
-        s = s.reshape(n_dp, 2048)
+        lines = [jnp.pad(a, (0, 128 - r)) for a in vectors[:8]] + [b_up, jnp.zeros((5 * 128,), BF16)]
+        own_s = jnp.concatenate(lines).reshape(16, 128)
+        w, vec, bu, x, q, qt, k, v, kt, wd, mixed_t, lse = forward_all(lengths, deal_order, own_w, own_s, tokens)
+        w = w.reshape(2, n_tp, width, w_up.shape[1])
+        bu = bu.reshape(-1)
+        wq, wk, wv, wo = (wd[i] for i in range(4))
+        bq, bv, bo, g1, h1, bd, g2, h2 = (vec[i] for i in range(8))
     else:
         w = lax.all_gather(own_w, ("tp", "dp"), axis=0).reshape((n_tp, n_dp) + own_w.shape)
-        w = jnp.moveaxis(w, 2, 0)
-        s = lax.all_gather(own_s, "dp", axis=0)
+        w = jnp.moveaxis(w, 2, 0).reshape(3, n_tp, width, w_up.shape[1])
+        s = lax.all_gather(jnp.concatenate(vectors), "dp", axis=0)
         x = lax.all_gather(tokens, "tp", axis=0, tiled=True)
-    w = w.reshape(3, n_tp, width, w_up.shape[1])
-    small = [s[:, i * r : (i + 1) * r].reshape(width).astype(F32) for i in range(8)]
-    bq, bv, bo, g1, h1, bd, g2, h2 = small
-    bu = s[:, 8 * r : n_small].reshape(-1).astype(F32)
-    wq, wk, wv, wo = (
-        w[0, :, :, i * hw : (i + 1) * hw].transpose(1, 0, 2).reshape(width, width) for i in range(4)
-    )
+        small = [s[:, i * r : (i + 1) * r].reshape(width).astype(F32) for i in range(8)]
+        bq, bv, bo, g1, h1, bd, g2, h2 = small
+        bu = s[:, 8 * r : n_small].reshape(-1).astype(F32)
+        wq, wk, wv, wo = (
+            w[0, :, :, i * hw : (i + 1) * hw].transpose(1, 0, 2).reshape(width, width) for i in range(4)
+        )
+        w = w[1:]
+        q = (dot(tokens, wq) + bq).astype(BF16) * jnp.asarray(HD ** (-0.5), BF16)
+        k = dot(x, wk).astype(BF16)
+        v = (dot(x, wv) + bv).astype(BF16)
+        qt, kt = q.T, k.T
 
     pair = lax.dynamic_slice_in_dim(deal_order, 2 * g, 1)
     first_len = jnp.sum(jnp.where(jnp.arange(lengths.shape[0], dtype=jnp.int32) == pair[0], lengths, 0))
@@ -847,32 +1015,29 @@
     sub = jnp.arange(8, dtype=jnp.int32)[:, None]
     ma = jnp.where(((sub == 0) & row_seg) | ((sub == 1) & ~row_seg), MASKED, 0.0).astype(F32)
 
-    q = (dot(tokens, wq) + bq).astype(BF16) * jnp.asarray(HD ** (-0.5), BF16)
-    k = dot(x, wk).astype(BF16)
-    v = (dot(x, wv) + bv).astype(BF16)
-    qt = q.T
-    mixed_t, lse = attention(qt, k, v.T, ka, ma)
+    if not direct:
+        mixed_t, lse = attention(qt, k, v.T, ka, ma)
     mixed = mixed_t.T.astype(BF16)
     first_residual = tokens.astype(F32) + contract_last(mixed, wo) + bo
     xhat1, inv1 = normalize_layer(first_residual)
     y1 = xhat1 * g1 + h1
     y1r = y1.astype(BF16)
 
-    u = [dot(y1r, w[1, t]) + bu.reshape(n_tp, -1)[t] for t in range(n_tp)]
+    u = [dot(y1r, w[0, t]) + bu.reshape(n_tp, -1)[t] for t in range(n_tp)]
     hr = [jax.nn.gelu(a, approximate=False).astype(BF16) for a in u]
-    ffn = sum(contract_last(hr[t], w[2, t]) for t in range(n_tp))
+    ffn = sum(contract_last(hr[t], w[1, t]) for t in range(n_tp))
     xhat2, inv2 = normalize_layer(y1 + ffn + bd)
     encoder_output = (xhat2 * g2 + h2).astype(BF16)
 
     grad = cotangent.astype(F32)
     dr2 = normalize_backward(grad, xhat2, inv2, g2)
     dfr = dr2.astype(BF16)
-    du = [(dot(dfr, w[2, t]) * gelu_slope(u[t])).astype(BF16) for t in range(n_tp)]
-    dy1 = dr2 + sum(contract_last(du[t], w[1, t]) for t in range(n_tp))
+    du = [(dot(dfr, w[1, t]) * gelu_slope(u[t])).astype(BF16) for t in range(n_tp)]
+    dy1 = dr2 + sum(contract_last(du[t], w[0, t]) for t in range(n_tp))
     dr1 = normalize_backward(dy1, xhat1, inv1, g1)
     dar = dr1.astype(BF16)
     dm = dot(dar, wo).astype(BF16)
-    dqt, dk, dv = attention_back(qt, q, k, k.T, v, ka, ma, mixed_t, lse, dm.T, dm)
+    dqt, dk, dv = attention_back(qt, q, k, kt, v, ka, ma, mixed_t, lse, dm.T, dm)
     dq = dqt.T
     base = dr1 + contract_last(dq, wq)
     far = contract_last(dk, wk) + contract_last(dv, wv)

time: 523 us -> 441 us (0.84)
  local copies, waits for them, and re-layouts: 71 us -> 31.3 us
  matrix products: 121 us -> 94.2 us
  Pallas kernels: 282 us -> 274 us
    dot_general x12 -> x9, matrix products: 57.6 us -> 33.3 us  [dot(): return jnp.dot(left, right, preferred_element_type=F32)]
    convert_element_type x10 -> x0, local copies, waits for them, and re-layouts: 16.7 us -> none  [the longest x1 6.29 us: body(): v = (dot(x, wv) + bv).astype(BF16)]
    pallas_call x2 -> x1, Pallas kernels: 123 us -> 112 us  [forward_all(): pl.pallas_call(forward_kernel, out_shape=(shape((packs - 1, 4, 8, r, c),...]
    slice x6 -> x1, local copies, waits for them, and re-layouts: 8.92 us -> 1.13 us  [body(): bq, bv, bo, g1, h1, bd, g2, h2 = (vec[i] for i in range(8))]
    concatenate x1, local copies, waits for them, and re-layouts: 6.11 us -> 0.2 us  [body(): own_s = jnp.concatenate(lines).reshape(16, 128)]
    unnamed x128 -> x70, local copies, waits for them, and re-layouts: 14.6 us -> 8.72 us
    pad x0 -> x8, local copies, waits for them, and re-layouts: none -> 5.28 us  [body(): jnp.pad(a, (0, 128 - r))]
where the time goes in v2:
time: 441 us; the launch traced here: 434 us
  Pallas kernels  274 us (62%)
  matrix products  94.2 us (21%)
  other arithmetic  33.4 us (8%)
  local copies, waits for them, and re-layouts  31.3 us (7%)
    pallas_call x1, Pallas kernels, reduce_all(): pl.pallas_call(reduce_kernel, out_shape=(jax.ShapeDtypeStruct((packs,) +...  119 us
    pallas_call x1, Pallas kernels, forward_all(): pl.pallas_call(forward_kernel, out_shape=(shape((packs - 1, 4, 8, r, c),...  112 us
    pallas_call x1, Pallas kernels, attention_back(): pl.pallas_call(attention_back_kernel, out_shape=(jax.ShapeDtypeStruct((wi...  43.6 us
    dot_general x9, matrix products, dot(): return jnp.dot(left, right, preferred_element_type=F32)  33.3 us
    dot_general x12, matrix products, contract_last(): lax.dot_general(left, right, (((1,), (1,)), ((), ())), preferred_element_...  31.2 us
    dot_general x12, matrix products, contract_first(): lax.dot_general(left, right, (((0,), (0,)), ((), ())), preferred_element_...  29.7 us
    another operation x1, other arithmetic, body(): grads = jnp.stack([ga, gu, gd]).astype(BF16).reshape(3, n_tp, n_dp, r, -1)  9.39 us

profile of v2, /device:TPU:0, one launch (start us, length us, event | category | flops | bytes accessed | tf_op | source)
XLA Modules:
  0.0 434.3 jit_solution(5696003914943083970)
XLA Ops:
  1.6 1.8 pad_maximum_fusion.4.own_w
  11.8 111.8 %forward_all.1 = (bf16[2,4,8,96,768]{4,3,2,1,0:T(8,128)(2,1)}, f32[8,768]{1,0:T(8,128)}, f32[1,3072]{1,0:T(1,128)}, bf16[2560,768]{1,0:T(8,128)(2,1)}, bf16[640,...) custom-call(s32[16]{0:T(128)} %lengths.1, ...), custom_call_target="tpu_custom_call" | custom-call | tf_op jit(solution)/shard_map/forward_all/pallas_call | solution.py:476
  123.7 1.1 slice_reduce_fusion.1
  124.8 3.4 fusion.109
  129.7 5.2 %fusion.17 = (bf16[640,768]{1,0:T(8,128)(2,1)S(1)}, f32[640,768]{1,0:T(8,128)S(1)}) fusion(f32[768]{0:T(1024)S(1)} %get-tuple-element.133, bf16[640,768]{1,0:T(8,128)(2,1)S(1)} %fusion.71, bf16[2,4,768,768]{3,2,1,0:T(8,128)(2,1)S(1)} %bitcast.161), kind=kOutput, calls=%fused_computation.31 | convolution fusion | flops 787415040 | bytes 5115904 | tf_op jit(solution)/shard_map/dot_general | solution.py:25
  134.9 5.2 %fusion.14 = (bf16[640,768]{1,0:T(8,128)(2,1)S(1)}, f32[640,768]{1,0:T(8,128)S(1)}) fusion(f32[768]{0:T(1024)S(1)} %get-tuple-element.132, bf16[640,768]{1,0:T(8,128)(2,1)S(1)} %fusion.71, bf16[2,4,768,768]{3,2,1,0:T(8,128)(2,1)S(1)} %bitcast.162), kind=kOutput, calls=%fused_computation.28 | convolution fusion | flops 787415040 | bytes 5115904 | tf_op jit(solution)/shard_map/dot_general | solution.py:25
  141.1 5.4 %fusion.8 = (bf16[640,768]{1,0:T(8,128)(2,1)S(1)}, f32[640,768]{1,0:T(8,128)S(1)}) fusion(f32[768]{0:T(1024)S(1)} %get-tuple-element.130, bf16[640,768]{1,0:T(8,128)(2,1)S(1)} %fusion.71, bf16[2,4,768,768]{3,2,1,0:T(8,128)(2,1)S(1)} %bitcast.164), kind=kOutput, calls=%fused_computation.22 | convolution fusion | flops 787415040 | bytes 5115904 | tf_op jit(solution)/shard_map/dot_general | solution.py:25
  147.5 5.2 %fusion.11 = (bf16[640,768]{1,0:T(8,128)(2,1)S(1)}, f32[640,768]{1,0:T(8,128)S(1)}) fusion(f32[768]{0:T(1024)S(1)} %get-tuple-element.131, bf16[640,768]{1,0:T(8,128)(2,1)S(1)} %fusion.71, bf16[2,4,768,768]{3,2,1,0:T(8,128)(2,1)S(1)} %bitcast.166), kind=kOutput, calls=%fused_computation.25 | convolution fusion | flops 787415040 | bytes 5115904 | tf_op jit(solution)/shard_map/dot_general | solution.py:25
  153.7 1.6 fusion.110
  156.5 1.5 fusion.18
  158.0 2.3 convert_reduce_fusion.6
  160.3 2.2 convolution_convert_fusion.3
  162.5 2.1 convolution_convert_fusion.4
  164.6 2.1 convolution_convert_fusion.5
  166.8 2.2 convolution_convert_fusion.6
  169.0 2.8 convert_reduce_fusion.2
  171.8 2.1 convolution_convert_fusion.7
  173.9 2.4 convert_reduce_fusion.3
  176.4 2.2 convolution_convert_fusion.8
  178.5 2.4 convert_reduce_fusion.4
  181.0 2.2 convolution_convert_fusion.9
  183.2 2.4 convert_reduce_fusion.5
  185.6 2.2 convolution_convert_fusion.10
  190.6 2.8 multiply_reduce_fusion
  193.4 1.2 convert_reduce_fusion.7
  195.0 1.1 convolution_convert_fusion.2
  196.1 1.0 fusion.106
  197.7 1.3 fusion.97
  199.7 2.7 select_convert_fusion.ka
  203.7 2.2 convolution_convert_fusion.12.dm
  206.9 1.3 copy.36.dmt
  208.2 43.6 %attention_back.1 = (bf16[768,640]{1,0:T(8,128)(2,1)}, bf16[2560,768]{1,0:T(8,128)(2,1)}, bf16[2560,768]{1,0:T(8,128)(2,1)}) custom-call(bf16[768,640]{1,0:T(8,128)(2,1)} %get-tuple-element.40.qt, bf16[640,768]{1,0:T(8,128)(2,1)} %get-tuple-element.41.q, bf16[2560,768]{1,0:T(8,128)(2,1)} %get-tuple-element.42.k, bf16[768,2560]{1,0:T(8,128)(2,1)} %get-tuple-element.43.kt, ...), custom_call_target="tpu_custom_call" | custom-call | tf_op jit(solution)/shard_map/attention_back/pallas_call | solution.py:951
  251.8 6.7 %convolution_convert_fusion = bf16[768,768]{0,1:T(8,128)(2,1)S(1)} fusion(bf16[2560,768]{1,0:T(8,128)(2,1)} %get-tuple-element.47, bf16[2560,768]{1,0:T(8,128)(2,1)} %get-tuple-element.49), kind=kOutput, calls=%fused_computation.139 | convolution fusion | flops 3020488704 | bytes 9043968 | tf_op jit(solution)/shard_map/dot_general | solution.py:33
  259.5 3.4 convolution_convert_fusion.1
  264.8 1.1 fusion.72
  267.7 1.3 pad_maximum_fusion.2
  269.6 2.4 pad_maximum_fusion.1
  272.0 1.6 copy.38
  273.6 2.3 pad_maximum_fusion
  275.9 2.4 copy.37
  278.3 9.4 %maximum_maximum_fusion.g = bf16[3,4,4,2,96,768]{5,4,3,2,1,0:T(8,128)(2,1)} fusion(bf16[1,1,4,2,96,768]{5,4,3,2,1,0:T(8,128)(2,1)} %bitcast.153, bf16[1,1,4,2,96,768]{5,4,3,2,1,0:T(8,128)(2,1)} %bitcast.154, bf16[1,1,4,2,96,768]{5,4,3,2,1,0:T(8,128)(2,1)} %bitcast.155, bf16[1,1,4,2,96,768]{5,4,3,2,1,0:T(8,128)(2,1)} %bitcast.156, ...), kind=kLoop, calls=%fused_computation | loop fusion | flops 77856768 | bytes 28311552 | tf_op jit(solution)/shard_map/stack | solution.py:1070
  288.1 2.7 convert_reduce_fusion
  292.2 6.0 %fusion.75 = f32[2560,768]{1,0:T(8,128)S(1)} fusion(bf16[2560,768]{1,0:T(8,128)(2,1)} %get-tuple-element.48, bf16[4,768,768]{2,1,0:T(8,128)(2,1)} %get-tuple-element.36), kind=kOutput, calls=%fused_computation.168 | convolution fusion | flops 3019898880 | bytes 12976128 | tf_op jit(solution)/shard_map/dot_general | solution.py:29
  298.2 7.6 %fusion.111 = (bf16[2560,768]{1,0:T(8,128)(2,1)}, f32[2560,768]{1,0:T(8,128)}) fusion(f32[2560,768]{1,0:T(8,128)S(1)} %fusion.75, bf16[2560,768]{1,0:T(8,128)(2,1)S(1)} %copy-done, bf16[4,768,768]{2,1,0:T(8,128)(2,1)} %get-tuple-element.36), kind=kOutput, calls=%fused_computation.238 | convolution fusion | flops 3023831040 | bytes 24772608 | tf_op jit(solution)/shard_map/dot_general | solution.py:29
  305.8 4.2 dynamic-slice_add_fusion.base
  310.0 118.6 %reduce_all.1 = (f32[3,96,768]{2,1,0:T(8,128)}, f32[16,128]{1,0:T(8,128)}, f32[640,768]{1,0:T(8,128)}) custom-call(bf16[3,4,4,2,96,768]{5,4,3,2,1,0:T(8,128)(2,1)} %maximum_maximum_fusion.g, f32[4,2,16,128]{3,2,1,0:T(8,128)} %bitcast.177, bf16[20,128,768]{2,1,0:T(8,128)(2,1)} %bitcast.147, f32[640,768]{1,0:T(8,128)} %dynamic-slice_add_fusion.base), custom_call_target="tpu_custom_call" | custom-call | tf_op jit(solution)/shard_map/reduce_all/pallas_call | solution.py:757
  428.6 2.1 slice_bitcast_fusion.24
  432.8 1.3 copy.53
  (129 shorter events, 30.5 us)
Async XLA Ops:
  11.2 0.6 copy-start.20
  124.8 4.9 %copy-start.12 = (bf16[2,4,8,96,768]{4,3,2,1,0:T(8,128)(2,1)S(1)}, bf16[2,4,8,96,768]{4,3,2,1,0:T(8,128)(2,1)}, u32[]{:S(2)}) copy-start(bf16[2,4,8,96,768]{4,3,2,1,0:T(8,128)(2,1)} %get-tuple-element.38) | copy-start | bytes 28311556
  155.3 1.2 copy-start.3
  193.4 1.5 copy-start.4
  194.6 9.1 %copy-start.1 = (f32[640,768]{1,0:T(8,128)}, f32[640,768]{1,0:T(8,128)S(1)}, u32[]{:S(2)}) copy-start(f32[640,768]{1,0:T(8,128)S(1)} %get-tuple-element.74) | copy-start | bytes 5898244
  196.1 1.1 copy-start.25
  196.1 1.6 copy-start.26
  206.0 0.9 copy-start.5
  251.8 7.7 %copy-start.27 = (bf16[2560,768]{1,0:T(8,128)(2,1)S(1)}, bf16[2560,768]{1,0:T(8,128)(2,1)}, u32[]{:S(2)}) copy-start(bf16[2560,768]{1,0:T(8,128)(2,1)} %get-tuple-element.47) | copy-start | bytes 11796484
  251.8 7.7 %copy-start.28 = (bf16[2560,768]{1,0:T(8,128)(2,1)S(1)}, bf16[2560,768]{1,0:T(8,128)(2,1)}, u32[]{:S(2)}) copy-start(bf16[2560,768]{1,0:T(8,128)(2,1)} %get-tuple-element.48) | copy-start | bytes 11796484
  263.0 1.5 copy-start.6
  263.0 1.8 copy-start.11
  265.9 1.1 copy-start.10
  278.3 9.4 %copy-start.7 = (bf16[768,640]{1,0:T(8,128)(2,1)S(1)}, bf16[768,640]{1,0:T(8,128)(2,1)}, u32[]{:S(2)}) copy-start(bf16[768,640]{1,0:T(8,128)(2,1)} %get-tuple-element.46) | copy-start | bytes 2949124
  288.0 2.9 copy-start.18
  288.0 3.0 copy-start.16
  288.0 3.0 copy-start.15
  288.0 3.1 copy-start.17
  288.0 3.2 copy-start.14
  288.0 3.2 copy-start.13
  288.0 3.3 copy-start.21
  288.1 3.3 copy-start.22
  288.1 3.3 copy-start.23
  288.1 3.3 copy-start.24
  292.2 6.0 %copy-start = (bf16[2560,768]{1,0:T(8,128)(2,1)S(1)}, bf16[2560,768]{1,0:T(8,128)(2,1)}, u32[]{:S(2)}) copy-start(bf16[2560,768]{1,0:T(8,128)(2,1)} %get-tuple-element.49) | copy-start | bytes 11796484
  298.2 7.7 %copy-start.2 = (f32[640,768]{1,0:T(8,128)S(1)}, f32[640,768]{1,0:T(8,128)}, u32[]{:S(2)}) copy-start(f32[640,768]{1,0:T(8,128)} %copy-done.1) | copy-start | bytes 5898244
  298.2 7.6 %copy-start.8 = (bf16[768,640]{1,0:T(8,128)(2,1)S(1)}, bf16[768,640]{1,0:T(8,128)(2,1)}, u32[]{:S(2)}) copy-start(bf16[768,640]{1,0:T(8,128)(2,1)} %get-tuple-element.46) | copy-start | bytes 2949124
  428.6 3.0 copy-start.19
  428.6 4.1 copy-start.9

commit v3 on v2

--- a/solution.py
+++ b/solution.py
@@ -530,177 +530,316 @@
     )(lengths, deal, own_w, own_s, own_t)
 
 
-def reduce_kernel(
-    g, sv, dt, base, out_w, out_s, out_t,
-    gk, r1, b2, r2, b3, r3, s3, b4, r4, ds, dr, sk, q1, q2, q3, c2, c3, q4,
-    gk_sem, p1_s, p1_r, p2_s, p2_r, p3_s, p3_r, p4_s, p4_r, t_l, t_s, t_r, v_s, v_r,
+def up(ref):
+    return ref[...].astype(F32)
+
+
+class Sums:
+    def __init__(self, z, d, core, e_mask, f_mask, give, mine, ready, bufs, sems):
+        self.z, self.d, self.give, self.mine, self.ready = z, d, give, mine, ready
+        self.r1, self.b2, self.r2, self.b3, self.r3, self.s3, self.b4, self.r4 = bufs
+        self.sems = sems
+        self.xy = d // 2
+        self.e, self.f = xor(d, e_mask) // 2, xor(d, f_mask) // 2
+        self.ef = xor(xor(d, e_mask), f_mask) // 2
+        self.d_e, self.d_f, self.pal = xor(d, e_mask), xor(d, f_mask), xor(d, 1)
+
+    def one(self, p, t):
+        return put(self.give(p, t), self.r1.at[p, t], self.sems[0].at[p, t], self.sems[1].at[p, t], self.pal, self.z)
+
+    def two(self, p, t):
+        return put(self.b2.at[p, t], self.r2.at[p, t], self.sems[2].at[p, t], self.sems[3].at[p, t], self.d_e, self.z)
+
+    def three(self, p, t):
+        return put(self.b3.at[p, t], self.r3.at[p, t], self.sems[4].at[p, t], self.sems[5].at[p, t], self.d_f, self.z)
+
+    def four(self, p, t, way):
+        to = jnp.minimum(self.z + 1, 3) if way == 0 else jnp.maximum(self.z - 1, 0)
+        return put(
+            self.b4.at[p, way, t], self.r4.at[p, way, t],
+            self.sems[6].at[p, way, t], self.sems[7].at[p, way, t], self.d, to,
+        )
+
+    def at_two(self, p, t):
+        self.ready(p, t)
+        self.one(p, t).wait_recv()
+        for i, x in enumerate((self.e, self.ef)):
+            self.b2[p, t, i] = (self.mine(p, t, x) + up(self.r1.at[p, t, x])).astype(BF16)
+        self.two(p, t).start()
+
+    def at_three(self, p, t):
+        self.two(p, t).wait_recv()
+        f = self.f
+        self.b3[p, t] = (self.mine(p, t, f) + up(self.r1.at[p, t, f]) + up(self.r2.at[p, t, 1])).astype(BF16)
+        self.three(p, t).start()
+
+    def at_kept(self, p, t):
+        self.three(p, t).wait_recv()
+        xy = self.xy
+        self.s3[p, t] = self.mine(p, t, xy) + up(self.r1.at[p, t, xy]) + up(self.r2.at[p, t, 0]) + up(self.r3.at[p, t])
+
+    def at_four(self, p, t, step):
+        for way in range(2):
+            pos = step if way == 0 else 3 - step
+            if not (t > pos if way == 0 else t < pos):
+                continue
+
+            @pl.when(self.z == pos)
+            def _():
+                if step == 0:
+                    self.b4[p, way, t] = self.s3[p, t].astype(BF16)
+                else:
+                    self.four(p, t, way).wait_recv()
+                    self.b4[p, way, t] = (self.s3[p, t] + up(self.r4.at[p, way, t])).astype(BF16)
+                self.four(p, t, way).start()
+
+    def result(self, p, out):
+        z = self.z
+        out[...] = self.s3[p, z]
+
+        @pl.when(z > 0)
+        def _():
+            self.four(p, z, 0).wait_recv()
+            out[...] += up(self.r4.at[p, 0, z])
+
+        @pl.when(z < 3)
+        def _():
+            self.four(p, z, 1).wait_recv()
+            out[...] += up(self.r4.at[p, 1, z])
+
+    def drain(self, p):
+        for t in range(4):
+            self.one(p, t).wait_send()
+            self.two(p, t).wait_send()
+            self.three(p, t).wait_send()
+            for way in range(2):
+
+                @pl.when((t > self.z) if way == 0 else (t < self.z))
+                def _():
+                    self.four(p, t, way).wait_send()
+
+
+def sum_buffers(packs, block):
+    vm = pltpu.VMEM
+    return [
+        vm((packs, 4, 4) + block, BF16),
+        vm((packs, 4, 2) + block, BF16),
+        vm((packs, 4, 2) + block, BF16),
+        vm((packs, 4) + block, BF16),
+        vm((packs, 4) + block, BF16),
+        vm((packs, 4) + block, F32),
+        vm((packs, 2, 4) + block, BF16),
+        vm((packs, 2, 4) + block, BF16),
+    ]
+
+
+def sum_semaphores(packs):
+    dma = pltpu.SemaphoreType.DMA
+    return [dma((packs, 4))] * 6 + [dma((packs, 2, 4))] * 2
+
+
+def finish_kernel(
+    dqt, dk, dv, x, dar, mixed_t, wd, dr1, vecs, bup,
+    out_w, out_s, out_t,
+    xt, dart, dq, mixed, gp, sv, ds, dr, sk, q1, q2, q3, c2, c3, q4,
+    r1, b2, r2, b3, r3, s3, b4, r4,
+    p1_s, p1_r, p2_s, p2_r, p3_s, p3_r, p4_s, p4_r, t_s, t_r, v_s, v_r,
 ):
     z, d, core, first, second = position()
-    e_mask, f_mask = second, first
-    packs = g.shape[0]
-    xy = d // 2
-    e, f = xor(d, e_mask) // 2, xor(d, f_mask) // 2
-    ef = xor(xor(d, e_mask), f_mask) // 2
-    d_e, d_f, pal = xor(d, e_mask), xor(d, f_mask), xor(d, 1)
-    chunks = base.shape[0] // ROWS
+    own, width = out_t.shape
+    chunks = own // ROWS
     total = 4 * chunks
     edge = SHORT // ROWS
-
-    def up(ref):
-        return ref[...].astype(F32)
-
+    hw = width // 4
+    r = width // 8
     greet(z, d)
-    fetch = [
-        [pltpu.make_async_copy(g.at[p, t, :, core], gk.at[p, t], gk_sem.at[p, t]) for t in range(4)]
-        for p in range(packs)
-    ]
-    one = [
-        [put(g.at[p, t, :, 1 - core], r1.at[p, t], p1_s.at[p, t], p1_r.at[p, t], pal, z) for t in range(4)]
-        for p in range(packs)
-    ]
-    two = [
-        [put(b2.at[p, t], r2.at[p, t], p2_s.at[p, t], p2_r.at[p, t], d_e, z) for t in range(4)]
-        for p in range(packs)
-    ]
-    three = [
-        [put(b3.at[p, t], r3.at[p, t], p3_s.at[p, t], p3_r.at[p, t], d_f, z) for t in range(4)]
-        for p in range(packs)
-    ]
-
-    def four(p, t, way):
+
+    def token(k, way):
         to = jnp.minimum(z + 1, 3) if way == 0 else jnp.maximum(z - 1, 0)
-        return put(b4.at[p, way, t], r4.at[p, way, t], p4_s.at[p, way, t], p4_r.at[p, way, t], d, to)
-
-    load = pltpu.make_async_copy(dt, ds, t_l)
-    load.start()
-    for p in range(packs):
-        for t in range(4):
-            one[p][t].start()
-            fetch[p][t].start()
-
+        slot = k if way == 0 else jnp.where(k // chunks == to, total + k % chunks, k)
+        return put(ds.at[k], dr.at[slot], t_s.at[k], t_r.at[slot], d, to)
+
+    def token_in(k, way):
+        slot = k if way == 0 else jnp.where(k // chunks == z, total + k % chunks, k)
+        return put(ds.at[k], dr.at[slot], t_s.at[k], t_r.at[slot], d, z), slot
+
+    def sends(k, way):
+        o = k // chunks
+        if way == 0:
+            low = jnp.where(k < total - edge, 0, 1)
+            return (z >= low) & (z < o) & (o > low)
+        high = jnp.where(k >= edge, 3, 2)
+        return (z <= high) & (z > o) & (o < high)
+
+    def starts(k, way):
+        if way == 0:
+            return z == jnp.where(k < total - edge, 0, 1)
+        return z == jnp.where(k >= edge, 3, 2)
+
+    def pick(a, b, c, e):
+        return jnp.where(z == 0, a, jnp.where(z == 1, b, jnp.where(z == 2, c, e)))
+
+    tile = 256
+
+    def far_shard(o, mine):
+        rows = pl.ds(pl.multiple_of(o * own, ROWS), own)
+
+        def one_tile(n, carry):
+            lanes = pl.ds(pl.multiple_of(n * tile, tile), tile)
+            far = contract_last(dk[rows, :], wd[1, lanes, :]) + contract_last(dv[rows, :], wd[2, lanes, :])
+            if mine:
+                out_t[:, lanes] = dr1[:, lanes] + far
+            else:
+                ds[pl.ds(o * chunks, chunks), :, lanes] = far.reshape(chunks, ROWS, tile).astype(BF16)
+            return carry
+
+        lax.fori_loop(0, width // tile, one_tile, 0)
+
+    def far_and_send(j, carry):
+        o = jnp.where(j == 0, pick(2, 3, 0, 1), jnp.where(j == 1, pick(1, 2, 1, 2), pick(3, 0, 3, 0)))
+
+        @pl.when((j < 2) | (z == 1) | (z == 2))
+        def _():
+            far_shard(o, False)
+
+        for i in range(chunks):
+            for way in range(2):
+                k = o * chunks + i
+
+                @pl.when(sends(k, way) & starts(k, way))
+                def _():
+                    token(k, way).start()
+
+        return carry
+
+    lax.fori_loop(0, 3, far_and_send, 0)
+
+    right_order = [k for o in (3, 2, 1) for k in range(o * chunks, (o + 1) * chunks)]
+    left_order = [total - 1 - k for k in right_order]
+
+    def forward_tokens(at):
+        for k, way in [(k, 0) for k in right_order] + [(k, 1) for k in left_order]:
+            pos = at if way == 0 else 3 - at
+            passes = (at < k // chunks) if way == 0 else (3 - at > k // chunks)
+            begins = (0 if k < total - edge else 1) if way == 0 else (3 if k >= edge else 2)
+            if not passes or (begins >= pos if way == 0 else begins <= pos):
+                continue
+
+            @pl.when(z == pos)
+            def _():
+                got, slot = token_in(k, way)
+                got.wait_recv()
+                ds[k] = (ds[k].astype(F32) + dr[slot].astype(F32)).astype(BF16)
+                token(k, way).start()
+
+    def flip(i, carry):
+        cols = pl.ds(pl.multiple_of(i * ROWS, ROWS), ROWS)
+        xt[:, cols] = x[cols, :].T
+        return carry
+
+    lax.fori_loop(0, total, flip, 0)
+
+    def flip_own(i, carry):
+        cols = pl.ds(pl.multiple_of(i * ROWS, ROWS), ROWS)
+        dart[:, cols] = dar[cols, :].T
+        dq[cols, :] = dqt[:, cols].T
+        mixed[cols, :] = mixed_t[:, cols].T.astype(BF16)
+        return carry
+
+    lax.fori_loop(0, chunks, flip_own, 0)
+
+    def give(p, t):
+        return gp.at[t, :, 1 - core]
+
+    def mine(p, t, at):
+        return gp[t, at, core].astype(F32)
+
+    sums = Sums(
+        z, d, core, second, first, give, mine, lambda p, t: None,
+        (r1, b2, r2, b3, r3, s3, b4, r4), (p1_s, p1_r, p2_s, p2_r, p3_s, p3_r, p4_s, p4_r),
+    )
+    here = pl.ds(pl.multiple_of(z * own, ROWS), own)
+    half = width // 2
+
+    def weights(th):
+        lanes = pl.ds(th * half, half)
+
+        def rows_of(m, carry):
+            rows = pl.ds(pl.multiple_of(m * half, ROWS), half)
+            parts = (
+                lambda: dot(xt[rows, here], dq[:, lanes]),
+                lambda: dot(xt[rows, :], dk[:, lanes]),
+                lambda: dot(xt[rows, :], dv[:, lanes]),
+                lambda: dot(dart[rows, :], mixed[:, lanes]),
+            )
+            for i, part in enumerate(parts):
+                got = part().astype(BF16)
+                for h in range(2):
+                    block = got[:, h * hw : (h + 1) * hw].reshape(2, 2, r, hw)
+                    gp[2 * th + h, pl.ds(2 * m, 2), :, :, i * hw : (i + 1) * hw] = block
+            return carry
+
+        lax.fori_loop(0, 2, rows_of, 0)
+        for t in (2 * th, 2 * th + 1):
+            sums.one(0, t).start()
+
+    weights(0)
+    forward_tokens(1)
+    weights(1)
+
+    ones = jnp.ones((8, 4 * own), BF16)
+    index = lax.broadcasted_iota(jnp.int32, (8, width), 0)
+    small_rows = jnp.where(index == 0, dot(ones[:, :own], dq[...]), jnp.where(index == 1, dot(ones, dv[...]), vecs[...]))
+    pad = jnp.zeros((8, 128 - r), F32)
+    for i in range(8):
+        sv[i // 2, i % 2, 0:8, :] = jnp.concatenate([small_rows[:, i * r : (i + 1) * r], pad], axis=1)
+        wide = [bup[:, (i * 3 + j) * 128 : (i * 3 + j + 1) * 128] for j in range(3)]
+        sv[i // 2, i % 2, 8:16, :] = jnp.concatenate(wide + [jnp.zeros((5, 128), F32)], axis=0)
     small = [
-        put(sv.at[:, 1 - core], q1, v_s.at[0], v_r.at[0], pal, z),
-        put(c2, q2, v_s.at[1], v_r.at[1], d_e, z),
-        put(c3, q3, v_s.at[2], v_r.at[2], d_f, z),
+        put(sv.at[:, 1 - core], q1, v_s.at[0], v_r.at[0], sums.pal, z),
+        put(c2, q2, v_s.at[1], v_r.at[1], sums.d_e, z),
+        put(c3, q3, v_s.at[2], v_r.at[2], sums.d_f, z),
     ]
     small_z = [
         put(sk, q4.at[j - 1], v_s.at[2 + j], v_r.at[2 + j], d, lax.rem(z + j, 4)) for j in range(1, 4)
     ]
     small[0].start()
-
-    def token(k, way):
-        to = jnp.minimum(z + 1, 3) if way == 0 else jnp.maximum(z - 1, 0)
-        slot = k if way == 0 else jnp.where(k // chunks == to, total + k % chunks, k)
-        return put(ds.at[k], dr.at[slot], t_s.at[k], t_r.at[slot], d, to)
-
-    def token_in(k, way):
-        slot = k if way == 0 else jnp.where(k // chunks == z, total + k % chunks, k)
-        return put(ds.at[k], dr.at[slot], t_s.at[k], t_r.at[slot], d, z), slot
-
-    def sends(k, way):
-        o = k // chunks
-        if way == 0:
-            low = 0 if k < total - edge else 1
-            return (z >= low) & (z < o) & (o > low)
-        high = 3 if k >= edge else 2
-        return (z <= high) & (z > o) & (o < high)
-
-    def starts(k, way):
-        if way == 0:
-            return z == (0 if k < total - edge else 1)
-        return z == (3 if k >= edge else 2)
-
-    right_order = [k for o in (3, 2, 1) for k in range(o * chunks, (o + 1) * chunks)]
-    left_order = [total - 1 - k for k in right_order]
-    load.wait()
-    for kr, kl in zip(right_order, left_order):
-        for k, way in ((kr, 0), (kl, 1)):
-
-            @pl.when(sends(k, way) & starts(k, way))
-            def _():
-                token(k, way).start()
-
-    def forward_tokens(at):
-        for k, way in [(k, 0) for k in right_order] + [(k, 1) for k in left_order]:
-            pos = at if way == 0 else 3 - at
-
-            @pl.when(sends(k, way) & jnp.logical_not(starts(k, way)) & (z == pos))
-            def _():
-                got, slot = token_in(k, way)
-                got.wait_recv()
-                ds[k] = (ds[k].astype(F32) + dr[slot].astype(F32)).astype(BF16)
-                token(k, way).start()
-
-    def stage_two(p):
+    for t in range(4):
+        sums.at_two(0, t)
+    forward_tokens(2)
+
+    far_shard(z, True)
+
+    def query_tile(n, carry):
+        lanes = pl.ds(pl.multiple_of(n * tile, tile), tile)
+        out_t[:, lanes] += contract_last(dq[...], wd[0, lanes, :])
+        return carry
+
+    lax.fori_loop(0, width // tile, query_tile, 0)
+    small[0].wait_recv()
+    for i, at in enumerate((sums.e, sums.ef)):
+        c2[i] = sv[at, core] + q1[at]
+    small[1].start()
+    for t in range(4):
+        sums.at_three(0, t)
+    small[1].wait_recv()
+    c3[...] = sv[sums.f, core] + q1[sums.f] + q2[1]
+    small[2].start()
+    for t in range(4):
+        sums.at_kept(0, t)
+    for step in range(3):
         for t in range(4):
-            fetch[p][t].wait()
-            one[p][t].wait_recv()
-            for i, x in enumerate((e, ef)):
-                b2[p, t, i] = (up(gk.at[p, t, x]) + up(r1.at[p, t, x])).astype(BF16)
-            two[p][t].start()
-
-    def stage_three(p):
-        for t in range(4):
-            two[p][t].wait_recv()
-            b3[p, t] = (up(gk.at[p, t, f]) + up(r1.at[p, t, f]) + up(r2.at[p, t, 1])).astype(BF16)
-            three[p][t].start()
-
-    def stage_kept(p):
-        for t in range(4):
-            three[p][t].wait_recv()
-            s3[p, t] = up(gk.at[p, t, xy]) + up(r1.at[p, t, xy]) + up(r2.at[p, t, 0]) + up(r3.at[p, t])
-
-    def stage_four(p, t, way):
-        goes = (t > z) if way == 0 else (t < z)
-        inner = z > 0 if way == 0 else z < 3
-
-        @pl.when(goes & inner)
-        def _():
-            four(p, t, way).wait_recv()
-            b4[p, way, t] = (s3[p, t] + up(r4.at[p, way, t])).astype(BF16)
-
-        @pl.when(goes & jnp.logical_not(inner))
-        def _():
-            b4[p, way, t] = s3[p, t].astype(BF16)
-
-        @pl.when(goes)
-        def _():
-            four(p, t, way).start()
-
-    for p in range(packs):
-        stage_two(p)
-        if p == 0:
-            small[0].wait_recv()
-            for i, x in enumerate((e, ef)):
-                c2[i] = sv[x, core] + q1[x]
-            small[1].start()
-    forward_tokens(1)
-    for p in range(packs):
-        stage_three(p)
-        if p == 0:
-            small[1].wait_recv()
-            c3[...] = sv[f, core] + q1[f] + q2[1]
-            small[2].start()
-    forward_tokens(2)
-    small[2].wait_recv()
-    sk[...] = sv[xy, core] + q1[xy] + q2[0] + q3[...]
-    for copy in small_z:
-        copy.start()
-    for p in range(packs):
-        stage_kept(p)
-        for i in range(3):
-            stage_four(p, 3 - i, 0)
-            stage_four(p, i, 1)
-    for copy in small_z:
-        copy.wait_recv()
-    out_s[...] = sk[...] + q4[0] + q4[1] + q4[2]
+            sums.at_four(0, t, step)
+        if step == 0:
+            small[2].wait_recv()
+            sk[...] = sv[sums.xy, core] + q1[sums.xy] + q2[0] + q3[...]
+            for copy in small_z:
+                copy.start()
     for i in range(chunks):
         k = z * chunks + i
         rows = pl.ds(i * ROWS, ROWS)
-        out_t[rows, :] = base[rows, :]
-        from_left = (z > 0) & ((z > 1) | (k < total - edge))
-        from_left = from_left & ((z != 1) | (k < total - edge))
-        from_right = (z < 3) & ((z < 2) | (k >= edge))
+        from_left = (z > 0) & ((z == 1) & (k < total - edge) | (z > 1))
+        from_right = (z < 3) & ((z == 2) & (k >= edge) | (z < 2))
 
         @pl.when(from_left)
         def _():
@@ -712,67 +851,45 @@
             put(ds.at[k], dr.at[total + i], t_s.at[k], t_r.at[total + i], d, z).wait_recv()
             out_t[rows, :] += dr[total + i].astype(F32)
 
-    for p in range(packs):
-        out_w[p] = s3[p, z]
-
-        @pl.when(z > 0)
-        def _():
-            four(p, z, 0).wait_recv()
-            out_w[p] += up(r4.at[p, 0, z])
-
-        @pl.when(z < 3)
-        def _():
-            four(p, z, 1).wait_recv()
-            out_w[p] += up(r4.at[p, 1, z])
-
+    for copy in small_z:
+        copy.wait_recv()
+    out_s[...] = sk[...] + q4[0] + q4[1] + q4[2]
+    sums.result(0, out_w)
     for copy in small + small_z:
         copy.wait_send()
-    for p in range(packs):
-        for t in range(4):
-            one[p][t].wait_send()
-            two[p][t].wait_send()
-            three[p][t].wait_send()
-            for way in range(2):
-
-                @pl.when((t > z) if way == 0 else (t < z))
-                def _():
-                    four(p, t, way).wait_send()
-
-    for k, way in [(k, 0) for k in right_order] + [(k, 1) for k in left_order]:
-
-        @pl.when(sends(k, way))
-        def _():
-            token(k, way).wait_send()
-
-
-def reduce_all(g, sv, dt, base):
-    packs, _, _, r, c = g.shape
-    rows, width = base.shape
-    chunks = rows // ROWS
-    dma = pltpu.SemaphoreType.DMA
-    any_ = pl.BlockSpec(memory_space=pl.ANY)
+    sums.drain(0)
+    for k in range(total):
+        for way in range(2):
+
+            @pl.when(sends(k, way))
+            def _():
+                token(k, way).wait_send()
+
+
+def finish(dqt, dk, dv, x, dar, mixed_t, wd, dr1, vecs, bup):
+    own, width = dr1.shape
+    r = width // 8
+    chunks = own // ROWS
+    total = 4 * own
+    dma, vm = pltpu.SemaphoreType.DMA, pltpu.VMEM
     vmem = pl.BlockSpec(memory_space=pltpu.VMEM)
-    vm = pltpu.VMEM
-    block, sb = (r, c), sv.shape[1:]
+    block, sb = (r, width), (16, 128)
     return pl.pallas_call(
-        reduce_kernel,
+        finish_kernel,
         out_shape=(
-            jax.ShapeDtypeStruct((packs,) + block, F32),
+            jax.ShapeDtypeStruct(block, F32),
             jax.ShapeDtypeStruct(sb, F32),
-            jax.ShapeDtypeStruct((rows, width), F32),
+            jax.ShapeDtypeStruct((own, width), F32),
         ),
-        in_specs=[any_, vmem, any_, vmem],
+        in_specs=[vmem] * 10,
         out_specs=(vmem, vmem, vmem),
         scratch_shapes=[
-            vm((packs, 4, 4) + block, BF16),
-            vm((packs, 4, 4) + block, BF16),
-            vm((packs, 4, 2) + block, BF16),
-            vm((packs, 4, 2) + block, BF16),
-            vm((packs, 4) + block, BF16),
-            vm((packs, 4) + block, BF16),
-            vm((packs, 4) + block, F32),
-            vm((packs, 2, 4) + block, BF16),
-            vm((packs, 2, 4) + block, BF16),
+            vm((width, total), BF16),
+            vm((width, own), BF16),
+            vm((own, width), BF16),
+            vm((own, width), BF16),
+            vm((4, 4, 2) + block, BF16),
+            vm((4, 2) + sb, F32),
             vm((4 * chunks, ROWS, width), BF16),
             vm((5 * chunks, ROWS, width), BF16),
             vm(sb, F32),
@@ -782,16 +899,8 @@
             vm((2,) + sb, F32),
             vm(sb, F32),
             vm((3,) + sb, F32),
-            dma((packs, 4)),
-            dma((packs, 4)),
-            dma((packs, 4)),
-            dma((packs, 4)),
-            dma((packs, 4)),
-            dma((packs, 4)),
-            dma((packs, 4)),
-            dma((packs, 2, 4)),
-            dma((packs, 2, 4)),
-            dma(()),
+            *sum_buffers(1, block),
+            *sum_semaphores(1),
             dma((4 * chunks,)),
             dma((5 * chunks,)),
             dma((6,)),
@@ -800,13 +909,8 @@
         compiler_params=pltpu.CompilerParams(
             collective_id=1, has_side_effects=True, vmem_limit_bytes=VMEM_MAX
         ),
-        name="reduce_all",
-    )(
-        g.reshape(packs, 4, 4, 2, r, c),
-        sv.reshape((4, 2) + sb),
-        dt.reshape(4 * chunks, ROWS, width),
-        base,
-    )
+        name="finish",
+    )(dqt, dk, dv, x, dar, mixed_t, wd, dr1, vecs, bup)
 
 
 def parts_of(z, own):
@@ -892,79 +996,183 @@
     )(qt, k, vt, ka, ma)
 
 
-def attention_back_kernel(qt, q, k, kt, v, ka, ma, mixed_t, lse, dmt, dm, dqt, dk, dv, dka, dva, dqa):
+def back_pair(z, pair, pause, qt, q, k, kt, v, ka, ma, mixed_t, lse, dmt, dm, dqt, dk, dv, dka, dva, dqa):
+    own, total = qt.shape[1], k.shape[0]
+    lanes = pl.ds(pl.multiple_of(pair * 128, 128), 128)
+    dka[...] = jnp.zeros_like(dka)
+    dva[...] = jnp.zeros_like(dva)
+    for part, (row0, r, start) in enumerate(parts_of(z, own)):
+        pause(part)
+        cols = pl.ds(pl.multiple_of(row0, 128), r)
+        qs, gs, qm, gm = [], [], [], []
+        low = lax.broadcasted_iota(jnp.int32, (r, 128), 1) < HD
+        for half in range(2):
+            rows = pl.ds(pl.multiple_of(pair * 128 + half * HD, HD), HD)
+            delta = jnp.sum(dmt[rows, cols].astype(F32) * mixed_t[rows, cols], axis=0, keepdims=True)
+            total_log = lse[pair, half : half + 1, cols]
+            q_aug = pick_rows((ma[0:1, cols], ma[1:2, cols]) + split3(-total_log), r)
+            zero = jnp.zeros((1, r), F32)
+            g_aug = pick_rows((zero, zero) + split3(-delta), r)
+            qs.append(padded(qt[rows, cols], half, aug_rows(q_aug, r), r))
+            gs.append(padded(dmt[rows, cols], half, aug_rows(g_aug, r), r))
+            mine = low if half == 0 else jnp.logical_not(low)
+            here = pl.ds(pl.multiple_of(row0, 128), r)
+            qm.append(jnp.where(mine, q[here, lanes], jnp.zeros((), BF16)))
+            gm.append(jnp.where(mine, dm[here, lanes], jnp.zeros((), BF16)))
+            dqa[half, :, :r] = jnp.zeros((HD, r), F32)
+
+        def step(key0):
+            keys = pl.ds(key0, KEYS)
+            k_left = jnp.concatenate([k[keys, lanes], ka[keys, :]], axis=1)
+            v_left = jnp.concatenate([v[keys, lanes], ka[keys, :]], axis=1)
+            for half in range(2):
+                share = jnp.exp(dot(k_left, qs[half]))
+                slope = (share * dot(v_left, gs[half])).astype(BF16)
+                dva[keys, :] += dot(share.astype(BF16), gm[half])
+                dka[keys, :] += dot(slope, qm[half])
+                rows = pl.ds(pl.multiple_of(pair * 128 + half * HD, HD), HD)
+                dqa[half, :, :r] += dot(kt[rows, keys], slope)
+
+        over_keys(z, part, start, total, step)
+        for half in range(2):
+            rows = pl.ds(pl.multiple_of(pair * 128 + half * HD, HD), HD)
+            dqt[rows, cols] = (dqa[half, :, :r] * HD ** (-0.5)).astype(BF16)
+    dk[:, lanes] = dka[...].astype(BF16)
+    dv[:, lanes] = dva[...].astype(BF16)
+
+
+def attention_back_kernel(*refs):
     z = lax.axis_index("tp")
-    own, total = qt.shape[1], k.shape[0]
-    pairs = k.shape[1] // 128
 
     def one_pair(pair, carry):
-        lanes = pl.ds(pl.multiple_of(pair * 128, 128), 128)
-        dka[...] = jnp.zeros_like(dka)
-        dva[...] = jnp.zeros_like(dva)
-        for part, (row0, r, start) in enumerate(parts_of(z, own)):
-            cols = pl.ds(pl.multiple_of(row0, 128), r)
-            qs, gs, qm, gm = [], [], [], []
-            low = lax.broadcasted_iota(jnp.int32, (r, 128), 1) < HD
-            for half in range(2):
-                rows = pl.ds(pl.multiple_of(pair * 128 + half * HD, HD), HD)
-                delta = jnp.sum(dmt[rows, cols].astype(F32) * mixed_t[rows, cols], axis=0, keepdims=True)
-                total_log = lse[pair, half : half + 1, cols]
-                q_aug = pick_rows((ma[0:1, cols], ma[1:2, cols]) + split3(-total_log), r)
-                zero = jnp.zeros((1, r), F32)
-                g_aug = pick_rows((zero, zero) + split3(-delta), r)
-                qs.append(padded(qt[rows, cols], half, aug_rows(q_aug, r), r))
-                gs.append(padded(dmt[rows, cols], half, aug_rows(g_aug, r), r))
-                mine = low if half == 0 else jnp.logical_not(low)
-                here = pl.ds(pl.multiple_of(row0, 128), r)
-                qm.append(jnp.where(mine, q[here, lanes], jnp.zeros((), BF16)))
-                gm.append(jnp.where(mine, dm[here, lanes], jnp.zeros((), BF16)))
-                dqa[half, :, :r] = jnp.zeros((HD, r), F32)
-
-            def step(key0):
-                keys = pl.ds(key0, KEYS)
-                k_left = jnp.concatenate([k[keys, lanes], ka[keys, :]], axis=1)
-                v_left = jnp.concatenate([v[keys, lanes], ka[keys, :]], axis=1)
-                for half in range(2):
-                    share = jnp.exp(dot(k_left, qs[half]))
-                    slope = (share * dot(v_left, gs[half])).astype(BF16)
-                    dva[keys, :] += dot(share.astype(BF16), gm[half])
-                    dka[keys, :] += dot(slope, qm[half])
-                    rows = pl.ds(pl.multiple_of(pair * 128 + half * HD, HD), HD)
-                    dqa[half, :, :r] += dot(kt[rows, keys], slope)
-
-            over_keys(z, part, start, total, step)
-            for half in range(2):
-                rows = pl.ds(pl.multiple_of(pair * 128 + half * HD, HD), HD)
-                dqt[rows, cols] = (dqa[half, :, :r] * HD ** (-0.5)).astype(BF16)
-        dk[:, lanes] = dka[...].astype(BF16)
-        dv[:, lanes] = dva[...].astype(BF16)
+        back_pair(z, pair, lambda part: None, *refs)
         return carry
 
-    lax.fori_loop(0, pairs, one_pair, 0)
-
-
-def attention_back(qt, q, k, kt, v, ka, ma, mixed_t, lse, dmt, dm):
-    width, own = qt.shape
-    total = k.shape[0]
+    lax.fori_loop(0, refs[2].shape[1] // 128, one_pair, 0)
+
+
+def back_sums_kernel(qt, q, k, kt, v, ka, ma, mixed_t, lse, dmt, dm, *refs):
+    g = (refs[0:4], refs[4:8])
+    dqt, dk, dv, out_u, out_d, dka, dva, dqa, gk, *bufs = refs[8:]
+    bufs, (gk_sem, *sems) = bufs[:8], bufs[8:]
+    z, d, core, first, second = position()
+    greet(z, d)
+
+    def fetch(p, t):
+        return pltpu.make_async_copy(g[p][t].at[:, core], gk.at[p, t], gk_sem.at[p, t])
+
+    sums = Sums(
+        z, d, core, second, first,
+        lambda p, t: g[p][t].at[:, 1 - core],
+        lambda p, t, at: up(gk.at[p, t, at]),
+        lambda p, t: fetch(p, t).wait(),
+        bufs, sems,
+    )
+    for p in range(2):
+        for t in range(4):
+            sums.one(p, t).start()
+            fetch(p, t).start()
+
+    def each(act, *units):
+        def run():
+            for p, t in units:
+                act(p, t)
+
+        return run
+
+    def kept_and_four(p):
+        def run():
+            for t in range(4):
+                sums.at_kept(p, t)
+                sums.at_four(p, t, 0)
+
+        return run
+
+    def four(p, step):
+        return each(lambda p, t: sums.at_four(p, t, step), *[(p, t) for t in range(4)])
+
+    packs = [[(p, t) for t in range(4)] for p in range(2)]
+    between = {
+        (1, 0): each(sums.at_two, *packs[0]),
+        (1, 1): each(sums.at_two, *packs[1]),
+        (2, 1): each(sums.at_three, *packs[0][:2]),
+        (3, 0): each(sums.at_three, *packs[0][2:]),
+        (3, 1): each(sums.at_three, *packs[1][:2]),
+        (4, 0): each(sums.at_three, *packs[1][2:]),
+        (4, 1): kept_and_four(0),
+        (5, 0): four(0, 1),
+        (5, 1): kept_and_four(1),
+    }
+
+    def one_pair(pair, carry):
+        def pause(part):
+            for (i, at), run in between.items():
+                if at == part:
+
+                    @pl.when(pair == i)
+                    def _():
+                        run()
+
+        back_pair(z, pair, pause, qt, q, k, kt, v, ka, ma, mixed_t, lse, dmt, dm, dqt, dk, dv, dka, dva, dqa)
+        return carry
+
+    lax.fori_loop(0, k.shape[1] // 128, one_pair, 0)
+    for p, step in ((0, 2), (1, 1), (1, 2)):
+        four(p, step)()
+    sums.result(0, out_u)
+    sums.result(1, out_d)
+    for p in range(2):
+        sums.drain(p)
+
+
+def back_shapes(own, total, width):
     widest = max(SHORT - own, own - (SHORT - own))
     vm = pltpu.VMEM
+    outs = (
+        jax.ShapeDtypeStruct((width, own), BF16),
+        jax.ShapeDtypeStruct((total, width), BF16),
+        jax.ShapeDtypeStruct((total, width), BF16),
+    )
+    return outs, [vm((total, 128), F32), vm((total, 128), F32), vm((2, HD, widest), F32)]
+
+
+def attention_back(*args):
+    (width, own), total = args[0].shape, args[2].shape[0]
+    outs, scratch = back_shapes(own, total, width)
     return pl.pallas_call(
         attention_back_kernel,
-        out_shape=(
-            jax.ShapeDtypeStruct((width, own), BF16),
-            jax.ShapeDtypeStruct((total, width), BF16),
-            jax.ShapeDtypeStruct((total, width), BF16),
-        ),
+        out_shape=outs,
         in_specs=[pl.BlockSpec(memory_space=pltpu.VMEM)] * 11,
         out_specs=(pl.BlockSpec(memory_space=pltpu.VMEM),) * 3,
-        scratch_shapes=[
-            vm((total, 128), F32),
-            vm((total, 128), F32),
-            vm((2, HD, widest), F32),
-        ],
+        scratch_shapes=scratch,
         compiler_params=pltpu.CompilerParams(vmem_limit_bytes=VMEM_MAX),
         name="attention_back",
-    )(qt, q, k, kt, v, ka, ma, mixed_t, lse, dmt, dm)
+    )(*args)
+
+
+def back_sums(args, gu, gd):
+    (width, own), total = args[0].shape, args[2].shape[0]
+    outs, scratch = back_shapes(own, total, width)
+    block = (width // 8, gu[0].shape[1])
+    g = [a.reshape((4, 2) + block) for a in (*gu, *gd)]
+    vmem = pl.BlockSpec(memory_space=pltpu.VMEM)
+    return pl.pallas_call(
+        back_sums_kernel,
+        out_shape=outs + (jax.ShapeDtypeStruct(block, F32),) * 2,
+        in_specs=[vmem] * 11 + [pl.BlockSpec(memory_space=pl.ANY)] * 8,
+        out_specs=(vmem,) * 5,
+        scratch_shapes=[
+            *scratch,
+            pltpu.VMEM((2, 4, 4) + block, BF16),
+            *sum_buffers(2, block),
+            pltpu.SemaphoreType.DMA((2, 4)),
+            *sum_semaphores(2),
+        ],
+        compiler_params=pltpu.CompilerParams(
+            collective_id=2, has_side_effects=True, vmem_limit_bytes=VMEM_MAX
+        ),
+        name="back_sums",
+    )(*args, *g)
 
 
 def body(
@@ -982,8 +1190,8 @@
     vectors = (b_query, b_value, b_out, gain_attn, shift_attn, b_down, gain_ffn, shift_ffn, b_up)
     n_small = 8 * r + b_up.shape[0]
     if direct:
-        lines = [jnp.pad(a, (0, 128 - r)) for a in vectors[:8]] + [b_up, jnp.zeros((5 * 128,), BF16)]
-        own_s = jnp.concatenate(lines).reshape(16, 128)
+        narrow = jnp.pad(jnp.concatenate(vectors[:8]).reshape(8, r), ((0, 0), (0, 128 - r)))
+        own_s = jnp.concatenate([narrow, jnp.pad(b_up.reshape(-1, 128), ((0, 5), (0, 0)))])
         w, vec, bu, x, q, qt, k, v, kt, wd, mixed_t, lse = forward_all(lengths, deal_order, own_w, own_s, tokens)
         w = w.reshape(2, n_tp, width, w_up.shape[1])
         bu = bu.reshape(-1)
@@ -1037,25 +1245,9 @@
     dr1 = normalize_backward(dy1, xhat1, inv1, g1)
     dar = dr1.astype(BF16)
     dm = dot(dar, wo).astype(BF16)
-    dqt, dk, dv = attention_back(qt, q, k, kt, v, ka, ma, mixed_t, lse, dm.T, dm)
-    dq = dqt.T
-    base = dr1 + contract_last(dq, wq)
-    far = contract_last(dk, wk) + contract_last(dv, wv)
-    base = base + lax.dynamic_slice_in_dim(far, z * own, own)
-    dt = far.astype(BF16)
-    gq, gk, gv = contract_first(tokens, dq), contract_first(x, dk), contract_first(x, dv)
-    go = contract_first(dar, mixed)
-    ga = jnp.stack(
-        [
-            jnp.concatenate([m[:, t * hw : (t + 1) * hw] for m in (gq, gk, gv, go)], axis=1)
-            for t in range(n_tp)
-        ]
-    )
-    gu = jnp.stack([contract_first(y1r, du[t]) for t in range(n_tp)])
-    gd = jnp.stack([contract_first(dfr, hr[t]) for t in range(n_tp)])
-    sums = [
-        jnp.sum(dq, axis=0, dtype=F32),
-        jnp.sum(dv, axis=0, dtype=F32),
+    gu = [contract_first(y1r, du[t]) for t in range(n_tp)]
+    gd = [contract_first(dfr, hr[t]) for t in range(n_tp)]
+    row_sums = [
         jnp.sum(dar, axis=0, dtype=F32),
         jnp.sum(dy1 * xhat1, axis=0),
         jnp.sum(dy1, axis=0),
@@ -1063,28 +1255,45 @@
         jnp.sum(grad * xhat2, axis=0),
         jnp.sum(grad, axis=0),
     ]
-    sums = [a.reshape(n_dp, r) for a in sums]
-    sums.append(jnp.concatenate([jnp.sum(a, axis=0, dtype=F32) for a in du]).reshape(n_dp, -1))
-    sv = jnp.concatenate(sums, axis=1)
+    wide_sum = jnp.concatenate([jnp.sum(a, axis=0, dtype=F32) for a in du])
+    back_args = (qt, q, k, kt, v, ka, ma, mixed_t, lse, dm.T, dm)
     if direct:
-        grads = jnp.stack([ga, gu, gd]).astype(BF16).reshape(3, n_tp, n_dp, r, -1)
-        sv = jnp.pad(sv, ((0, 0), (0, 2048 - n_small))).reshape(n_dp, 16, 128)
-        gw, gs, grad_tokens = reduce_all(grads, sv, dt, base)
-        gs = gs.reshape(-1)
+        gu, gd = [a.astype(BF16) for a in gu], [a.astype(BF16) for a in gd]
+        dqt, dk, dv, g_up, g_down = back_sums(back_args, gu, gd)
+        vecs = jnp.stack([jnp.zeros((width,), F32)] * 2 + row_sums)
+        a, gs, grad_tokens = finish(dqt, dk, dv, x, dar, mixed_t, wd, dr1, vecs, wide_sum.reshape(1, -1))
+        gs = [gs[i, :r] for i in range(8)] + [gs[8:11].reshape(-1)]
     else:
-        grads = jnp.stack([ga, gu, gd], axis=1).reshape(n_tp, 3, n_dp, r, -1)
+        dqt, dk, dv = attention_back(*back_args)
+        dq = dqt.T
+        base = dr1 + contract_last(dq, wq)
+        far = contract_last(dk, wk) + contract_last(dv, wv)
+        base = base + lax.dynamic_slice_in_dim(far, z * own, own)
+        dt = far.astype(BF16)
+        gq, gk, gv = contract_first(tokens, dq), contract_first(x, dk), contract_first(x, dv)
+        go = contract_first(dar, mixed)
+        ga = jnp.stack(
+            [
+                jnp.concatenate([m[:, t * hw : (t + 1) * hw] for m in (gq, gk, gv, go)], axis=1)
+                for t in range(n_tp)
+            ]
+        )
+        sums = [jnp.sum(dq, axis=0, dtype=F32), jnp.sum(dv, axis=0, dtype=F32)] + row_sums
+        sums = [a.reshape(n_dp, r) for a in sums]
+        sv = jnp.concatenate(sums + [wide_sum.reshape(n_dp, -1)], axis=1)
+        grads = jnp.stack([ga, jnp.stack(gu), jnp.stack(gd)], axis=1).reshape(n_tp, 3, n_dp, r, -1)
         grads = jnp.moveaxis(grads, 1, 2).reshape(n_tp * n_dp, 3, r, -1)
         gw = lax.psum_scatter(grads, ("tp", "dp"), scatter_dimension=0, tiled=True)[0]
         gs = lax.psum_scatter(lax.psum(sv, "tp"), "dp", scatter_dimension=0, tiled=True)[0]
         others = jnp.where(jnp.arange(total)[:, None] // own == z, jnp.zeros((), BF16), dt)
         grad_tokens = base + lax.psum_scatter(others, "tp", scatter_dimension=0, tiled=True).astype(F32)
-    gs = [gs[i * r : (i + 1) * r] for i in range(8)] + [gs[8 * r : n_small]]
-    a = gw[0]
+        gs = [gs[i * r : (i + 1) * r] for i in range(8)] + [gs[8 * r : n_small]]
+        a, g_up, g_down = gw[0], gw[1], gw[2]
     return (
         encoder_output, grad_tokens,
         a[:, :hw], a[:, hw : 2 * hw], a[:, 2 * hw : 3 * hw], gs[0], gs[1],
         a[:, 3 * hw :], gs[2], gs[3], gs[4],
-        gw[1], gs[8], gw[2], gs[5], gs[6], gs[7],
+        g_up, gs[8], g_down, gs[5], gs[6], gs[7],
     )
 
 

time: 441 us -> 386 us (0.88)
  matrix products: 94.2 us -> 62.7 us
  other arithmetic: 33.4 us -> 16.5 us
  local copies, waits for them, and re-layouts: 31.3 us -> 20.9 us
  Pallas kernels: 274 us -> 279 us
    dot_general x12 -> x9, matrix products: 31.2 us -> 13 us  [contract_last(): lax.dot_general(left, right, (((1,), (1,)), ((), ())), preferred_element_...]
    dot_general x12 -> x8, matrix products: 29.7 us -> 18.8 us  [contract_first(): lax.dot_general(left, right, (((0,), (0,)), ((), ())), preferred_element_...]
    another operation x1 -> x0, other arithmetic: 9.39 us -> none  [body(): grads = jnp.stack([ga, gu, gd]).astype(BF16).reshape(3, n_tp, n_dp, r, -1)]
    pad x8 -> x0, local copies, waits for them, and re-layouts: 5.28 us -> none  [body(): jnp.pad(a, (0, 128 - r))]
    slice x6 -> x0, local copies, waits for them, and re-layouts: 5.12 us -> none  [the longest x4 3.93 us: body(): m[:, t * hw:(t + 1) * hw]]
    pallas_call x2, Pallas kernels: 162 us -> 167 us  [the longest x1 91.4 us: back_sums(): pl.pallas_call(back_sums_kernel, out_shape=outs + (jax.ShapeDtypeStruct(b...]
where the time goes in v3:
time: 386 us; the launch traced here: 381 us
  Pallas kernels  279 us (72%)
  matrix products  62.7 us (16%)
  local copies, waits for them, and re-layouts  20.9 us (5%)
  other arithmetic  16.5 us (4%)
    pallas_call x1, Pallas kernels, forward_all(): pl.pallas_call(forward_kernel, out_shape=(shape((packs - 1, 4, 8, r, c),...  112 us
    pallas_call x1, Pallas kernels, back_sums(): pl.pallas_call(back_sums_kernel, out_shape=outs + (jax.ShapeDtypeStruct(b...  91.4 us
    pallas_call x1, Pallas kernels, finish(): pl.pallas_call(finish_kernel, out_shape=(jax.ShapeDtypeStruct(block, F32)...  75.7 us
    dot_general x9, matrix products, dot(): return jnp.dot(left, right, preferred_element_type=F32)  31 us
    dot_general x8, matrix products, contract_first(): lax.dot_general(left, right, (((0,), (0,)), ((), ())), preferred_element_...  18.8 us
    dot_general x9, matrix products, contract_last(): lax.dot_general(left, right, (((1,), (1,)), ((), ())), preferred_element_...  13 us

profile of v3, /device:TPU:0, one launch (start us, length us, event | category | flops | bytes accessed | tf_op | source)
XLA Modules:
  0.0 380.6 jit_solution(13644552013357229168)
XLA Ops:
  0.7 1.0 maximum_bitcast_fusion
  1.6 1.8 pad_maximum_fusion.own_w
  3.4 5.4 %concatenate.13 = bf16[768]{0:T(1024)(128)(2,1)S(1)} concatenate(bf16[96]{0:T(256)(128)(2,1)} %param.23, bf16[96]{0:T(256)(128)(2,1)} %param.24, bf16[96]{0:T(256)(128)(2,1)} %param.26, bf16[96]{0:T(256)(128)(2,1)} %param.27, bf16[96]{0:T(256)(128)(2,1)} %param.28, bf16[96]{0:T(256)(128)(2,1)} %param.32, bf16[96]{0:T(256)(128)(2,1)} %param.33, bf16[96]{0:T(256)(128)(2,1)} %param.34), dimensions={0} | concatenate | bytes 3072 | tf_op jit(solution)/shard_map/concatenate | solution.py:1193
  8.9 1.3 fusion.89.own_s
  10.2 111.7 %forward_all.1 = (bf16[2,4,8,96,768]{4,3,2,1,0:T(8,128)(2,1)}, f32[8,768]{1,0:T(8,128)}, f32[1,3072]{1,0:T(1,128)}, bf16[2560,768]{1,0:T(8,128)(2,1)}, bf16[640,...) custom-call(s32[16]{0:T(128)} %lengths.1, ...), custom_call_target="tpu_custom_call" | custom-call | tf_op jit(solution)/shard_map/forward_all/pallas_call | solution.py:476
  122.0 1.0 slice_reduce_fusion.1
  123.0 3.4 fusion.96
  127.2 0.8 copy-done.7
  127.9 5.2 %fusion.11 = (bf16[640,768]{1,0:T(8,128)(2,1)S(1)}, f32[640,768]{1,0:T(8,128)S(1)}) fusion(f32[768]{0:T(1024)S(1)} %get-tuple-element.115, bf16[640,768]{1,0:T(8,128)(2,1)S(1)} %fusion.71, bf16[2,4,768,768]{3,2,1,0:T(8,128)(2,1)S(1)} %bitcast.136), kind=kOutput, calls=%fused_computation.22 | convolution fusion | flops 787415040 | bytes 5115904 | tf_op jit(solution)/shard_map/dot_general | solution.py:25
  133.1 1.0 fusion.79
  134.1 5.2 %fusion.8 = (bf16[640,768]{1,0:T(8,128)(2,1)S(1)}, f32[640,768]{1,0:T(8,128)S(1)}) fusion(f32[768]{0:T(1024)S(1)} %get-tuple-element.114, bf16[640,768]{1,0:T(8,128)(2,1)S(1)} %fusion.71, bf16[2,4,768,768]{3,2,1,0:T(8,128)(2,1)S(1)} %bitcast.138), kind=kOutput, calls=%fused_computation.19 | convolution fusion | flops 787415040 | bytes 5115904 | tf_op jit(solution)/shard_map/dot_general | solution.py:25
  139.3 1.0 fusion.76
  140.3 5.6 %fusion.14 = (bf16[640,768]{1,0:T(8,128)(2,1)S(1)}, f32[640,768]{1,0:T(8,128)S(1)}) fusion(f32[768]{0:T(1024)S(1)} %get-tuple-element.116, bf16[640,768]{1,0:T(8,128)(2,1)S(1)} %fusion.71, bf16[2,4,768,768]{3,2,1,0:T(8,128)(2,1)S(1)} %bitcast.140), kind=kOutput, calls=%fused_computation.25 | convolution fusion | flops 787415040 | bytes 5115904 | tf_op jit(solution)/shard_map/dot_general | solution.py:25
  145.9 1.0 fusion.82
  146.9 5.2 %fusion.17 = (bf16[640,768]{1,0:T(8,128)(2,1)S(1)}, f32[640,768]{1,0:T(8,128)S(1)}) fusion(f32[768]{0:T(1024)S(1)} %get-tuple-element.117, bf16[640,768]{1,0:T(8,128)(2,1)S(1)} %fusion.71, bf16[2,4,768,768]{3,2,1,0:T(8,128)(2,1)S(1)} %bitcast.142), kind=kOutput, calls=%fused_computation.28 | convolution fusion | flops 787415040 | bytes 5115904 | tf_op jit(solution)/shard_map/dot_general | solution.py:25
  152.1 1.6 fusion.97
  154.1 0.8 copy-done
  154.9 1.0 fusion.18
  155.9 1.8 convert_reduce_fusion.5
  157.7 1.8 convert_reduce_fusion.3
  159.6 1.9 convert_reduce_fusion.4
  161.4 1.9 convert_reduce_fusion.2
  163.3 2.0 convert_reduce_fusion.1
  166.0 1.0 fusion.77
  167.0 1.0 fusion.74
  168.0 1.0 fusion.80
  169.0 2.2 multiply_reduce_fusion
  171.2 1.9 convert_reduce_fusion.6
  173.2 0.8 stack.47.vecs
  174.0 3.5 convolution_convert_fusion
  177.5 2.1 convolution_convert_fusion.1
  179.6 2.1 convolution_convert_fusion.2
  181.8 2.1 convolution_convert_fusion.3
  183.9 2.2 convolution_convert_fusion.4
  186.1 2.2 convolution_convert_fusion.5
  188.3 2.1 convolution_convert_fusion.6
  190.4 2.4 convolution_convert_fusion.7
  192.8 2.2 convolution_convert_fusion.8.dm
  195.1 0.9 copy-done.2
  196.0 1.3 copy.36.dmt
  197.9 1.3 fusion.91
  201.2 2.7 select_convert_fusion.ka
  203.9 91.4 %back_sums.1 = (bf16[768,640]{1,0:T(8,128)(2,1)}, bf16[2560,768]{1,0:T(8,128)(2,1)}, bf16[2560,768]{1,0:T(8,128)(2,1)}, f32[96,768]{1,0:T(8,128)}, f32[96,768]{1,0:T(8,128)}) custom-call(bf16[768,640]{1,0:T(8,128)(2,1)} %get-tuple-element.42.qt, bf16[640,768]{1,0:T(8,128)(2,1)} %get-tuple-element.43.q, bf16[2560,768]{1,0:T(8,128)(2,1)} %get-tuple-element.44.k, ...), custom_call_target="tpu_custom_call" | custom-call | tf_op jit(solution)/shard_map/back_sums/pallas_call | solution.py:1159
  295.3 75.7 %finish.1 = (f32[96,768]{1,0:T(8,128)}, f32[16,128]{1,0:T(8,128)}, f32[640,768]{1,0:T(8,128)}) custom-call(bf16[768,640]{1,0:T(8,128)(2,1)} %get-tuple-element.48.dqt, bf16[2560,768]{1,0:T(8,128)(2,1)} %get-tuple-element.49.dk, bf16[2560,768]{1,0:T(8,128)(2,1)} %get-tuple-element.50.dv, bf16[2560,768]{1,0:T(8,128)(2,1)} %get-tuple-element.51.x, ...), custom_call_target="tpu_custom_call" | custom-call | tf_op jit(solution)/shard_map/finish/pallas_call | solution.py:877
  371.0 1.9 fusion.95
  372.9 1.5 slice_bitcast_fusion.25
  374.4 1.3 slice_bitcast_fusion.24
  375.7 3.0 copy.40
  (74 shorter events, 6.1 us)
Async XLA Ops:
  123.0 4.9 %copy-start.7 = (bf16[2,4,8,96,768]{4,3,2,1,0:T(8,128)(2,1)S(1)}, bf16[2,4,8,96,768]{4,3,2,1,0:T(8,128)(2,1)}, u32[]{:S(2)}) copy-start(bf16[2,4,8,96,768]{4,3,2,1,0:T(8,128)(2,1)} %get-tuple-element.40) | copy-start | bytes 28311556
  133.1 1.0 copy-start.12
  139.3 1.0 copy-start.14
  145.9 1.0 copy-start.16
  153.7 1.2 copy-start
  157.7 5.6 %copy-start.3 = (bf16[640,768]{1,0:T(8,128)(2,1)}, bf16[640,768]{1,0:T(8,128)(2,1)S(1)}, u32[]{:S(2)}) copy-start(bf16[640,768]{1,0:T(8,128)(2,1)S(1)} %get-tuple-element.76) | copy-start | bytes 2949124
  159.6 6.5 %copy-start.18 = (bf16[640,768]{1,0:T(8,128)(2,1)}, bf16[640,768]{1,0:T(8,128)(2,1)S(1)}, u32[]{:S(2)}) copy-start(bf16[640,768]{1,0:T(8,128)(2,1)S(1)} %get-tuple-element.111) | copy-start | bytes 2949124
  161.4 5.6 %copy-start.20 = (bf16[640,768]{1,0:T(8,128)(2,1)}, bf16[640,768]{1,0:T(8,128)(2,1)S(1)}, u32[]{:S(2)}) copy-start(bf16[640,768]{1,0:T(8,128)(2,1)S(1)} %get-tuple-element.113) | copy-start | bytes 2949124
  163.3 4.7 %copy-start.22 = (bf16[640,768]{1,0:T(8,128)(2,1)}, bf16[640,768]{1,0:T(8,128)(2,1)S(1)}, u32[]{:S(2)}) copy-start(bf16[640,768]{1,0:T(8,128)(2,1)S(1)} %get-tuple-element.109) | copy-start | bytes 2949124
  165.4 3.6 copy-start.5
  173.2 19.7 %copy-start.1 = (bf16[640,768]{1,0:T(8,128)(2,1)}, bf16[640,768]{1,0:T(8,128)(2,1)S(1)}, u32[]{:S(2)}) copy-start(bf16[640,768]{1,0:T(8,128)(2,1)S(1)} %get-tuple-element.78.dar) | copy-start | bytes 2949124
  174.0 3.5 copy-start.4
  174.0 3.5 copy-start.17
  177.5 2.1 copy-start.13
  179.6 2.1 copy-start.15
  181.8 2.1 copy-start.6
  183.9 2.2 copy-start.23
  186.1 2.2 copy-start.19
  188.3 2.1 copy-start.21
  195.0 0.9 copy-start.2
  195.0 2.3 copy-start.10
  195.0 2.8 copy-start.11
  375.7 3.0 copy-start.9
  375.7 3.7 copy-start.8
